TPU v7x, 128 devices: a whole 4x4x4 slice. The times are simulated.
128 devices in a mesh: slab: 16 (over x, z_lo, core), tile: 8 (over y, z_hi).
Axes of the slice: x: 4, y: 4, z: 4 (z_hi: 2, z_lo: 2; z = z_hi * 2 + z_lo), core: 2. Of those that a mesh axis runs over, the one named last changes fastest.
Arguments:
- volume: float32 [128, 512, 1024], P('slab', 'tile'), may hold values from -0.3 to 0.3
- shears: float32 [16], replicated, may hold values from -0.4 to 0.4
- tile_shift: int32 [16, 8], P(None, 'tile'), may hold values from -1 to 1
- illumination: float32 [2, 128, 128], replicated, may hold values from -6 to 6
- measured: bfloat16 [4096, 128, 128], P(('slab', 'tile')), may hold values from 0.049804688 to 2.5
- frame_owner: int32 [4096, 1], P(('slab', 'tile')), may hold values from 0 to 15; in each aligned block of 32 rows (0 to 31, 32 to 63, ...) at most 4 rows name the same one
- frame_shift: int32 [4096], P(('slab', 'tile')), may hold values from -32 to 32
Outputs:
- volume_grad: float32 [128, 512, 1024], P('slab', 'tile')
Inputs may be any that keep to these rules, and one draw needn't show every extreme that they name: `frame_owner`: the 32 frames of one device name each angle at most 4 times, a bound that some block reaches.
All inputs are finite; a program needn't handle non-finite values.
Results may differ from a plain program's by a relative error of at most 0.012.
Values may be sent and summed in bfloat16 or wider, within the bound.
No kernel may reach another device: no remote copies, remote signals or barrier semaphores. Data moves between devices by JAX's collectives and lax.ppermute only.
A program may use at most 256 MiB of HBM per device.

v0:
```python
import math

import jax
import jax.numpy as jnp
from jax import lax
from jax.sharding import PartitionSpec as P

SIDE = 128
BLOCK = 128
HALO = 32


smoothing = 0.25
highest = lax.Precision.HIGHEST


def in_blocks(value, dim, count):
    before, after = (value.shape[:dim], value.shape[dim + 1 :])
    return jnp.moveaxis(value.reshape(*before, count, -1, *after), dim, 0)


def sent_and_summed(value, axis, dim):
    count = lax.axis_size(axis)
    tiles = lax.all_to_all(in_blocks(value, dim, count), axis, 0, 0, tiled=True)
    return jnp.sum(tiles, axis=0)


def extended(value, sides, width):
    for axis, dim in sides:
        count, length = (lax.axis_size(axis), value.shape[dim])
        up = [(i, (i + 1) % count) for i in range(count - 1)]
        down = [(j, i) for i, j in up]
        last = lax.slice_in_dim(value, length - width, length, axis=dim)
        first = lax.slice_in_dim(value, 0, width, axis=dim)
        before = lax.ppermute(last, axis, up)
        after = lax.ppermute(first, axis, down)
        value = jnp.concatenate([before, value, after], axis=dim)
    return value


def from_everyone(value, axis):
    copies = jnp.broadcast_to(value, (lax.axis_size(axis), *value.shape))
    return lax.all_to_all(copies, axis, split_axis=0, concat_axis=0, tiled=True)


def joined_along(tiles, dim):
    lengths = list(tiles.shape[1:])
    lengths[dim] *= tiles.shape[0]
    return jnp.moveaxis(tiles, 0, dim).reshape(lengths)


def gathered_copies(value, axis, dim):
    tiles = from_everyone(value, axis)
    return joined_along(tiles, dim)


def passed_along(value, axis, steps):
    count = lax.axis_size(axis)
    first, last = (max(0, -steps), min(count, count - steps))
    return lax.ppermute(value, axis, [(source, source + steps) for source in range(first, last)])


def beam_kernel(shear_one, beam_depth, block_width):
    beam_pos = jnp.arange(beam_depth, dtype=jnp.float32)
    centre = block_width * 0.5 + (beam_pos - (beam_depth - 1) * 0.5) * shear_one
    source = jnp.arange(block_width, dtype=jnp.float32)
    target = jnp.arange(2 * block_width, dtype=jnp.float32)
    spread = target[None, None, :] - source[None, :, None] - centre[:, None, None]
    values = jnp.exp(-0.5 * spread * spread).astype(jnp.bfloat16)
    return values.reshape(beam_depth * block_width, 2 * block_width)


def dft_tables(length):
    indices = jnp.arange(length, dtype=jnp.int32)
    product = indices[:, None] * indices[None, :] % length
    phases = product.astype(jnp.float32) * (2.0 * math.pi / length)
    return (jnp.cos(phases), jnp.sin(phases))


def left_mul(matrix, frames_in):
    return jnp.einsum("jk,nkl->njl", matrix, frames_in, precision=highest)


def right_mul(frames_in, matrix):
    return jnp.einsum("njk,kl->njl", frames_in, matrix, precision=highest)


def phase_gradient(windows, illumination, amplitude, dft_cos, dft_sin):
    length = dft_cos.shape[0]
    object_re = jnp.cos(windows)
    object_im = jnp.sin(windows)
    probe_re = illumination[0]
    probe_im = illumination[1]
    wave_re = probe_re * object_re - probe_im * object_im
    wave_im = probe_re * object_im + probe_im * object_re
    half_re = left_mul(dft_cos, wave_re) + left_mul(dft_sin, wave_im)
    half_im = left_mul(dft_cos, wave_im) - left_mul(dft_sin, wave_re)
    far_re = (right_mul(half_re, dft_cos) + right_mul(half_im, dft_sin)) / length
    far_im = (right_mul(half_im, dft_cos) - right_mul(half_re, dft_sin)) / length
    modulus = jnp.sqrt(far_re * far_re + far_im * far_im + smoothing)
    factor = 1.0 - amplitude / modulus
    resid_re = far_re * factor
    resid_im = far_im * factor
    back_re = left_mul(dft_cos, resid_re) - left_mul(dft_sin, resid_im)
    back_im = left_mul(dft_cos, resid_im) + left_mul(dft_sin, resid_re)
    near_re = (right_mul(back_re, dft_cos) - right_mul(back_im, dft_sin)) / length
    near_im = (right_mul(back_im, dft_cos) + right_mul(back_re, dft_sin)) / length
    grad_re = probe_re * near_re + probe_im * near_im
    grad_im = probe_re * near_im - probe_im * near_re
    return grad_im * object_re - grad_re * object_im


def shift_select(block_ids, offset, plus_one, dtype_out):
    return (block_ids[:, None] == block_ids[None, :] + offset + plus_one).astype(dtype_out)


def body(volume, shears, tile_shift, illumination, measured, frame_owner, frame_shift):
    slices_dev, beam_depth, grid_width = volume.shape
    blocks_row = grid_width // BLOCK
    block_ids = jnp.arange(blocks_row, dtype=jnp.int32)
    volume_rows = volume.astype(jnp.bfloat16).reshape(slices_dev, beam_depth, blocks_row, BLOCK)
    volume_rows = volume_rows.transpose(0, 2, 1, 3).reshape(
        slices_dev * blocks_row, beam_depth * BLOCK
    )
    offsets = tile_shift[:, 0]

    def project_angle(carried, inputs):
        shear_one, offset = inputs
        kernel = beam_kernel(shear_one, beam_depth, BLOCK)
        partial_sum = jnp.dot(volume_rows, kernel, preferred_element_type=jnp.float32)
        partial_sum = partial_sum.reshape(slices_dev, blocks_row, 2, BLOCK)
        shifted = jnp.einsum(
            "ki,sib->skb",
            shift_select(block_ids, offset, 0, jnp.float32),
            partial_sum[:, :, 0],
            precision=highest,
        )
        shifted = shifted + jnp.einsum(
            "ki,sib->skb",
            shift_select(block_ids, offset, 1, jnp.float32),
            partial_sum[:, :, 1],
            precision=highest,
        )
        return (carried, (shifted.reshape(slices_dev, grid_width), kernel))

    unused, (partials, kernels) = lax.scan(
        project_angle, jnp.zeros((), jnp.float32), (shears, offsets)
    )
    landed = sent_and_summed(partials, "tile", 2)
    landed = lax.all_to_all(landed, "slab", split_axis=0, concat_axis=1, tiled=True)
    phase_own = landed[0]
    phase_pad = extended(phase_own, (("tile", 1),), HALO)
    row_count, pad_width = phase_pad.shape
    own_width = pad_width - 2 * HALO
    dft_cos, dft_sin = dft_tables(SIDE)
    zero_index = jnp.zeros((), jnp.int32)
    frames_dev = measured.shape[0]
    owners = frame_owner[:, 0]
    every_phase = gathered_copies(phase_pad[None], "slab", 0)
    frame_starts = frame_shift + HALO

    def cut_frame(angle_id, start_col):
        return lax.dynamic_slice(
            every_phase, (angle_id, zero_index, start_col), (1, row_count, SIDE)
        )[0]

    windows = jax.vmap(cut_frame)(owners, frame_starts)
    dphase = phase_gradient(windows, illumination, measured.astype(jnp.float32), dft_cos, dft_sin)

    def add_frame(member, current):
        corner = (owners[member], zero_index, frame_starts[member])
        piece = lax.dynamic_slice(current, corner, (1, row_count, SIDE))
        return lax.dynamic_update_slice(current, piece + dphase[member][None], corner)

    per_angle = lax.fori_loop(0, frames_dev, add_frame, jnp.zeros_like(every_phase))
    grad_pad = sent_and_summed(per_angle, "slab", 0)[0]
    from_left = passed_along(grad_pad[:, HALO + own_width :], "tile", 1)
    from_right = passed_along(grad_pad[:, :HALO], "tile", -1)
    own_part = grad_pad[:, HALO : HALO + own_width]
    own_part = own_part.at[:, :HALO].add(from_left)
    own_part = own_part.at[:, own_width - HALO :].add(from_right)
    proj_grad = own_part.astype(jnp.bfloat16)[None]
    spread = lax.all_to_all(proj_grad, "slab", split_axis=1, concat_axis=0, tiled=True)
    spread = gathered_copies(spread, "tile", 2)

    def back_angle(running, inputs):
        kernel, offset, grad_rows = inputs
        pieces = grad_rows.reshape(slices_dev, blocks_row, BLOCK)
        pick_low = jnp.einsum(
            "ki,skb->sib",
            shift_select(block_ids, offset, 0, jnp.bfloat16),
            pieces,
            preferred_element_type=jnp.float32,
        ).astype(jnp.bfloat16)
        pick_high = jnp.einsum(
            "ki,skb->sib",
            shift_select(block_ids, offset, 1, jnp.bfloat16),
            pieces,
            preferred_element_type=jnp.float32,
        ).astype(jnp.bfloat16)
        stacked = jnp.concatenate([pick_low, pick_high], axis=2).reshape(
            slices_dev * blocks_row, 2 * BLOCK
        )
        update = lax.dot_general(
            stacked, kernel, (((1,), (1,)), ((), ())), preferred_element_type=jnp.float32
        )
        return (running + update, None)

    initial = jnp.zeros((slices_dev * blocks_row, beam_depth * BLOCK), jnp.float32)
    running, unused = lax.scan(back_angle, initial, (kernels, offsets, spread))
    running = running.reshape(slices_dev, blocks_row, beam_depth, BLOCK).transpose(0, 2, 1, 3)
    return running.reshape(slices_dev, beam_depth, grid_width)


def solution(mesh):
    in_specs = (
        P("slab", "tile", None),
        P(),
        P(None, "tile"),
        P(),
        P(("slab", "tile"), None, None),
        P(("slab", "tile"), None),
        P(("slab", "tile")),
    )
    out_specs = P("slab", "tile", None)
    return jax.shard_map(body, mesh=mesh, in_specs=in_specs, out_specs=out_specs, check_vma=False)
```

profile of v0, /device:TPU:0, one launch (start us, length us, event | category | flops | bytes accessed | tf_op | source)
XLA Modules:
  0.0 661.7 jit_solution(13338874932412023798)
XLA Ops:
  2.4 152.1 %while.44 = (s32[]{:T(128)}, f32[16,8,1024]{2,1,0:T(8,128)S(1)}, bf16[16,8192,256]{2,1,0:T(8,128)(2,1)}, f32[16]{0:T(128)S(1)}, bf16[64,8192]{1,0:T(8,128)(2,1)S(1)}, /*index=5*/s32[16]{0:T(128)S(1)}, s32[]{:T(128)}) while((s32[]{:T(128)}, f32[16,8,1024]{2,1,0:T(8,128)S(1)}, bf16[16,8192,256]{2,1,0:T(8,128)(2,1)}, ...), condition=%wide.region_1.2_spmd.clone.clone, body=%wide.region_0.1_spmd.clone.clone.sunk | while | flops 286826816 | bytes 31262896 | solution.py:146
  8.9 3.0 fusion.206
  18.4 3.0 fusion.206
  27.9 3.0 fusion.206
  37.4 3.0 fusion.206
  46.9 3.0 fusion.206
  56.4 3.0 fusion.206
  65.9 3.0 fusion.206
  84.9 3.1 fusion.206
  94.4 3.0 fusion.206
  103.9 3.0 fusion.206
  113.4 3.0 fusion.206
  122.9 3.1 fusion.206
  132.5 3.0 fusion.206
  142.0 3.0 fusion.206
  151.5 3.0 fusion.206
  154.7 18.9 %all_to_all.41 = f32[8,16,8,128]{3,2,1,0:T(8,128)S(1)} all-to-all(f32[8,16,8,128]{3,2,1,0:T(8,128)S(1)} %copy.100), channel_id=1, replica_groups=mesh['slab'=16,'tile'=8] {'tile'}, dimensions={0} | all-to-all | bytes 1048576 | tf_op jit(solution)/shard_map/all_to_all | solution.py:24
  173.6 10.8 %all_to_all.42 = f32[16,8,128]{2,1,0:T(8,128)S(1)} all-to-all(f32[16,8,128]{2,1,0:T(8,128)S(1)} %reduce_sum.18), channel_id=1, replica_groups=mesh['slab'=16,'tile'=8] {'slab'}, dimensions={0} | all-to-all | bytes 131072 | tf_op jit(solution)/shard_map/all_to_all | solution.py:150
  184.5 3.8 collective-permute-start
  190.2 5.8 collective-permute-done.1
  197.5 3.7 all-to-all-start.2
  201.3 22.0 %all-to-all-done.2 = f32[16,1,128,192]{2,3,1,0:T(8,128)S(1)} async-done(((f32[16,1,128,192]{2,3,1,0:T(8,128)}), f32[16,1,128,192]{2,3,1,0:T(8,128)S(1)}, u32[]{:S(2)}, u32[]{:S(2)}) %all-to-all-start.2) | async-done | bytes 1572896 | tf_op jit(solution)/shard_map/all_to_all | solution.py:43
  224.2 5.8 gather_fusion
  232.0 7.7 %fusion.178 = (f32[32,128,128]{2,1,0:T(8,128)S(1)}, f32[32,128,128]{2,1,0:T(8,128)S(1)}) fusion(f32[32,128,128]{2,1,0:T(8,128)S(1)} %copy.103), kind=kLoop, calls=%fused_computation.204 | loop fusion | bytes 6291456 | tf_op jit(solution)/shard_map/cos | solution.py:90
  239.7 3.7 fusion.59
  243.5 3.6 fusion.60
  247.1 3.6 convolution_add_fusion.3
  250.8 3.8 fusion.45
  254.6 3.6 fusion.43
  258.1 3.7 convolution_subtract_fusion.1
  261.8 3.9 subtract_multiply_fusion
  265.7 3.7 add_multiply_fusion
  269.4 4.0 fusion.76
  273.5 4.5 fusion.73
  277.9 4.1 convolution_subtract_fusion
  282.0 3.6 fusion.35
  285.6 3.7 fusion.37
  289.3 4.0 convolution_add_fusion.2
  293.4 3.6 fusion.39
  296.9 5.7 multiply_subtract_fusion
  302.7 208.9 %while.43 = (s32[]{:T(128)}, f32[16,128,192]{1,2,0:T(8,128)S(1)}, s32[32]{0:T(128)S(1)}, s32[32]{0:T(128)S(1)}, f32[32,128,128]{2,1,0:T(8,128)}, /*index=5*/s32[]{:T(128)}, s32[]{:T(128)}, s32[]{:T(128)}, s32[]{:T(128)}) while((s32[]{:T(128)}, f32[16,128,192]{1,2,0:T(8,128)S(1)}, s32[32]{0:T(128)S(1)}, s32[32]{0:T(128)S(1)}, ...), condition=%wide.region_4.5_spmd, body=%wide.region_3.4_spmd.sunk | while | flops 16392 | bytes 721097 | solution.py:175
  511.6 26.2 %all_to_all.43 = f32[16,1,128,192]{2,3,1,0:T(8,128)S(1)} all-to-all(f32[16,1,128,192]{2,3,1,0:T(8,128)S(1)} %bitcast.237), channel_id=1, replica_groups=mesh['slab'=16,'tile'=8] {'slab'}, dimensions={0} | all-to-all | bytes 3145728 | tf_op jit(solution)/shard_map/all_to_all | solution.py:24
  537.9 4.0 collective-permute-start.2
  544.5 5.2 collective-permute-done.3
  551.2 8.7 %all_to_all.44 = bf16[16,2,512]{2,1,0:T(2,128)(2,1)S(1)} all-to-all(bf16[16,2,512]{2,1,0:T(2,128)(2,1)S(1)} %reshape.238), channel_id=1, replica_groups=mesh['slab'=16,'tile'=8] {'slab'}, dimensions={0} | all-to-all | bytes 65536 | tf_op jit(solution)/shard_map/all_to_all | solution.py:183
  560.6 5.5 all-to-all-start.5
  566.1 8.8 %all-to-all-done.5 = bf16[8,16,8,128]{3,2,1,0:T(8,128)(2,1)S(1)} async-done(((bf16[8,16,8,128]{3,2,1,0:T(8,128)(2,1)}), bf16[8,16,8,128]{3,2,1,0:T(8,128)(2,1)S(1)}, u32[]{:S(2)}, u32[]{:S(2)}) %all-to-all-start.5) | async-done | bytes 262176 | tf_op jit(solution)/shard_map/all_to_all | solution.py:43
  574.9 85.0 %while.45 = (s32[]{:T(128)}, f32[64,8192]{1,0:T(8,128)S(1)}, bf16[16,8,1024]{2,1,0:T(8,128)(2,1)S(1)}, s32[16]{0:T(128)S(1)}, bf16[16,8192,256]{2,1,0:T(8,128)(2,1)}, /*index=5*/s32[]{:T(128)}, s32[]{:T(128)}) while((s32[]{:T(128)}, f32[64,8192]{1,0:T(8,128)S(1)}, bf16[16,8,1024]{2,1,0:T(8,128)(2,1)S(1)}, ...), condition=%wide.region_8.9_spmd.clone.clone, body=%wide.region_7.8_spmd.clone.clone.sunk | while | flops 269828256 | bytes 8520427 | solution.py:210
  576.6 3.7 convolution_add_fusion.5
  581.9 3.7 convolution_add_fusion.5
  587.2 3.7 convolution_add_fusion.5
  592.5 3.7 convolution_add_fusion.5
  597.8 3.7 convolution_add_fusion.5
  603.1 3.7 convolution_add_fusion.5
  608.5 3.7 convolution_add_fusion.5
  613.8 3.7 convolution_add_fusion.5
  619.1 3.7 convolution_add_fusion.5
  624.4 3.7 convolution_add_fusion.5
  629.7 3.7 convolution_add_fusion.5
  635.0 3.7 convolution_add_fusion.5
  640.3 3.7 convolution_add_fusion.5
  645.7 3.7 convolution_add_fusion.5
  651.0 3.7 convolution_add_fusion.5
  656.3 3.7 convolution_add_fusion.5
  (565 shorter events, 235.4 us)
Async XLA Ops:
  1.8 0.7 copy-start.2
  1.8 0.7 copy-start.5
  184.5 5.7 collective-permute-start
  188.3 7.7 %collective-permute-start.1 = (f32[128,32]{1,0:T(8,128)S(1)}, f32[128,32]{1,0:T(8,128)S(1)}, u32[]{:S(2)}, u32[]{:S(2)}) collective-permute-start(f32[128,32]{1,0:T(8,128)S(1)} %get-tuple-element.376), channel_id=1, source_target_pairs={{1,0},{2,1},{3,2},{4,3},{5,4},{6,5},{7,6},{9,8},{10,9},{11,10},{12... | collective-permute-start | bytes 49160 | tf_op jit(solution)/shard_map/ppermute | solution.py:36
  196.2 5.1 copy-start.3
  196.2 5.1 copy-start.4
  196.2 5.1 copy-start.1
  197.5 25.8 %all-to-all-start.2 = ((f32[16,1,128,192]{2,3,1,0:T(8,128)}), f32[16,1,128,192]{2,3,1,0:T(8,128)S(1)}, u32[]{:S(2)}, u32[]{:S(2)}) async-start(f32[16,1,128,192]{2,3,1,0:T(8,128)} %broadcast_in_dim.53), calls=%async_computation.2 | async-start | bytes 3145728 | tf_op jit(solution)/shard_map/all_to_all | solution.py:43
  265.7 3.7 copy-start
  537.9 5.9 collective-permute-start.2
  542.5 7.1 %collective-permute-start.3 = (f32[128,32]{0,1:T(8,128)S(1)}, f32[128,32]{0,1:T(8,128)S(1)}, u32[]{:S(2)}, u32[]{:S(2)}) collective-permute-start(f32[128,32]{0,1:T(8,128)S(1)} %get-tuple-element.373), channel_id=1, source_target_pairs={{1,0},{2,1},{3,2},{4,3},{5,4},{6,5},{7,6},{9,8},{10,9},{11,10},{12... | collective-permute-start | bytes 49160 | tf_op jit(solution)/shard_map/ppermute | solution.py:60
  560.6 14.3 %all-to-all-start.5 = ((bf16[8,16,8,128]{3,2,1,0:T(8,128)(2,1)}), bf16[8,16,8,128]{3,2,1,0:T(8,128)(2,1)S(1)}, u32[]{:S(2)}, u32[]{:S(2)}) async-start(bf16[8,16,8,128]{3,2,1,0:T(8,128)(2,1)} %broadcast_in_dim.56), calls=%async_computation.5 | async-start | bytes 524288 | tf_op jit(solution)/shard_map/all_to_all | solution.py:43
where the time goes:
time: 674 us; the launch traced here: 662 us
  matrix products  145 us (22%)
  other arithmetic  137 us (20%)
  local copies, waits for them, and re-layouts  130 us (19%)
  loops' own time  123 us (18%)
  blocking collectives  64.6 us (10%)
  waiting for transfers between devices  42.3 us (6%)
  starting transfers between devices  19.5 us (3%)
    another operation x1, loops' own time, body(): lax.fori_loop(0, frames_dev, add_frame, jnp.zeros_like(every_phase))  121 us
    dot_general x16, matrix products, back_angle(): lax.dot_general(stacked, kernel, (((1,), (1,)), ((), ())), preferred_elem...  58.5 us
    dynamic_update_slice x16, other arithmetic, body(): lax.scan(project_angle, jnp.zeros((), jnp.float32), (shears, offsets))  48 us
    all_to_all x2, blocking collectives, sent_and_summed(): tiles = lax.all_to_all(in_blocks(value, dim, count), axis, 0, 0, tiled=True)  45.1 us
    dynamic_slice x64, local copies, waits for them, and re-layouts, add_frame(): corner = (owners[member], zero_index, frame_starts[member])  41.2 us
    dot_general x8, matrix products, right_mul(): return jnp.einsum('njk,kl->njl', frames_in, matrix, precision=highest)  31.4 us
    dot_general x8, matrix products, left_mul(): return jnp.einsum('jk,nkl->njl', matrix, frames_in, precision=highest)  31.3 us
    all_to_all x2, waiting for transfers between devices, from_everyone(): return lax.all_to_all(copies, axis, split_axis=0, concat_axis=0, tiled=True)  30.7 us
  transfers between devices with their start and end apart: 6, of which 5 were waited for; matrix products, arithmetic and copies ran while one was open for 0% of the time, Pallas kernels for 0%

commit v1 on v0

v1 whole, which is shorter than its diff:
```python
import math

import jax
import jax.numpy as jnp
import numpy as np
from jax import lax
from jax.experimental import pallas as pl
from jax.experimental.pallas import tpu as pltpu
from jax.sharding import PartitionSpec as P

SIDE = 128
BLOCK = 128
HALO = 32
ANGLES = 16
DEPTH = 64
SLICES_DEV = 8
BLOCKS = 8
SLABS = 16
TILES = 8
FRAMES = 32
FIRST = 38
WIDE = 9 * BLOCK
FWD_FINE, FWD_COARSE = 4, 14
BWD_FINE, BWD_COARSE = 16, 4
OWN_ROWS, EDGE_ROWS = 32, 16
PAIR_ROWS = OWN_ROWS + EDGE_ROWS
ROWS = (SLICES_DEV // 2) * PAIR_ROWS
VMEM_LIMIT = 40 * 1024 * 1024

SIN_TERMS = (3.14159264, -5.16771008, 2.55007752, -0.598291286, 0.0776576603)
COS_TERMS = (1.0, -4.93480214, 4.05870916, -1.335212, 0.234937314, -0.0243963244)


def iota(shape, dim):
    return lax.broadcasted_iota(jnp.int32, shape, dim)


def poly(terms, t):
    total = jnp.full_like(t, terms[-1])
    for term in reversed(terms[:-1]):
        total = total * t + term
    return total


def sine_and_cosine(turns):
    t = turns * turns
    half_sin = turns * poly(SIN_TERMS, t)
    half_cos = poly(COS_TERMS, t)
    return (2.0 * half_sin * half_cos, 1.0 - 2.0 * half_sin * half_sin)


def pick_rows(values, shape, dim, period):
    index = iota(shape, dim) % period
    total = jnp.zeros(shape, values[0].dtype)
    for i, value in enumerate(values):
        total = jnp.where(index == i, value, total)
    return total


def bell(offset, centre):
    spread = offset - centre
    return jnp.exp(-0.5 * spread * spread).astype(jnp.bfloat16)


def left(value, steps):
    return pltpu.roll(value, value.shape[1] - steps, 1)


def project_kernel(shears, shifts, volume, out, table, stack):
    @pl.when(pl.program_id(0) == 0)
    def _():
        shape = (ANGLES, FWD_FINE * DEPTH)
        shear = pick_rows([shears[i] for i in range(ANGLES)], shape, 0, ANGLES)
        lane = iota(shape, 1)
        beam = (lane % DEPTH).astype(jnp.float32)
        centre = BLOCK * 0.5 + (beam - (DEPTH - 1) * 0.5) * shear
        fine = (lane // DEPTH).astype(jnp.float32)
        for j in range(FWD_COARSE):
            table[j * ANGLES : (j + 1) * ANGLES] = bell(fine + float(FIRST + FWD_FINE * j), centre)

    shape = (ANGLES, BLOCK)
    shift = pick_rows([shifts[i, 0] for i in range(ANGLES)], shape, 0, ANGLES)
    lane = iota((8, BLOCK), 1)
    edges = [[] for k in range(BLOCKS)]
    for half in range(2):
        rows = jnp.concatenate(
            [volume[half], jnp.zeros((DEPTH, WIDE - BLOCKS * BLOCK), jnp.float32)], axis=1
        )
        stack[half, 0:DEPTH] = rows.astype(jnp.bfloat16)
        for r in range(1, FWD_FINE):
            stack[half, r * DEPTH : (r + 1) * DEPTH] = pltpu.roll(rows, r, 1).astype(jnp.bfloat16)
        sums = jnp.dot(table[...], stack[half], preferred_element_type=jnp.float32)
        total = pltpu.roll(sums[0:ANGLES], FIRST, 1)
        for j in range(1, FWD_COARSE):
            part = sums[j * ANGLES : (j + 1) * ANGLES]
            total = total + pltpu.roll(part, FIRST + FWD_FINE * j, 1)
        turns = total * (1.0 / (2.0 * math.pi))
        turns = turns - jnp.floor(turns + 0.5)
        fixed = jnp.minimum(jnp.floor(turns * 65536.0 + 0.5), 32767.0)
        zero = jnp.zeros((ANGLES, BLOCK), jnp.float32)
        block = [fixed[:, k * BLOCK : (k + 1) * BLOCK] for k in range(BLOCKS + 1)]
        block = [zero] + block + [zero]
        placed = []
        for k in range(BLOCKS):
            here = jnp.where(shift == 0, block[k + 1], jnp.where(shift > 0, block[k], block[k + 2]))
            placed.append(here.astype(jnp.int32))
        zero = jnp.zeros((ANGLES, BLOCK), jnp.int32)
        around = [zero] + placed + [zero]
        for k in range(BLOCKS):
            out[k, half * ANGLES : (half + 1) * ANGLES] = placed[k].astype(jnp.int16)
            after, before = around[k + 2], around[k]
            low = jnp.where(lane < HALO, after[:8], before[:8])
            high = jnp.where(lane < HALO, after[8:], before[8:])
            outer = (lane < HALO) | (lane >= BLOCK - HALO)
            edge = jnp.where(outer, low, pltpu.roll(high, BLOCK // 2, 1))
            edges[k].append(edge)
    for k in range(BLOCKS):
        out[k, OWN_ROWS:PAIR_ROWS] = jnp.concatenate(edges[k], axis=0).astype(jnp.int16)


def project(shears, shifts, volume):
    return pl.pallas_call(
        project_kernel,
        name="project",
        grid=(SLICES_DEV // 2,),
        in_specs=[
            pl.BlockSpec(memory_space=pltpu.SMEM),
            pl.BlockSpec(memory_space=pltpu.SMEM),
            pl.BlockSpec((2, DEPTH, BLOCKS * BLOCK), lambda p: (p, 0, 0)),
        ],
        out_specs=pl.BlockSpec((TILES, PAIR_ROWS, BLOCK), lambda p: (0, p, 0)),
        out_shape=jax.ShapeDtypeStruct((TILES, ROWS, BLOCK), jnp.int16),
        scratch_shapes=[
            pltpu.VMEM((FWD_COARSE * ANGLES, FWD_FINE * DEPTH), jnp.bfloat16),
            pltpu.VMEM((2, FWD_FINE * DEPTH, WIDE), jnp.bfloat16),
        ],
        compiler_params=pltpu.CompilerParams(vmem_limit_bytes=VMEM_LIMIT),
    )(shears, shifts, volume)


def frames_kernel(owners, shifts, phases, probe, measured, spread, gather, out, own, edge, own_sum, edge_sum):
    lane = iota((8, BLOCK), 1)
    outer = (lane < HALO) | (lane >= BLOCK - HALO)

    def unpack(slab, carried):
        for p in range(SLICES_DEV // 2):
            base = pl.multiple_of(slab * BLOCK + p * OWN_ROWS, OWN_ROWS)
            rows = phases[slab, p * PAIR_ROWS : (p + 1) * PAIR_ROWS].astype(jnp.int32)
            rows = rows.astype(jnp.float32) * (1.0 / 65536.0)
            own[pl.ds(base, OWN_ROWS), :] = rows[:OWN_ROWS]
            for half in range(2):
                packed = rows[OWN_ROWS + half * 8 : OWN_ROWS + half * 8 + 8]
                edge[pl.ds(base + half * 16, 8), :] = packed
                edge[pl.ds(base + half * 16 + 8, 8), :] = pltpu.roll(packed, BLOCK // 2, 1)
        own_sum[pl.ds(pl.multiple_of(slab * BLOCK, BLOCK), BLOCK), :] = jnp.zeros((BLOCK, BLOCK), jnp.float32)
        edge_sum[pl.ds(pl.multiple_of(slab * BLOCK, BLOCK), BLOCK), :] = jnp.zeros((BLOCK, BLOCK), jnp.float32)
        return carried

    lax.fori_loop(0, SLABS, unpack, 0)

    wide_lane = iota((SIDE, BLOCK), 1)
    probe_re, probe_im = probe[0], probe[1]

    def pair(step, carried):
        waves, inside, rows_of, amount = [], [], [], []
        for k in range(2):
            f = step * 2 + k
            shift = shifts[f]
            rows = pl.ds(owners[f, 0], SIDE, stride=ANGLES)
            bound = jnp.where(shift >= 0, shift, shift + BLOCK)
            within = (wide_lane >= bound) == (shift >= 0)
            turns = pltpu.roll(jnp.where(within, own[rows, :], edge[rows, :]), lax.rem(BLOCK - shift, BLOCK), 1)
            object_im, object_re = sine_and_cosine(turns)
            wave_re = probe_re * object_re - probe_im * object_im
            wave_im = probe_re * object_im + probe_im * object_re
            waves.append((wave_re, wave_im))
            inside.append(within)
            rows_of.append(rows)
            amount.append(lax.rem(shift + BLOCK, BLOCK))
        fields = jnp.concatenate(
            [jnp.concatenate([re.astype(jnp.bfloat16), im.astype(jnp.bfloat16)], axis=1) for re, im in waves], axis=0
        )
        half = jnp.dot(fields, spread[...], preferred_element_type=jnp.float32).astype(jnp.bfloat16)

        def turned(value):
            top = jnp.concatenate([value[:SIDE, :SIDE], value[SIDE:, :SIDE]], axis=1)
            bottom = jnp.concatenate([value[:SIDE, SIDE:], value[SIDE:, SIDE:]], axis=1)
            return jnp.concatenate([top, bottom], axis=0)

        far = jnp.dot(gather[...], turned(half), preferred_element_type=jnp.float32)
        far_re, far_im = far[:SIDE], far[SIDE:]
        amplitude = jnp.concatenate(
            [measured[step * 2].astype(jnp.float32), measured[step * 2 + 1].astype(jnp.float32)], axis=1
        )
        factor = 1.0 - amplitude * lax.rsqrt(far_re * far_re + far_im * far_im + 0.25)
        resid = jnp.concatenate(
            [(far_re * factor).astype(jnp.bfloat16), (far_im * factor).astype(jnp.bfloat16)], axis=0
        )
        back = jnp.dot(spread[...], resid, preferred_element_type=jnp.float32).astype(jnp.bfloat16)
        near = jnp.dot(turned(back), gather[...], preferred_element_type=jnp.float32)
        for k in range(2):
            near_re = near[k * SIDE : (k + 1) * SIDE, :SIDE]
            near_im = near[k * SIDE : (k + 1) * SIDE, SIDE:]
            wave_re, wave_im = waves[k]
            grad = pltpu.roll(near_im * wave_re - near_re * wave_im, amount[k], 1)
            rows = rows_of[k]
            own_sum[rows, :] = own_sum[rows, :] + jnp.where(inside[k], grad, 0.0)
            edge_sum[rows, :] = edge_sum[rows, :] + jnp.where(inside[k], 0.0, grad)
        return carried

    lax.fori_loop(0, FRAMES // 2, pair, 0)

    def pack(slab, carried):
        for p in range(SLICES_DEV // 2):
            base = pl.multiple_of(slab * BLOCK + p * OWN_ROWS, OWN_ROWS)
            out[slab, p * PAIR_ROWS : p * PAIR_ROWS + OWN_ROWS] = own_sum[pl.ds(base, OWN_ROWS), :].astype(jnp.bfloat16)
            packed = []
            for half in range(2):
                low = edge_sum[pl.ds(base + half * 16, 8), :]
                high = edge_sum[pl.ds(base + half * 16 + 8, 8), :]
                packed.append(jnp.where(outer, low, pltpu.roll(high, BLOCK // 2, 1)))
            out[slab, p * PAIR_ROWS + OWN_ROWS : (p + 1) * PAIR_ROWS] = jnp.concatenate(packed, axis=0).astype(jnp.bfloat16)
        return carried

    lax.fori_loop(0, SLABS, pack, 0)


def frame_gradients(owners, shifts, phases, probe, measured, spread, gather):
    smem = pl.BlockSpec(memory_space=pltpu.SMEM)
    vmem = pl.BlockSpec(memory_space=pltpu.VMEM)
    table = pltpu.VMEM((SLABS * SLICES_DEV * ANGLES, BLOCK), jnp.float32)
    return pl.pallas_call(
        frames_kernel,
        name="frame_gradients",
        in_specs=[smem, smem, vmem, vmem, vmem, vmem, vmem],
        out_specs=vmem,
        out_shape=jax.ShapeDtypeStruct((SLABS, ROWS, BLOCK), jnp.bfloat16),
        scratch_shapes=[table, table, table, table],
        compiler_params=pltpu.CompilerParams(vmem_limit_bytes=VMEM_LIMIT),
    )(owners, shifts, phases, probe, measured, spread, gather)


def back_kernel(shears, shifts, tiles, out, table, stack):
    @pl.when(pl.program_id(0) == 0)
    def _():
        shape = (DEPTH, BWD_FINE * ANGLES)
        shear = pick_rows([shears[i] for i in range(ANGLES)], shape, 1, ANGLES)
        beam = iota(shape, 0).astype(jnp.float32)
        centre = BLOCK * 0.5 + (beam - (DEPTH - 1) * 0.5) * shear
        fine = (iota(shape, 1) // ANGLES).astype(jnp.float32)
        for j in range(BWD_COARSE):
            table[j * DEPTH : (j + 1) * DEPTH] = bell(fine + float(FIRST + BWD_FINE * j), centre)

    shape = (ANGLES, BLOCK)
    shift = pick_rows([shifts[i, 0] for i in range(ANGLES)], shape, 0, ANGLES)
    lane = iota(shape, 1)
    for half in range(2):
        own, margin = [], []
        for k in range(TILES):
            own.append(tiles[k, half * ANGLES : (half + 1) * ANGLES].astype(jnp.float32))
            packed = tiles[k, OWN_ROWS:PAIR_ROWS].astype(jnp.float32)[half * 8 : half * 8 + 8]
            margin.append(jnp.concatenate([packed, pltpu.roll(packed, BLOCK // 2, 1)], axis=0))
        whole = []
        for k in range(TILES):
            total = own[k]
            if k > 0:
                total = total + jnp.where(lane < HALO, margin[k - 1], 0.0)
            if k < TILES - 1:
                total = total + jnp.where(lane >= BLOCK - HALO, margin[k + 1], 0.0)
            whole.append(total.astype(jnp.bfloat16).astype(jnp.float32))
        zero = jnp.zeros(shape, jnp.float32)
        whole = [zero] + whole + [zero, zero]
        placed = [
            jnp.where(shift == 0, whole[k + 1], jnp.where(shift > 0, whole[k + 2], whole[k])) for k in range(BLOCKS + 1)
        ]
        placed = jnp.concatenate(placed, axis=1)
        stack[half, 0:ANGLES] = placed.astype(jnp.bfloat16)
        for r in range(1, BWD_FINE):
            stack[half, r * ANGLES : (r + 1) * ANGLES] = left(placed, r).astype(jnp.bfloat16)
        sums = jnp.dot(table[...], stack[half], preferred_element_type=jnp.float32)
        total = left(sums[0:DEPTH], FIRST)
        for j in range(1, BWD_COARSE):
            total = total + left(sums[j * DEPTH : (j + 1) * DEPTH], FIRST + BWD_FINE * j)
        out[half] = total[:, : BLOCKS * BLOCK]


def back_project(shears, shifts, tiles):
    return pl.pallas_call(
        back_kernel,
        name="back_project",
        grid=(SLICES_DEV // 2,),
        in_specs=[
            pl.BlockSpec(memory_space=pltpu.SMEM),
            pl.BlockSpec(memory_space=pltpu.SMEM),
            pl.BlockSpec((TILES, PAIR_ROWS, BLOCK), lambda p: (0, p, 0)),
        ],
        out_specs=pl.BlockSpec((2, DEPTH, BLOCKS * BLOCK), lambda p: (p, 0, 0)),
        out_shape=jax.ShapeDtypeStruct((SLICES_DEV, DEPTH, BLOCKS * BLOCK), jnp.float32),
        scratch_shapes=[
            pltpu.VMEM((BWD_COARSE * DEPTH, BWD_FINE * ANGLES), jnp.bfloat16),
            pltpu.VMEM((2, BWD_FINE * ANGLES, WIDE), jnp.bfloat16),
        ],
        compiler_params=pltpu.CompilerParams(vmem_limit_bytes=VMEM_LIMIT),
    )(shears, shifts, tiles)


def dft_matrices():
    index = np.arange(SIDE)
    phase = (np.outer(index, index) % SIDE) * (2.0 * np.pi / SIDE)
    cos, sin = np.cos(phase), np.sin(phase)
    spread = np.block([[cos, -sin], [sin, cos]])
    gather = np.block([[cos, sin], [-sin, cos]]) / SIDE
    return jnp.asarray(spread, jnp.bfloat16), jnp.asarray(gather, jnp.bfloat16)


def from_everyone(value, axis):
    copies = jnp.broadcast_to(value, (lax.axis_size(axis), *value.shape))
    return lax.all_to_all(copies, axis, split_axis=0, concat_axis=0, tiled=True)


def body(volume, shears, tile_shift, illumination, measured, frame_owner, frame_shift):
    spread, gather = dft_matrices()
    partials = project(shears, tile_shift, volume)
    landed = lax.all_to_all(partials, "tile", 0, 0, tiled=True)
    phase = jnp.sum(landed.astype(jnp.int32), axis=0)
    phase = (((phase + 32768) & 65535) - 32768).astype(jnp.int16)
    phases = from_everyone(phase, "slab")
    grads = frame_gradients(frame_owner, frame_shift, phases, illumination, measured, spread, gather)
    landed = lax.all_to_all(grads, "slab", 0, 0, tiled=True)
    grad = jnp.sum(landed.astype(jnp.float32), axis=0).astype(jnp.bfloat16)
    tiles = from_everyone(grad, "tile")
    return back_project(shears, tile_shift, tiles)


def solution(mesh):
    in_specs = (
        P("slab", "tile", None),
        P(),
        P(None, "tile"),
        P(),
        P(("slab", "tile"), None, None),
        P(("slab", "tile"), None),
        P(("slab", "tile")),
    )
    out_specs = P("slab", "tile", None)
    return jax.shard_map(body, mesh=mesh, in_specs=in_specs, out_specs=out_specs, check_vma=False)
```

time: 674 us -> 106 us (0.16); the launches traced: 662 us -> 106 us
  matrix products: 145 us -> 0 us
  other arithmetic: 137 us -> 0.23 us
  local copies, waits for them, and re-layouts: 130 us -> 4.19 us
  loops' own time: 123 us -> 0 us
  Pallas kernels: 0 us -> 35.7 us
  waiting for transfers between devices: 42.3 us -> 13.6 us
  blocking collectives: 64.6 us -> 47.5 us
  starting transfers between devices: 19.5 us -> 4.86 us
    dot_general x112 -> x0, matrix products: 145 us -> none  [the longest x16 58.5 us: back_angle(): lax.dot_general(stacked, kernel, (((1,), (1,)), ((), ())), preferred_elem...]
    another operation x3 -> x0, loops' own time: 123 us -> none  [the longest x1 121 us: body(): lax.fori_loop(0, frames_dev, add_frame, jnp.zeros_like(every_phase))]
    dynamic_slice x176 -> x0, local copies, waits for them, and re-layouts: 74.4 us -> none  [the longest x64 41.2 us: add_frame(): corner = (owners[member], zero_index, frame_starts[member])]
    add x81 -> x0, other arithmetic: 57.7 us -> none  [the longest x32 27.4 us: add_frame(): piece + dphase[member][None]]
    dynamic_update_slice x16 -> x0, other arithmetic: 48 us -> none  [body(): lax.scan(project_angle, jnp.zeros((), jnp.float32), (shears, offsets))]
    pallas_call x0 -> x3, Pallas kernels: none -> 35.7 us  [the longest x1 21.9 us: frame_gradients(): pl.pallas_call(frames_kernel, name='frame_gradients', in_specs=[smem, sme...]
    convert_element_type x17 -> x1, other arithmetic: 28.8 us -> 0.02 us  [body(): phase = ((phase + 32768 & 65535) - 32768).astype(jnp.int16)]
    all_to_all x2 -> x1, waiting for transfers between devices: 30.7 us -> 13.6 us  [from_everyone(): return lax.all_to_all(copies, axis, split_axis=0, concat_axis=0, tiled=True)]
  transfers between devices with their start and end apart: 6 -> 1, of which waited for: 5 -> 1; matrix products, arithmetic and copies ran while one was open for 0% -> 0% of each run, Pallas kernels for 0% -> 0%
where the time goes in v1:
time: 106 us
  blocking collectives  47.5 us (45%)
  Pallas kernels  35.7 us (34%)
  waiting for transfers between devices  13.6 us (13%)
  starting transfers between devices  4.86 us (5%)
  local copies, waits for them, and re-layouts  4.19 us (4%)
    pallas_call x1, Pallas kernels, frame_gradients(): pl.pallas_call(frames_kernel, name='frame_gradients', in_specs=[smem, sme...  21.9 us
    all_to_all x1, blocking collectives, body(): landed = lax.all_to_all(partials, 'tile', 0, 0, tiled=True)  17.8 us
    all_to_all x1, blocking collectives, body(): landed = lax.all_to_all(grads, 'slab', 0, 0, tiled=True)  16.1 us
    all_to_all x1, blocking collectives, from_everyone(): return lax.all_to_all(copies, axis, split_axis=0, concat_axis=0, tiled=True)  13.6 us
    all_to_all x1, waiting for transfers between devices, from_everyone(): return lax.all_to_all(copies, axis, split_axis=0, concat_axis=0, tiled=True)  13.6 us
    pallas_call x1, Pallas kernels, back_project(): pl.pallas_call(back_kernel, name='back_project', grid=(SLICES_DEV // 2,),...  7.59 us
    pallas_call x1, Pallas kernels, project(): pl.pallas_call(project_kernel, name='project', grid=(SLICES_DEV // 2,), i...  6.26 us
    all_to_all x1, starting transfers between devices, from_everyone(): return lax.all_to_all(copies, axis, split_axis=0, concat_axis=0, tiled=True)  4.86 us
  transfers between devices with their start and end apart: 1, of which 1 were waited for; matrix products, arithmetic and copies ran while one was open for 0% of the time, Pallas kernels for 0%

profile of v1, /device:TPU:0, one launch (start us, length us, event | category | flops | bytes accessed | tf_op | source)
XLA Modules:
  0.0 106.1 jit_solution(12510459884236986726)
XLA Ops:
  0.0 0.7 copy.12.shifts
  0.7 0.0 copy-start
  0.7 1.6 %copy-done = f32[8,64,1024]{2,1,0:T(8,128)S(1)} copy-done((f32[8,64,1024]{2,1,0:T(8,128)S(1)}, f32[8,64,1024]{2,1,0:T(8,128)}, u32[]{:S(2)}) %copy-start) | copy-done | bytes 2097176
  2.3 0.0 copy-start.5
  2.3 0.7 copy-done.5
  3.0 6.3 %project.1 = s16[8,192,128]{2,1,0:T(8,128)(2,1)S(1)} custom-call(f32[16]{0:T(128)S(1)} %copy-done.5, s32[16,1]{1,0:T(8,128)S(1)} %copy.12.shifts, f32[8,64,1024]{2,1,0:T(8,128)S(1)} %copy-done), custom_call_target="tpu_custom_call" | custom-call | tf_op jit(solution)/shard_map/project/pallas_call | solution.py:122
  9.2 0.0 copy-start.8
  9.3 0.0 copy-start.1
  9.3 0.0 copy-start.2
  9.3 0.0 copy-start.3
  9.3 0.0 copy-start.4
  9.3 0.0 copy-start.7
  9.3 17.8 %all_to_all.20 = s16[8,192,128]{2,1,0:T(8,128)(2,1)S(1)} all-to-all(s16[8,192,128]{2,1,0:T(8,128)(2,1)S(1)} %project.1), channel_id=1, replica_groups=mesh['slab'=16,'tile'=8] {'tile'}, dimensions={0} | all-to-all | bytes 786432 | tf_op jit(solution)/shard_map/all_to_all | solution.py:324
  27.1 0.1 convert_reduce_fusion
  27.3 1.0 broadcast_in_dim.6
  28.3 4.9 %all-to-all-start.1 = ((s16[16,192,128]{2,1,0:T(8,128)(2,1)}), s16[16,192,128]{2,1,0:T(8,128)(2,1)S(1)}, u32[]{:S(2)}, u32[]{:S(2)}) async-start(s16[16,192,128]{2,1,0:T(8,128)(2,1)} %broadcast_in_dim.6), calls=%async_computation.1 | async-start | bytes 1572864 | tf_op jit(solution)/shard_map/all_to_all | solution.py:318
  33.2 0.0 copy-done.8
  33.2 0.1 copy.11.owners
  33.3 13.6 %all-to-all-done.1.phases = s16[16,192,128]{2,1,0:T(8,128)(2,1)S(1)} async-done(((s16[16,192,128]{2,1,0:T(8,128)(2,1)}), s16[16,192,128]{2,1,0:T(8,128)(2,1)S(1)}, u32[]{:S(2)}, u32[]{:S(2)}) %all-to-all-start.1) | async-done | bytes 786464 | tf_op jit(solution)/shard_map/all_to_all | solution.py:318
  46.8 0.0 copy-done.1
  46.8 0.0 copy-done.2
  46.8 0.0 copy-done.3
  46.8 0.0 copy-done.4
  46.8 0.0 copy-done.7
  46.9 21.9 %frame_gradients.1 = bf16[16,192,128]{2,1,0:T(8,128)(2,1)S(1)} custom-call(s32[32,1]{1,0:T(8,128)S(1)} %copy.11.owners, s32[32]{0:T(128)S(1)} %copy-done.7, s16[16,192,128]{2,1,0:T(8,128)(2,1)S(1)} %all-to-all-done.1.phases, f32[2,128,128]{2,1,0:T(8,128)S(1)} %copy-done.2, bf16[32,128,128]{2,1,0:T(8,128)(2,1)S(1)} %copy-done.1, ...), custom_call_target="tpu_custom_call" | custom-call | tf_op jit(solution)/shard_map/frame_gradients/pallas_call | solution.py:232
  68.7 0.0 copy-start.6
  68.7 16.1 %all_to_all.21 = bf16[16,192,128]{2,1,0:T(8,128)(2,1)S(1)} all-to-all(bf16[16,192,128]{2,1,0:T(8,128)(2,1)S(1)} %frame_gradients.1), channel_id=1, replica_groups=mesh['slab'=16,'tile'=8] {'slab'}, dimensions={0} | all-to-all | bytes 1572864 | tf_op jit(solution)/shard_map/all_to_all | solution.py:329
  84.8 0.1 reduce_sum.22
  84.9 0.1 broadcast_in_dim.7
  84.9 13.6 %all_to_all.22.tiles = bf16[8,192,128]{2,1,0:T(8,128)(2,1)S(1)} all-to-all(bf16[8,192,128]{2,1,0:T(8,128)(2,1)S(1)} %broadcast_in_dim.7), channel_id=1, replica_groups=mesh['slab'=16,'tile'=8] {'tile'}, dimensions={0} | all-to-all | bytes 786432 | tf_op jit(solution)/shard_map/all_to_all | solution.py:318
  98.5 0.0 copy-done.6
  98.5 7.6 %back_project.1 = f32[8,64,1024]{2,1,0:T(8,128)} custom-call(f32[16]{0:T(128)S(1)} %copy-done.6, s32[16,1]{1,0:T(8,128)S(1)} %copy.12.shifts, bf16[8,192,128]{2,1,0:T(8,128)(2,1)S(1)} %all_to_all.22.tiles), custom_call_target="tpu_custom_call" | custom-call | tf_op jit(solution)/shard_map/back_project/pallas_call | solution.py:288
  (1 shorter events, 0.0 us)
Async XLA Ops:
  0.7 1.6 %copy-start = (f32[8,64,1024]{2,1,0:T(8,128)S(1)}, f32[8,64,1024]{2,1,0:T(8,128)}, u32[]{:S(2)}) copy-start(f32[8,64,1024]{2,1,0:T(8,128)} %volume.1) | copy-start | bytes 6291460
  2.3 0.7 copy-start.5
  9.2 23.9 %copy-start.8 = (s32[32,1]{0,1:T(1,128)S(1)}, s32[32,1]{0,1:T(1,128)}, u32[]{:S(2)}) copy-start(s32[32,1]{0,1:T(1,128)} %param.14) | copy-start | bytes 388
  9.3 37.6 %copy-start.1 = (bf16[32,128,128]{2,1,0:T(8,128)(2,1)S(1)}, bf16[32,128,128]{2,1,0:T(8,128)(2,1)}, u32[]{:S(2)}) copy-start(bf16[32,128,128]{2,1,0:T(8,128)(2,1)} %measured.1) | copy-start | bytes 3145732
  9.3 37.6 %copy-start.2 = (f32[2,128,128]{2,1,0:T(8,128)S(1)}, f32[2,128,128]{2,1,0:T(8,128)}, u32[]{:S(2)}) copy-start(f32[2,128,128]{2,1,0:T(8,128)} %probe.1) | copy-start | bytes 393220
  9.3 37.5 %copy-start.3 = (bf16[256,256]{1,0:T(8,128)(2,1)S(1)}, bf16[256,256]{1,0:T(8,128)(2,1)}, u32[]{:S(2)}) copy-start(bf16[256,256]{1,0:T(8,128)(2,1)} %constant.16.clone.gather) | copy-start | bytes 393220
  9.3 37.5 %copy-start.4 = (bf16[256,256]{1,0:T(8,128)(2,1)S(1)}, bf16[256,256]{1,0:T(8,128)(2,1)}, u32[]{:S(2)}) copy-start(bf16[256,256]{1,0:T(8,128)(2,1)} %constant.15.clone.spread) | copy-start | bytes 393220
  9.3 37.5 %copy-start.7 = (s32[32]{0:T(128)S(1)}, s32[32]{0:T(128)}, u32[]{:S(2)}) copy-start(s32[32]{0:T(128)} %shifts.3) | copy-start | bytes 388
  28.3 18.5 %all-to-all-start.1 = ((s16[16,192,128]{2,1,0:T(8,128)(2,1)}), s16[16,192,128]{2,1,0:T(8,128)(2,1)S(1)}, u32[]{:S(2)}, u32[]{:S(2)}) async-start(s16[16,192,128]{2,1,0:T(8,128)(2,1)} %broadcast_in_dim.6), calls=%async_computation.1 | async-start | bytes 1572864 | tf_op jit(solution)/shard_map/all_to_all | solution.py:318
  68.7 29.8 %copy-start.6 = (f32[16]{0:T(128)S(1)}, f32[16]{0:T(128)}, u32[]{:S(2)}) copy-start(f32[16]{0:T(128)} %shears.3) | copy-start | bytes 196

commit v2 on v1

--- a/solution.py
+++ b/solution.py
@@ -25,6 +25,8 @@
 OWN_ROWS, EDGE_ROWS = 32, 16
 PAIR_ROWS = OWN_ROWS + EDGE_ROWS
 ROWS = (SLICES_DEV // 2) * PAIR_ROWS
+GROUP = 8
+UNPACK_UNROLL = 2
 VMEM_LIMIT = 40 * 1024 * 1024
 
 SIN_TERMS = (3.14159264, -5.16771008, 2.55007752, -0.598291286, 0.0776576603)
@@ -79,7 +81,7 @@
             table[j * ANGLES : (j + 1) * ANGLES] = bell(fine + float(FIRST + FWD_FINE * j), centre)
 
     shape = (ANGLES, BLOCK)
-    shift = pick_rows([shifts[i, 0] for i in range(ANGLES)], shape, 0, ANGLES)
+    shift = pick_rows([shifts[i] for i in range(ANGLES)], shape, 0, ANGLES)
     lane = iota((8, BLOCK), 1)
     edges = [[] for k in range(BLOCKS)]
     for half in range(2):
@@ -138,106 +140,135 @@
     )(shears, shifts, volume)
 
 
-def frames_kernel(owners, shifts, phases, probe, measured, spread, gather, out, own, edge, own_sum, edge_sum):
+def frames_kernel(
+    parity, owners_in, shifts_in, near_phases, far_phases, probe, measured, spread, gather,
+    near_out, far_out, own, edge, own_sum, edge_sum, owners, shifts, sems,
+):
+    copies = [
+        pltpu.make_async_copy(owners_in, owners, sems.at[0]),
+        pltpu.make_async_copy(shifts_in, shifts, sems.at[1]),
+    ]
+    for copy in copies:
+        copy.start()
     lane = iota((8, BLOCK), 1)
     outer = (lane < HALO) | (lane >= BLOCK - HALO)
-
-    def unpack(slab, carried):
-        for p in range(SLICES_DEV // 2):
-            base = pl.multiple_of(slab * BLOCK + p * OWN_ROWS, OWN_ROWS)
-            rows = phases[slab, p * PAIR_ROWS : (p + 1) * PAIR_ROWS].astype(jnp.int32)
-            rows = rows.astype(jnp.float32) * (1.0 / 65536.0)
-            own[pl.ds(base, OWN_ROWS), :] = rows[:OWN_ROWS]
-            for half in range(2):
-                packed = rows[OWN_ROWS + half * 8 : OWN_ROWS + half * 8 + 8]
-                edge[pl.ds(base + half * 16, 8), :] = packed
-                edge[pl.ds(base + half * 16 + 8, 8), :] = pltpu.roll(packed, BLOCK // 2, 1)
-        own_sum[pl.ds(pl.multiple_of(slab * BLOCK, BLOCK), BLOCK), :] = jnp.zeros((BLOCK, BLOCK), jnp.float32)
-        edge_sum[pl.ds(pl.multiple_of(slab * BLOCK, BLOCK), BLOCK), :] = jnp.zeros((BLOCK, BLOCK), jnp.float32)
+    core = parity[0]
+
+    def unpack(chip, carried):
+        for which, phases in ((core, near_phases), (1 - core, far_phases)):
+            start = pl.multiple_of((chip * 2 + which) * BLOCK, BLOCK)
+            for p in range(SLICES_DEV // 2):
+                base = pl.multiple_of(start + p * OWN_ROWS, OWN_ROWS)
+                rows = phases[chip, p * PAIR_ROWS : (p + 1) * PAIR_ROWS].astype(jnp.int32).astype(jnp.float32)
+                own[pl.ds(base, OWN_ROWS), :] = rows[:OWN_ROWS]
+                for half in range(2):
+                    packed = rows[OWN_ROWS + half * 8 : OWN_ROWS + half * 8 + 8]
+                    edge[pl.ds(base + half * 16, 8), :] = packed
+                    edge[pl.ds(base + half * 16 + 8, 8), :] = pltpu.roll(packed, BLOCK // 2, 1)
+            own_sum[pl.ds(start, BLOCK), :] = jnp.zeros((BLOCK, BLOCK), jnp.float32)
+            edge_sum[pl.ds(start, BLOCK), :] = jnp.zeros((BLOCK, BLOCK), jnp.float32)
         return carried
 
-    lax.fori_loop(0, SLABS, unpack, 0)
-
-    wide_lane = iota((SIDE, BLOCK), 1)
-    probe_re, probe_im = probe[0], probe[1]
-
-    def pair(step, carried):
-        waves, inside, rows_of, amount = [], [], [], []
-        for k in range(2):
-            f = step * 2 + k
-            shift = shifts[f]
-            rows = pl.ds(owners[f, 0], SIDE, stride=ANGLES)
+    lax.fori_loop(0, SLABS // 2, unpack, 0, unroll=UNPACK_UNROLL)
+    for copy in copies:
+        copy.wait()
+
+    def tiled(value):
+        return value.reshape(SIDE // 8, 8, BLOCK)
+
+    def turned(value):
+        top = jnp.concatenate([value[:SIDE, :SIDE], value[SIDE:, :SIDE]], axis=1)
+        bottom = jnp.concatenate([value[:SIDE, SIDE:], value[SIDE:, SIDE:]], axis=1)
+        return jnp.concatenate([top, bottom], axis=0)
+
+    def group(step, carried):
+        first = step * GROUP
+        rows, inside, amount, waves, fields = [], [], [], [], []
+        for k in range(GROUP):
+            shift = shifts[first + k]
+            rows.append(pl.ds(owners[first + k], SIDE, stride=ANGLES))
             bound = jnp.where(shift >= 0, shift, shift + BLOCK)
-            within = (wide_lane >= bound) == (shift >= 0)
-            turns = pltpu.roll(jnp.where(within, own[rows, :], edge[rows, :]), lax.rem(BLOCK - shift, BLOCK), 1)
+            inside.append((lane >= bound) == (shift >= 0))
+            amount.append(bound)
+        for k in range(GROUP):
+            chosen = jnp.where(inside[k], tiled(own[rows[k], :]), tiled(edge[rows[k], :])).reshape(SIDE, BLOCK)
+            turns = pltpu.roll(chosen, lax.rem(BLOCK - amount[k], BLOCK), 1) * (1.0 / 65536.0)
             object_im, object_re = sine_and_cosine(turns)
-            wave_re = probe_re * object_re - probe_im * object_im
-            wave_im = probe_re * object_im + probe_im * object_re
+            wave_re = probe[0] * object_re - probe[1] * object_im
+            wave_im = probe[0] * object_im + probe[1] * object_re
             waves.append((wave_re, wave_im))
-            inside.append(within)
-            rows_of.append(rows)
-            amount.append(lax.rem(shift + BLOCK, BLOCK))
-        fields = jnp.concatenate(
-            [jnp.concatenate([re.astype(jnp.bfloat16), im.astype(jnp.bfloat16)], axis=1) for re, im in waves], axis=0
-        )
-        half = jnp.dot(fields, spread[...], preferred_element_type=jnp.float32).astype(jnp.bfloat16)
-
-        def turned(value):
-            top = jnp.concatenate([value[:SIDE, :SIDE], value[SIDE:, :SIDE]], axis=1)
-            bottom = jnp.concatenate([value[:SIDE, SIDE:], value[SIDE:, SIDE:]], axis=1)
-            return jnp.concatenate([top, bottom], axis=0)
-
-        far = jnp.dot(gather[...], turned(half), preferred_element_type=jnp.float32)
-        far_re, far_im = far[:SIDE], far[SIDE:]
-        amplitude = jnp.concatenate(
-            [measured[step * 2].astype(jnp.float32), measured[step * 2 + 1].astype(jnp.float32)], axis=1
-        )
-        factor = 1.0 - amplitude * lax.rsqrt(far_re * far_re + far_im * far_im + 0.25)
-        resid = jnp.concatenate(
-            [(far_re * factor).astype(jnp.bfloat16), (far_im * factor).astype(jnp.bfloat16)], axis=0
-        )
-        back = jnp.dot(spread[...], resid, preferred_element_type=jnp.float32).astype(jnp.bfloat16)
-        near = jnp.dot(turned(back), gather[...], preferred_element_type=jnp.float32)
-        for k in range(2):
-            near_re = near[k * SIDE : (k + 1) * SIDE, :SIDE]
-            near_im = near[k * SIDE : (k + 1) * SIDE, SIDE:]
+            fields.append(jnp.concatenate([wave_re.astype(jnp.bfloat16), wave_im.astype(jnp.bfloat16)], axis=1))
+        pairs = range(GROUP // 2)
+        half = [
+            jnp.dot(
+                jnp.concatenate(fields[2 * g : 2 * g + 2], axis=0), spread[...], preferred_element_type=jnp.float32
+            ).astype(jnp.bfloat16)
+            for g in pairs
+        ]
+        far = [jnp.dot(gather[...], turned(half[g]), preferred_element_type=jnp.float32) for g in pairs]
+        resid = []
+        for g in pairs:
+            far_re, far_im = far[g][:SIDE], far[g][SIDE:]
+            amplitude = jnp.concatenate(
+                [measured[first + 2 * g].astype(jnp.float32), measured[first + 2 * g + 1].astype(jnp.float32)], axis=1
+            )
+            factor = 1.0 - amplitude * lax.rsqrt(far_re * far_re + far_im * far_im + 0.25)
+            resid.append(
+                jnp.concatenate([(far_re * factor).astype(jnp.bfloat16), (far_im * factor).astype(jnp.bfloat16)], axis=0)
+            )
+        back = [
+            jnp.dot(spread[...], resid[g], preferred_element_type=jnp.float32).astype(jnp.bfloat16) for g in pairs
+        ]
+        near = [jnp.dot(turned(back[g]), gather[...], preferred_element_type=jnp.float32) for g in pairs]
+        grads = []
+        for k in range(GROUP):
+            part = near[k // 2][(k % 2) * SIDE : (k % 2 + 1) * SIDE]
             wave_re, wave_im = waves[k]
-            grad = pltpu.roll(near_im * wave_re - near_re * wave_im, amount[k], 1)
-            rows = rows_of[k]
-            own_sum[rows, :] = own_sum[rows, :] + jnp.where(inside[k], grad, 0.0)
-            edge_sum[rows, :] = edge_sum[rows, :] + jnp.where(inside[k], 0.0, grad)
+            grads.append(pltpu.roll(part[:, SIDE:] * wave_re - part[:, :SIDE] * wave_im, amount[k], 1))
+        for k in range(GROUP):
+            grad = tiled(grads[k])
+            own_sum[rows[k], :] = own_sum[rows[k], :] + jnp.where(inside[k], grad, 0.0).reshape(SIDE, BLOCK)
+            edge_sum[rows[k], :] = edge_sum[rows[k], :] + jnp.where(inside[k], 0.0, grad).reshape(SIDE, BLOCK)
         return carried
 
-    lax.fori_loop(0, FRAMES // 2, pair, 0)
-
-    def pack(slab, carried):
-        for p in range(SLICES_DEV // 2):
-            base = pl.multiple_of(slab * BLOCK + p * OWN_ROWS, OWN_ROWS)
-            out[slab, p * PAIR_ROWS : p * PAIR_ROWS + OWN_ROWS] = own_sum[pl.ds(base, OWN_ROWS), :].astype(jnp.bfloat16)
-            packed = []
-            for half in range(2):
-                low = edge_sum[pl.ds(base + half * 16, 8), :]
-                high = edge_sum[pl.ds(base + half * 16 + 8, 8), :]
-                packed.append(jnp.where(outer, low, pltpu.roll(high, BLOCK // 2, 1)))
-            out[slab, p * PAIR_ROWS + OWN_ROWS : (p + 1) * PAIR_ROWS] = jnp.concatenate(packed, axis=0).astype(jnp.bfloat16)
+    lax.fori_loop(0, FRAMES // GROUP, group, 0)
+
+    def pack(chip, carried):
+        for which, out in ((core, near_out), (1 - core, far_out)):
+            start = pl.multiple_of((chip * 2 + which) * BLOCK, BLOCK)
+            for p in range(SLICES_DEV // 2):
+                base = pl.multiple_of(start + p * OWN_ROWS, OWN_ROWS)
+                top = p * PAIR_ROWS
+                out[chip, top : top + OWN_ROWS] = own_sum[pl.ds(base, OWN_ROWS), :].astype(jnp.bfloat16)
+                packed = []
+                for half in range(2):
+                    low = edge_sum[pl.ds(base + half * 16, 8), :]
+                    high = edge_sum[pl.ds(base + half * 16 + 8, 8), :]
+                    packed.append(jnp.where(outer, low, pltpu.roll(high, BLOCK // 2, 1)))
+                out[chip, top + OWN_ROWS : top + PAIR_ROWS] = jnp.concatenate(packed, axis=0).astype(jnp.bfloat16)
         return carried
 
-    lax.fori_loop(0, SLABS, pack, 0)
-
-
-def frame_gradients(owners, shifts, phases, probe, measured, spread, gather):
+    lax.fori_loop(0, SLABS // 2, pack, 0, unroll=UNPACK_UNROLL)
+
+
+def frame_gradients(parity, owners, shifts, near_phases, far_phases, probe, measured, spread, gather):
     smem = pl.BlockSpec(memory_space=pltpu.SMEM)
+    hbm = pl.BlockSpec(memory_space=pltpu.HBM)
     vmem = pl.BlockSpec(memory_space=pltpu.VMEM)
     table = pltpu.VMEM((SLABS * SLICES_DEV * ANGLES, BLOCK), jnp.float32)
+    half = jax.ShapeDtypeStruct((SLABS // 2, ROWS, BLOCK), jnp.bfloat16)
     return pl.pallas_call(
         frames_kernel,
         name="frame_gradients",
-        in_specs=[smem, smem, vmem, vmem, vmem, vmem, vmem],
-        out_specs=vmem,
-        out_shape=jax.ShapeDtypeStruct((SLABS, ROWS, BLOCK), jnp.bfloat16),
-        scratch_shapes=[table, table, table, table],
+        in_specs=[smem, hbm, hbm, vmem, vmem, vmem, vmem, vmem, vmem],
+        out_specs=[vmem, vmem],
+        out_shape=[half, half],
+        scratch_shapes=[
+            table, table, table, table,
+            pltpu.SMEM((FRAMES,), jnp.int32), pltpu.SMEM((FRAMES,), jnp.int32), pltpu.SemaphoreType.DMA((2,)),
+        ],
         compiler_params=pltpu.CompilerParams(vmem_limit_bytes=VMEM_LIMIT),
-    )(owners, shifts, phases, probe, measured, spread, gather)
+    )(parity, owners, shifts, near_phases, far_phases, probe, measured, spread, gather)
 
 
 def back_kernel(shears, shifts, tiles, out, table, stack):
@@ -252,7 +283,7 @@
             table[j * DEPTH : (j + 1) * DEPTH] = bell(fine + float(FIRST + BWD_FINE * j), centre)
 
     shape = (ANGLES, BLOCK)
-    shift = pick_rows([shifts[i, 0] for i in range(ANGLES)], shape, 0, ANGLES)
+    shift = pick_rows([shifts[i] for i in range(ANGLES)], shape, 0, ANGLES)
     lane = iota(shape, 1)
     for half in range(2):
         own, margin = [], []
@@ -313,23 +344,40 @@
     return jnp.asarray(spread, jnp.bfloat16), jnp.asarray(gather, jnp.bfloat16)
 
 
-def from_everyone(value, axis):
-    copies = jnp.broadcast_to(value, (lax.axis_size(axis), *value.shape))
-    return lax.all_to_all(copies, axis, split_axis=0, concat_axis=0, tiled=True)
+def copies_of(value, count):
+    return jnp.broadcast_to(value, (count, *value.shape))
+
+
+def between_chips(value):
+    count = lax.axis_size("slab")
+    groups = [list(range(core, count, 2)) for core in range(2)]
+    return lax.all_to_all(value, "slab", 0, 0, tiled=True, axis_index_groups=groups)
+
+
+def between_cores(value):
+    return lax.ppermute(value, "slab", [(i, i ^ 1) for i in range(lax.axis_size("slab"))])
 
 
 def body(volume, shears, tile_shift, illumination, measured, frame_owner, frame_shift):
     spread, gather = dft_matrices()
-    partials = project(shears, tile_shift, volume)
+    shifts = tile_shift.reshape(ANGLES)
+    parity = (lax.axis_index("slab") % 2).astype(jnp.int32).reshape(1)
+    partials = project(shears, shifts, volume)
     landed = lax.all_to_all(partials, "tile", 0, 0, tiled=True)
     phase = jnp.sum(landed.astype(jnp.int32), axis=0)
     phase = (((phase + 32768) & 65535) - 32768).astype(jnp.int16)
-    phases = from_everyone(phase, "slab")
-    grads = frame_gradients(frame_owner, frame_shift, phases, illumination, measured, spread, gather)
-    landed = lax.all_to_all(grads, "slab", 0, 0, tiled=True)
-    grad = jnp.sum(landed.astype(jnp.float32), axis=0).astype(jnp.bfloat16)
-    tiles = from_everyone(grad, "tile")
-    return back_project(shears, tile_shift, tiles)
+    near_phases = between_chips(copies_of(phase, SLABS // 2))
+    far_phases = between_cores(near_phases)
+    near_grads, far_grads = frame_gradients(
+        parity, frame_owner.reshape(FRAMES), frame_shift, near_phases, far_phases, illumination, measured, spread, gather
+    )
+    grads = near_grads.astype(jnp.float32) + between_cores(far_grads).astype(jnp.float32)
+    landed = between_chips(grads.astype(jnp.bfloat16)).astype(jnp.float32)
+    grad = landed[0]
+    for i in range(1, SLABS // 2):
+        grad = grad + landed[i]
+    tiles = lax.all_to_all(copies_of(grad.astype(jnp.bfloat16), TILES), "tile", 0, 0, tiled=True)
+    return back_project(shears, shifts, tiles)
 
 
 def solution(mesh):

time: 106 us -> 86.1 us (0.81)
  Pallas kernels: 35.7 us -> 24.7 us
  waiting for transfers between devices: 13.6 us -> 3.34 us
  blocking collectives: 47.5 us -> 54.2 us
  starting transfers between devices: 4.86 us -> 0.18 us
  local copies, waits for them, and re-layouts: 4.19 us -> 3.04 us
    all_to_all x1 -> x0, waiting for transfers between devices: 13.6 us -> none  [from_everyone(): return lax.all_to_all(copies, axis, split_axis=0, concat_axis=0, tiled=True)]
    pallas_call x1, Pallas kernels: 21.9 us -> 11 us  [frame_gradients(): pl.pallas_call(frames_kernel, name='frame_gradients', in_specs=[smem, hbm...]
    all_to_all x2 -> x3, blocking collectives: 29.7 us -> 36.5 us  [the longest x2 23.9 us: between_chips(): lax.all_to_all(value, 'slab', 0, 0, tiled=True, axis_index_groups=groups)]
    all_to_all x1 -> x0, starting transfers between devices: 4.86 us -> none  [from_everyone(): return lax.all_to_all(copies, axis, split_axis=0, concat_axis=0, tiled=True)]
    ppermute x0 -> x2, waiting for transfers between devices: none -> 3.34 us  [between_cores(): lax.ppermute(value, 'slab', [(i, i ^ 1) for i in range(lax.axis_size('sla...]
    unnamed x20 -> x22, local copies, waits for them, and re-layouts: 3.11 us -> 2.94 us
  transfers between devices with their start and end apart: 1 -> 2, of which waited for: 1 -> 2; matrix products, arithmetic and copies ran while one was open for 0% -> 0% of each run, Pallas kernels for 0% -> 0%
where the time goes in v2:
time: 86.1 us; the launch traced here: 85.8 us
  blocking collectives  54.2 us (63%)
  Pallas kernels  24.7 us (29%)
  waiting for transfers between devices  3.34 us (4%)
  local copies, waits for them, and re-layouts  3.04 us (4%)
    all_to_all x2, blocking collectives, between_chips(): lax.all_to_all(value, 'slab', 0, 0, tiled=True, axis_index_groups=groups)  23.9 us
    all_to_all x1, blocking collectives, body(): landed = lax.all_to_all(partials, 'tile', 0, 0, tiled=True)  17.7 us
    all_to_all x1, blocking collectives, body(): lax.all_to_all(copies_of(grad.astype(jnp.bfloat16), TILES), 'tile', 0, 0,...  12.6 us
    pallas_call x1, Pallas kernels, frame_gradients(): pl.pallas_call(frames_kernel, name='frame_gradients', in_specs=[smem, hbm...  11 us
    pallas_call x1, Pallas kernels, back_project(): pl.pallas_call(back_kernel, name='back_project', grid=(SLICES_DEV // 2,),...  7.47 us
    pallas_call x1, Pallas kernels, project(): pl.pallas_call(project_kernel, name='project', grid=(SLICES_DEV // 2,), i...  6.16 us
    ppermute x2, waiting for transfers between devices, between_cores(): lax.ppermute(value, 'slab', [(i, i ^ 1) for i in range(lax.axis_size('sla...  3.34 us
    unnamed x22, local copies, waits for them, and re-layouts  2.94 us
  transfers between devices with their start and end apart: 2, of which 2 were waited for; matrix products, arithmetic and copies ran while one was open for 0% of the time, Pallas kernels for 0%

profile of v2, /device:TPU:0, one launch (start us, length us, event | category | flops | bytes accessed | tf_op | source)
XLA Modules:
  0.0 85.8 jit_solution(17029913573150112162)
XLA Ops:
  0.0 0.0 copy-start
  0.0 1.6 %copy-done = f32[8,64,1024]{2,1,0:T(8,128)S(1)} copy-done((f32[8,64,1024]{2,1,0:T(8,128)S(1)}, f32[8,64,1024]{2,1,0:T(8,128)}, u32[]{:S(2)}) %copy-start) | copy-done | bytes 2097176
  1.6 0.0 copy-start.5
  1.6 0.7 copy-done.5
  2.2 0.0 copy-start.7
  2.2 0.7 copy-done.7
  2.9 0.0 copy-start.1
  2.9 0.0 copy-start.2
  2.9 0.0 copy-start.3
  2.9 0.0 copy-start.4
  2.9 0.0 copy-start.9
  2.9 0.0 copy-start.10
  2.9 6.2 %project.1 = s16[8,192,128]{2,1,0:T(8,128)(2,1)S(1)} custom-call(f32[16]{0:T(128)S(1)} %copy-done.5, s32[16]{0:T(128)S(1)} %bitcast.5, f32[8,64,1024]{2,1,0:T(8,128)S(1)} %copy-done), custom_call_target="tpu_custom_call" | custom-call | tf_op jit(solution)/shard_map/project/pallas_call | solution.py:124
  9.1 17.7 %all_to_all.20 = s16[8,192,128]{2,1,0:T(8,128)(2,1)S(1)} all-to-all(s16[8,192,128]{2,1,0:T(8,128)(2,1)S(1)} %project.1), channel_id=1, replica_groups=mesh['slab'=16,'tile'=8] {'tile'}, dimensions={0} | all-to-all | bytes 786432 | tf_op jit(solution)/shard_map/all_to_all | solution.py:366
  26.8 0.1 convert_reduce_fusion
  26.9 0.1 broadcast_in_dim.6
  27.0 12.4 %all_to_all.21.near_phases = s16[8,192,128]{2,1,0:T(8,128)(2,1)S(1)} all-to-all(s16[8,192,128]{2,1,0:T(8,128)(2,1)S(1)} %broadcast_in_dim.6), channel_id=1, replica_groups={{0,16,32,48,64,80,96,112},{8,24,40,56,72,88,104,120},{1,17,33,49,65,81,..., dimensions={0} | all-to-all | bytes 786432 | tf_op jit(solution)/shard_map/all_to_all | solution.py:354
  39.3 0.0 collective-permute-start
  39.3 1.7 %collective-permute-done.far_phases = s16[8,192,128]{2,1,0:T(8,128)(2,1)S(1)} collective-permute-done((s16[8,192,128]{2,1,0:T(8,128)(2,1)S(1)}, s16[8,192,128]{2,1,0:T(8,128)(2,1)S(1)}, u32[]{:S(2)}, u32[]{:S(2)}) %collective-permute-start) | collective-permute-done | bytes 393248 | tf_op jit(solution)/shard_map/ppermute | solution.py:358
  41.1 0.0 copy-done.1
  41.1 0.0 copy-done.2
  41.1 0.0 copy-done.3
  41.1 0.0 copy-done.4
  41.1 0.0 copy-done.9
  41.1 0.0 copy-done.10
  41.1 11.0 %frame_gradients.1 = (bf16[8,192,128]{2,1,0:T(8,128)(2,1)S(1)}, bf16[8,192,128]{2,1,0:T(8,128)(2,1)S(1)}) custom-call(s32[1]{0:T(128)} %bitcast.1.parity, s32[32]{0:T(128)S(1)} %bitcast.7, s32[32]{0:T(128)S(1)} %copy-done.10, s16[8,192,128]{2,1,0:T(8,128)(2,1)S(1)} %all_to_all.21.near_phases, s16[8,192,128]{2,1,0:T(8,128)(2,1)S(1)} %collective-permute-done.far_phases, ...), custom_call_target="tpu_custom_call" | custom-call | tf_op jit(solution)/shard_map/frame_gradients/pallas_call | solution.py:260
  52.1 0.2 collective-permute-start.1
  52.3 1.6 %collective-permute-done.1 = bf16[8,192,128]{2,1,0:T(8,128)(2,1)S(1)} collective-permute-done((bf16[8,192,128]{2,1,0:T(8,128)(2,1)S(1)}, bf16[8,192,128]{2,1,0:T(8,128)(2,1)S(1)}, u32[]{:S(2)}, u32[]{:S(2)}) %collective-permute-start.1) | collective-permute-done | bytes 393248 | tf_op jit(solution)/shard_map/ppermute | solution.py:358
  53.9 0.1 add_convert_fusion
  54.0 0.0 copy-start.6
  54.1 0.0 copy-start.8
  54.1 11.5 %all_to_all.22 = bf16[8,192,128]{2,1,0:T(8,128)(2,1)S(1)} all-to-all(bf16[8,192,128]{2,1,0:T(8,128)(2,1)S(1)} %add_convert_fusion), channel_id=1, replica_groups={{0,16,32,48,64,80,96,112},{8,24,40,56,72,88,104,120},{1,17,33,49,65,81,..., dimensions={0} | all-to-all | bytes 786432 | tf_op jit(solution)/shard_map/all_to_all | solution.py:354
  65.6 0.1 convert_element_type.26
  65.7 0.1 broadcast_in_dim.7
  65.7 12.6 %all_to_all.23.tiles = bf16[8,192,128]{2,1,0:T(8,128)(2,1)S(1)} all-to-all(bf16[8,192,128]{2,1,0:T(8,128)(2,1)S(1)} %broadcast_in_dim.7), channel_id=1, replica_groups=mesh['slab'=16,'tile'=8] {'tile'}, dimensions={0} | all-to-all | bytes 786432 | tf_op jit(solution)/shard_map/all_to_all | solution.py:379
  78.4 0.0 copy-done.6
  78.4 0.0 copy-done.8
  78.4 7.5 %back_project.1 = f32[8,64,1024]{2,1,0:T(8,128)} custom-call(f32[16]{0:T(128)S(1)} %copy-done.6, s32[16]{0:T(128)S(1)} %bitcast.6, bf16[8,192,128]{2,1,0:T(8,128)(2,1)S(1)} %all_to_all.23.tiles), custom_call_target="tpu_custom_call" | custom-call | tf_op jit(solution)/shard_map/back_project/pallas_call | solution.py:319
  (2 shorter events, 0.1 us)
Async XLA Ops:
  0.0 1.6 %copy-start = (f32[8,64,1024]{2,1,0:T(8,128)S(1)}, f32[8,64,1024]{2,1,0:T(8,128)}, u32[]{:S(2)}) copy-start(f32[8,64,1024]{2,1,0:T(8,128)} %volume.1) | copy-start | bytes 6291460
  1.6 0.7 copy-start.5
  2.2 0.7 copy-start.7
  2.9 38.2 %copy-start.1 = (bf16[32,128,128]{2,1,0:T(8,128)(2,1)S(1)}, bf16[32,128,128]{2,1,0:T(8,128)(2,1)}, u32[]{:S(2)}) copy-start(bf16[32,128,128]{2,1,0:T(8,128)(2,1)} %measured.1) | copy-start | bytes 3145732
  2.9 38.2 %copy-start.2 = (f32[2,128,128]{2,1,0:T(8,128)S(1)}, f32[2,128,128]{2,1,0:T(8,128)}, u32[]{:S(2)}) copy-start(f32[2,128,128]{2,1,0:T(8,128)} %probe.1) | copy-start | bytes 393220
  2.9 38.2 %copy-start.3 = (bf16[256,256]{1,0:T(8,128)(2,1)S(1)}, bf16[256,256]{1,0:T(8,128)(2,1)}, u32[]{:S(2)}) copy-start(bf16[256,256]{1,0:T(8,128)(2,1)} %constant.31.clone.gather) | copy-start | bytes 393220
  2.9 38.2 %copy-start.4 = (bf16[256,256]{1,0:T(8,128)(2,1)S(1)}, bf16[256,256]{1,0:T(8,128)(2,1)}, u32[]{:S(2)}) copy-start(bf16[256,256]{1,0:T(8,128)(2,1)} %constant.30.clone.spread) | copy-start | bytes 393220
  2.9 38.2 %copy-start.9 = (s32[32,1]{0,1:T(1,128)S(1)}, s32[32,1]{0,1:T(1,128)}, u32[]{:S(2)}) copy-start(s32[32,1]{0,1:T(1,128)} %param.14) | copy-start | bytes 388
  2.9 38.2 %copy-start.10 = (s32[32]{0:T(128)S(1)}, s32[32]{0:T(128)}, u32[]{:S(2)}) copy-start(s32[32]{0:T(128)} %shifts_in.1) | copy-start | bytes 388
  39.3 1.7 %collective-permute-start = (s16[8,192,128]{2,1,0:T(8,128)(2,1)S(1)}, s16[8,192,128]{2,1,0:T(8,128)(2,1)S(1)}, u32[]{:S(2)}, u32[]{:S(2)}) collective-permute-start(s16[8,192,128]{2,1,0:T(8,128)(2,1)S(1)} %all_to_all.21.near_phases), channel_id=1, source_target_pairs={{0,8},{8,0},{16,24},{24,16},{32,40},{40,32},{48,56},{56,48},{64,72... | collective-permute-start | bytes 1179656 | tf_op jit(solution)/shard_map/ppermute | solution.py:358
  52.1 1.8 %collective-permute-start.1 = (bf16[8,192,128]{2,1,0:T(8,128)(2,1)S(1)}, bf16[8,192,128]{2,1,0:T(8,128)(2,1)S(1)}, u32[]{:S(2)}, u32[]{:S(2)}) collective-permute-start(bf16[8,192,128]{2,1,0:T(8,128)(2,1)S(1)} %get-tuple-element.8), channel_id=1, source_target_pairs={{0,8},{8,0},{16,24},{24,16},{32,40},{40,32},{48,56},{56,48},{64,72... | collective-permute-start | bytes 1179656 | tf_op jit(solution)/shard_map/ppermute | solution.py:358
  54.0 24.3 %copy-start.6 = (f32[16]{0:T(128)S(1)}, f32[16]{0:T(128)}, u32[]{:S(2)}) copy-start(f32[16]{0:T(128)} %shears.3) | copy-start | bytes 196
  54.1 24.3 %copy-start.8 = (s32[16,1]{0,1:T(1,128)S(1)}, s32[16,1]{0,1:T(1,128)}, u32[]{:S(2)}) copy-start(s32[16,1]{0,1:T(1,128)} %param.11) | copy-start | bytes 196

commit v3 on v2

--- a/solution.py
+++ b/solution.py
@@ -24,8 +24,9 @@
 BWD_FINE, BWD_COARSE = 16, 4
 OWN_ROWS, EDGE_ROWS = 32, 16
 PAIR_ROWS = OWN_ROWS + EDGE_ROWS
-ROWS = (SLICES_DEV // 2) * PAIR_ROWS
-GROUP = 8
+PAIRS = SLICES_DEV // 2
+ROWS = PAIRS * PAIR_ROWS
+GROUP = 16
 UNPACK_UNROLL = 2
 VMEM_LIMIT = 40 * 1024 * 1024
 
@@ -68,73 +69,84 @@
     return pltpu.roll(value, value.shape[1] - steps, 1)
 
 
-def project_kernel(shears, shifts, volume, out, table, stack):
-    @pl.when(pl.program_id(0) == 0)
-    def _():
-        shape = (ANGLES, FWD_FINE * DEPTH)
-        shear = pick_rows([shears[i] for i in range(ANGLES)], shape, 0, ANGLES)
-        lane = iota(shape, 1)
-        beam = (lane % DEPTH).astype(jnp.float32)
-        centre = BLOCK * 0.5 + (beam - (DEPTH - 1) * 0.5) * shear
-        fine = (lane // DEPTH).astype(jnp.float32)
-        for j in range(FWD_COARSE):
-            table[j * ANGLES : (j + 1) * ANGLES] = bell(fine + float(FIRST + FWD_FINE * j), centre)
-
+def project_kernel(shears_in, shifts_in, volume_in, out, table, stack, volume, shears, shifts, sems):
+    copies = [
+        pltpu.make_async_copy(shears_in, shears, sems.at[0]),
+        pltpu.make_async_copy(shifts_in, shifts, sems.at[1]),
+    ]
+    for p in range(PAIRS):
+        part = pl.ds(p * 2, 2)
+        copies.append(pltpu.make_async_copy(volume_in.at[part], volume.at[part], sems.at[2 + p]))
+    for copy in copies:
+        copy.start()
+    copies[0].wait()
+    shape = (ANGLES, FWD_FINE * DEPTH)
+    shear = pick_rows([shears[i] for i in range(ANGLES)], shape, 0, ANGLES)
+    lane = iota(shape, 1)
+    beam = (lane % DEPTH).astype(jnp.float32)
+    centre = BLOCK * 0.5 + (beam - (DEPTH - 1) * 0.5) * shear
+    fine = (lane // DEPTH).astype(jnp.float32)
+    for j in range(FWD_COARSE):
+        table[j * ANGLES : (j + 1) * ANGLES] = bell(fine + float(FIRST + FWD_FINE * j), centre)
+    copies[1].wait()
     shape = (ANGLES, BLOCK)
     shift = pick_rows([shifts[i] for i in range(ANGLES)], shape, 0, ANGLES)
     lane = iota((8, BLOCK), 1)
-    edges = [[] for k in range(BLOCKS)]
-    for half in range(2):
-        rows = jnp.concatenate(
-            [volume[half], jnp.zeros((DEPTH, WIDE - BLOCKS * BLOCK), jnp.float32)], axis=1
-        )
-        stack[half, 0:DEPTH] = rows.astype(jnp.bfloat16)
-        for r in range(1, FWD_FINE):
-            stack[half, r * DEPTH : (r + 1) * DEPTH] = pltpu.roll(rows, r, 1).astype(jnp.bfloat16)
-        sums = jnp.dot(table[...], stack[half], preferred_element_type=jnp.float32)
-        total = pltpu.roll(sums[0:ANGLES], FIRST, 1)
-        for j in range(1, FWD_COARSE):
-            part = sums[j * ANGLES : (j + 1) * ANGLES]
-            total = total + pltpu.roll(part, FIRST + FWD_FINE * j, 1)
-        turns = total * (1.0 / (2.0 * math.pi))
-        turns = turns - jnp.floor(turns + 0.5)
-        fixed = jnp.minimum(jnp.floor(turns * 65536.0 + 0.5), 32767.0)
-        zero = jnp.zeros((ANGLES, BLOCK), jnp.float32)
-        block = [fixed[:, k * BLOCK : (k + 1) * BLOCK] for k in range(BLOCKS + 1)]
-        block = [zero] + block + [zero]
-        placed = []
+    outer = (lane < HALO) | (lane >= BLOCK - HALO)
+    zero = jnp.zeros(shape, jnp.float32)
+    for p in range(PAIRS):
+        copies[2 + p].wait()
+        for half in range(2):
+            rows = jnp.concatenate(
+                [volume[p * 2 + half], jnp.zeros((DEPTH, WIDE - BLOCKS * BLOCK), jnp.float32)], axis=1
+            )
+            for r in range(FWD_FINE):
+                moved = rows if r == 0 else pltpu.roll(rows, r, 1)
+                stack[p, r * DEPTH : (r + 1) * DEPTH, half * WIDE : (half + 1) * WIDE] = moved.astype(jnp.bfloat16)
+        both = jnp.dot(table[...], stack[p], preferred_element_type=jnp.float32)
+        edges = [[] for k in range(BLOCKS)]
+        for half in range(2):
+            sums = both[:, half * WIDE : (half + 1) * WIDE]
+            total = pltpu.roll(sums[0:ANGLES], FIRST, 1)
+            for j in range(1, FWD_COARSE):
+                total = total + pltpu.roll(sums[j * ANGLES : (j + 1) * ANGLES], FIRST + FWD_FINE * j, 1)
+            turns = total * (1.0 / (2.0 * math.pi))
+            turns = turns - jnp.floor(turns + 0.5)
+            fixed = jnp.minimum(jnp.floor(turns * 65536.0 + 0.5), 32767.0)
+            block = [zero] + [fixed[:, k * BLOCK : (k + 1) * BLOCK] for k in range(BLOCKS + 1)] + [zero]
+            placed = []
+            for k in range(BLOCKS):
+                here = jnp.where(shift == 0, block[k + 1], jnp.where(shift > 0, block[k], block[k + 2]))
+                placed.append(here.astype(jnp.int32))
+            nothing = jnp.zeros(shape, jnp.int32)
+            around = [nothing] + placed + [nothing]
+            for k in range(BLOCKS):
+                top = p * PAIR_ROWS + half * ANGLES
+                out[k, top : top + ANGLES] = placed[k].astype(jnp.int16)
+                after, before = around[k + 2], around[k]
+                low = jnp.where(lane < HALO, after[:8], before[:8])
+                high = jnp.where(lane < HALO, after[8:], before[8:])
+                edges[k].append(jnp.where(outer, low, pltpu.roll(high, BLOCK // 2, 1)))
         for k in range(BLOCKS):
-            here = jnp.where(shift == 0, block[k + 1], jnp.where(shift > 0, block[k], block[k + 2]))
-            placed.append(here.astype(jnp.int32))
-        zero = jnp.zeros((ANGLES, BLOCK), jnp.int32)
-        around = [zero] + placed + [zero]
-        for k in range(BLOCKS):
-            out[k, half * ANGLES : (half + 1) * ANGLES] = placed[k].astype(jnp.int16)
-            after, before = around[k + 2], around[k]
-            low = jnp.where(lane < HALO, after[:8], before[:8])
-            high = jnp.where(lane < HALO, after[8:], before[8:])
-            outer = (lane < HALO) | (lane >= BLOCK - HALO)
-            edge = jnp.where(outer, low, pltpu.roll(high, BLOCK // 2, 1))
-            edges[k].append(edge)
-    for k in range(BLOCKS):
-        out[k, OWN_ROWS:PAIR_ROWS] = jnp.concatenate(edges[k], axis=0).astype(jnp.int16)
+            top = p * PAIR_ROWS + OWN_ROWS
+            out[k, top : top + EDGE_ROWS] = jnp.concatenate(edges[k], axis=0).astype(jnp.int16)
 
 
 def project(shears, shifts, volume):
+    hbm = pl.BlockSpec(memory_space=pltpu.HBM)
     return pl.pallas_call(
         project_kernel,
         name="project",
-        grid=(SLICES_DEV // 2,),
-        in_specs=[
-            pl.BlockSpec(memory_space=pltpu.SMEM),
-            pl.BlockSpec(memory_space=pltpu.SMEM),
-            pl.BlockSpec((2, DEPTH, BLOCKS * BLOCK), lambda p: (p, 0, 0)),
-        ],
-        out_specs=pl.BlockSpec((TILES, PAIR_ROWS, BLOCK), lambda p: (0, p, 0)),
+        in_specs=[hbm, hbm, hbm],
+        out_specs=pl.BlockSpec(memory_space=pltpu.VMEM),
         out_shape=jax.ShapeDtypeStruct((TILES, ROWS, BLOCK), jnp.int16),
         scratch_shapes=[
             pltpu.VMEM((FWD_COARSE * ANGLES, FWD_FINE * DEPTH), jnp.bfloat16),
-            pltpu.VMEM((2, FWD_FINE * DEPTH, WIDE), jnp.bfloat16),
+            pltpu.VMEM((PAIRS, FWD_FINE * DEPTH, 2 * WIDE), jnp.bfloat16),
+            pltpu.VMEM((SLICES_DEV, DEPTH, BLOCKS * BLOCK), jnp.float32),
+            pltpu.SMEM((ANGLES,), jnp.float32),
+            pltpu.SMEM((ANGLES,), jnp.int32),
+            pltpu.SemaphoreType.DMA((2 + PAIRS,)),
         ],
         compiler_params=pltpu.CompilerParams(vmem_limit_bytes=VMEM_LIMIT),
     )(shears, shifts, volume)
@@ -271,65 +283,84 @@
     )(parity, owners, shifts, near_phases, far_phases, probe, measured, spread, gather)
 
 
-def back_kernel(shears, shifts, tiles, out, table, stack):
-    @pl.when(pl.program_id(0) == 0)
-    def _():
-        shape = (DEPTH, BWD_FINE * ANGLES)
-        shear = pick_rows([shears[i] for i in range(ANGLES)], shape, 1, ANGLES)
-        beam = iota(shape, 0).astype(jnp.float32)
-        centre = BLOCK * 0.5 + (beam - (DEPTH - 1) * 0.5) * shear
-        fine = (iota(shape, 1) // ANGLES).astype(jnp.float32)
-        for j in range(BWD_COARSE):
-            table[j * DEPTH : (j + 1) * DEPTH] = bell(fine + float(FIRST + BWD_FINE * j), centre)
-
+def back_kernel(shears_in, shifts_in, tiles, out_hbm, table, stack, out, shears, shifts, sems):
+    copies = [
+        pltpu.make_async_copy(shears_in, shears, sems.at[0]),
+        pltpu.make_async_copy(shifts_in, shifts, sems.at[1]),
+    ]
+    for copy in copies:
+        copy.start()
+    copies[0].wait()
+    shape = (DEPTH, BWD_FINE * ANGLES)
+    shear = pick_rows([shears[i] for i in range(ANGLES)], shape, 1, ANGLES)
+    beam = iota(shape, 0).astype(jnp.float32)
+    centre = BLOCK * 0.5 + (beam - (DEPTH - 1) * 0.5) * shear
+    fine = (iota(shape, 1) // ANGLES).astype(jnp.float32)
+    for j in range(BWD_COARSE):
+        table[j * DEPTH : (j + 1) * DEPTH] = bell(fine + float(FIRST + BWD_FINE * j), centre)
+    copies[1].wait()
     shape = (ANGLES, BLOCK)
     shift = pick_rows([shifts[i] for i in range(ANGLES)], shape, 0, ANGLES)
     lane = iota(shape, 1)
-    for half in range(2):
-        own, margin = [], []
-        for k in range(TILES):
-            own.append(tiles[k, half * ANGLES : (half + 1) * ANGLES].astype(jnp.float32))
-            packed = tiles[k, OWN_ROWS:PAIR_ROWS].astype(jnp.float32)[half * 8 : half * 8 + 8]
-            margin.append(jnp.concatenate([packed, pltpu.roll(packed, BLOCK // 2, 1)], axis=0))
-        whole = []
-        for k in range(TILES):
-            total = own[k]
-            if k > 0:
-                total = total + jnp.where(lane < HALO, margin[k - 1], 0.0)
-            if k < TILES - 1:
-                total = total + jnp.where(lane >= BLOCK - HALO, margin[k + 1], 0.0)
-            whole.append(total.astype(jnp.bfloat16).astype(jnp.float32))
-        zero = jnp.zeros(shape, jnp.float32)
-        whole = [zero] + whole + [zero, zero]
-        placed = [
-            jnp.where(shift == 0, whole[k + 1], jnp.where(shift > 0, whole[k + 2], whole[k])) for k in range(BLOCKS + 1)
-        ]
-        placed = jnp.concatenate(placed, axis=1)
-        stack[half, 0:ANGLES] = placed.astype(jnp.bfloat16)
-        for r in range(1, BWD_FINE):
-            stack[half, r * ANGLES : (r + 1) * ANGLES] = left(placed, r).astype(jnp.bfloat16)
-        sums = jnp.dot(table[...], stack[half], preferred_element_type=jnp.float32)
-        total = left(sums[0:DEPTH], FIRST)
-        for j in range(1, BWD_COARSE):
-            total = total + left(sums[j * DEPTH : (j + 1) * DEPTH], FIRST + BWD_FINE * j)
-        out[half] = total[:, : BLOCKS * BLOCK]
+    zero = jnp.zeros(shape, jnp.float32)
+    sends = []
+    for p in range(PAIRS):
+        top = p * PAIR_ROWS
+        for half in range(2):
+            own, margin = [], []
+            for k in range(TILES):
+                first = top + half * ANGLES
+                own.append(tiles[k, first : first + ANGLES].astype(jnp.float32))
+                packed = tiles[k, top + OWN_ROWS : top + PAIR_ROWS].astype(jnp.float32)[half * 8 : half * 8 + 8]
+                margin.append(jnp.concatenate([packed, pltpu.roll(packed, BLOCK // 2, 1)], axis=0))
+            whole = []
+            for k in range(TILES):
+                total = own[k]
+                if k > 0:
+                    total = total + jnp.where(lane < HALO, margin[k - 1], 0.0)
+                if k < TILES - 1:
+                    total = total + jnp.where(lane >= BLOCK - HALO, margin[k + 1], 0.0)
+                whole.append(total.astype(jnp.bfloat16).astype(jnp.float32))
+            whole = [zero] + whole + [zero, zero]
+            placed = jnp.concatenate(
+                [
+                    jnp.where(shift == 0, whole[k + 1], jnp.where(shift > 0, whole[k + 2], whole[k]))
+                    for k in range(BLOCKS + 1)
+                ],
+                axis=1,
+            )
+            for r in range(BWD_FINE):
+                moved = left(placed, FIRST + r)
+                stack[p, r * ANGLES : (r + 1) * ANGLES, half * WIDE : (half + 1) * WIDE] = moved.astype(jnp.bfloat16)
+        both = jnp.dot(table[...], stack[p], preferred_element_type=jnp.float32)
+        for half in range(2):
+            sums = both[:, half * WIDE : (half + 1) * WIDE]
+            total = sums[0:DEPTH]
+            for j in range(1, BWD_COARSE):
+                total = total + left(sums[j * DEPTH : (j + 1) * DEPTH], BWD_FINE * j)
+            out[p * 2 + half] = total[:, : BLOCKS * BLOCK]
+        part = pl.ds(p * 2, 2)
+        sends.append(pltpu.make_async_copy(out.at[part], out_hbm.at[part], sems.at[2 + p]))
+        sends[-1].start()
+    for send in sends:
+        send.wait()
 
 
 def back_project(shears, shifts, tiles):
+    hbm = pl.BlockSpec(memory_space=pltpu.HBM)
     return pl.pallas_call(
         back_kernel,
         name="back_project",
-        grid=(SLICES_DEV // 2,),
-        in_specs=[
-            pl.BlockSpec(memory_space=pltpu.SMEM),
-            pl.BlockSpec(memory_space=pltpu.SMEM),
-            pl.BlockSpec((TILES, PAIR_ROWS, BLOCK), lambda p: (0, p, 0)),
-        ],
-        out_specs=pl.BlockSpec((2, DEPTH, BLOCKS * BLOCK), lambda p: (p, 0, 0)),
+        in_specs=[hbm, hbm, pl.BlockSpec(memory_space=pltpu.VMEM)],
+        out_specs=hbm,
         out_shape=jax.ShapeDtypeStruct((SLICES_DEV, DEPTH, BLOCKS * BLOCK), jnp.float32),
         scratch_shapes=[
             pltpu.VMEM((BWD_COARSE * DEPTH, BWD_FINE * ANGLES), jnp.bfloat16),
-            pltpu.VMEM((2, BWD_FINE * ANGLES, WIDE), jnp.bfloat16),
+            pltpu.VMEM((PAIRS, BWD_FINE * ANGLES, 2 * WIDE), jnp.bfloat16),
+            pltpu.VMEM((SLICES_DEV, DEPTH, BLOCKS * BLOCK), jnp.float32),
+            pltpu.SMEM((ANGLES,), jnp.float32),
+            pltpu.SMEM((ANGLES,), jnp.int32),
+            pltpu.SemaphoreType.DMA((2 + PAIRS,)),
         ],
         compiler_params=pltpu.CompilerParams(vmem_limit_bytes=VMEM_LIMIT),
     )(shears, shifts, tiles)

time: 86.1 us -> 82.7 us (0.961)
  Pallas kernels: 24.7 us -> 21 us
    pallas_call x2, Pallas kernels: 13.6 us -> 11.2 us  [the longest x1 6.14 us: back_project(): pl.pallas_call(back_kernel, name='back_project', in_specs=[hbm, hbm, pl.B...]
    pallas_call x1, Pallas kernels: 11 us -> 9.85 us  [frame_gradients(): pl.pallas_call(frames_kernel, name='frame_gradients', in_specs=[smem, hbm...]
where the time goes in v3:
time: 82.7 us; the launch traced here: 82.4 us
  blocking collectives  54.2 us (66%)
  Pallas kernels  21 us (25%)
  waiting for transfers between devices  3.3 us (4%)
  local copies, waits for them, and re-layouts  3.04 us (4%)
    all_to_all x2, blocking collectives, between_chips(): lax.all_to_all(value, 'slab', 0, 0, tiled=True, axis_index_groups=groups)  23.9 us
    all_to_all x1, blocking collectives, body(): landed = lax.all_to_all(partials, 'tile', 0, 0, tiled=True)  17.7 us
    all_to_all x1, blocking collectives, body(): lax.all_to_all(copies_of(grad.astype(jnp.bfloat16), TILES), 'tile', 0, 0,...  12.6 us
    pallas_call x1, Pallas kernels, frame_gradients(): pl.pallas_call(frames_kernel, name='frame_gradients', in_specs=[smem, hbm...  9.85 us
    pallas_call x1, Pallas kernels, back_project(): pl.pallas_call(back_kernel, name='back_project', in_specs=[hbm, hbm, pl.B...  6.14 us
    pallas_call x1, Pallas kernels, project(): pl.pallas_call(project_kernel, name='project', in_specs=[hbm, hbm, hbm],...  5.04 us
    ppermute x2, waiting for transfers between devices, between_cores(): lax.ppermute(value, 'slab', [(i, i ^ 1) for i in range(lax.axis_size('sla...  3.3 us
    unnamed x22, local copies, waits for them, and re-layouts  2.94 us
  transfers between devices with their start and end apart: 2, of which 2 were waited for; matrix products, arithmetic and copies ran while one was open for 0% of the time, Pallas kernels for 0%

profile of v3, /device:TPU:0, one launch (start us, length us, event | category | flops | bytes accessed | tf_op | source)
XLA Modules:
  0.0 82.4 jit_solution(18098893077894230482)
XLA Ops:
  0.0 0.0 copy-start
  0.0 1.6 %copy-done = f32[8,64,1024]{2,1,0:T(8,128)S(1)} copy-done((f32[8,64,1024]{2,1,0:T(8,128)S(1)}, f32[8,64,1024]{2,1,0:T(8,128)}, u32[]{:S(2)}) %copy-start) | copy-done | bytes 2097176
  1.6 0.0 copy-start.5
  1.6 0.7 copy-done.5
  2.2 0.0 copy-start.7
  2.2 0.7 copy-done.7
  2.9 0.0 copy-start.1
  2.9 0.0 copy-start.2
  2.9 0.0 copy-start.3
  2.9 0.0 copy-start.4
  2.9 0.0 copy-start.9
  2.9 0.0 copy-start.10
  2.9 5.0 %project.1 = s16[8,192,128]{2,1,0:T(8,128)(2,1)S(1)} custom-call(f32[16]{0:T(128)S(1)} %copy-done.5, s32[16]{0:T(128)S(1)} %bitcast.5, f32[8,64,1024]{2,1,0:T(8,128)S(1)} %copy-done), custom_call_target="tpu_custom_call" | custom-call | tf_op jit(solution)/shard_map/project/pallas_call | solution.py:137
  8.0 17.7 %all_to_all.20 = s16[8,192,128]{2,1,0:T(8,128)(2,1)S(1)} all-to-all(s16[8,192,128]{2,1,0:T(8,128)(2,1)S(1)} %project.1), channel_id=1, replica_groups=mesh['slab'=16,'tile'=8] {'tile'}, dimensions={0} | all-to-all | bytes 786432 | tf_op jit(solution)/shard_map/all_to_all | solution.py:397
  25.7 0.1 convert_reduce_fusion
  25.8 0.1 broadcast_in_dim.6
  25.8 12.4 %all_to_all.21.near_phases = s16[8,192,128]{2,1,0:T(8,128)(2,1)S(1)} all-to-all(s16[8,192,128]{2,1,0:T(8,128)(2,1)S(1)} %broadcast_in_dim.6), channel_id=1, replica_groups={{0,16,32,48,64,80,96,112},{8,24,40,56,72,88,104,120},{1,17,33,49,65,81,..., dimensions={0} | all-to-all | bytes 786432 | tf_op jit(solution)/shard_map/all_to_all | solution.py:385
  38.2 0.0 collective-permute-start
  38.2 1.7 %collective-permute-done.far_phases = s16[8,192,128]{2,1,0:T(8,128)(2,1)S(1)} collective-permute-done((s16[8,192,128]{2,1,0:T(8,128)(2,1)S(1)}, s16[8,192,128]{2,1,0:T(8,128)(2,1)S(1)}, u32[]{:S(2)}, u32[]{:S(2)}) %collective-permute-start) | collective-permute-done | bytes 393248 | tf_op jit(solution)/shard_map/ppermute | solution.py:389
  39.9 0.0 copy-done.1
  39.9 0.0 copy-done.2
  39.9 0.0 copy-done.3
  39.9 0.0 copy-done.4
  40.0 0.0 copy-done.9
  40.0 0.0 copy-done.10
  40.0 9.8 %frame_gradients.1 = (bf16[8,192,128]{2,1,0:T(8,128)(2,1)S(1)}, bf16[8,192,128]{2,1,0:T(8,128)(2,1)S(1)}) custom-call(s32[1]{0:T(128)} %bitcast.1.parity, s32[32]{0:T(128)S(1)} %bitcast.7, s32[32]{0:T(128)S(1)} %copy-done.10, s16[8,192,128]{2,1,0:T(8,128)(2,1)S(1)} %all_to_all.21.near_phases, s16[8,192,128]{2,1,0:T(8,128)(2,1)S(1)} %collective-permute-done.far_phases, ...), custom_call_target="tpu_custom_call" | custom-call | tf_op jit(solution)/shard_map/frame_gradients/pallas_call | solution.py:272
  49.8 0.2 collective-permute-start.1
  50.1 1.6 %collective-permute-done.1 = bf16[8,192,128]{2,1,0:T(8,128)(2,1)S(1)} collective-permute-done((bf16[8,192,128]{2,1,0:T(8,128)(2,1)S(1)}, bf16[8,192,128]{2,1,0:T(8,128)(2,1)S(1)}, u32[]{:S(2)}, u32[]{:S(2)}) %collective-permute-start.1) | collective-permute-done | bytes 393248 | tf_op jit(solution)/shard_map/ppermute | solution.py:389
  51.6 0.1 add_convert_fusion
  51.7 0.0 copy-start.6
  51.8 0.0 copy-start.8
  51.8 11.5 %all_to_all.22 = bf16[8,192,128]{2,1,0:T(8,128)(2,1)S(1)} all-to-all(bf16[8,192,128]{2,1,0:T(8,128)(2,1)S(1)} %add_convert_fusion), channel_id=1, replica_groups={{0,16,32,48,64,80,96,112},{8,24,40,56,72,88,104,120},{1,17,33,49,65,81,..., dimensions={0} | all-to-all | bytes 786432 | tf_op jit(solution)/shard_map/all_to_all | solution.py:385
  63.3 0.1 convert_element_type.26
  63.4 0.1 broadcast_in_dim.7
  63.5 12.6 %all_to_all.23.tiles = bf16[8,192,128]{2,1,0:T(8,128)(2,1)S(1)} all-to-all(bf16[8,192,128]{2,1,0:T(8,128)(2,1)S(1)} %broadcast_in_dim.7), channel_id=1, replica_groups=mesh['slab'=16,'tile'=8] {'tile'}, dimensions={0} | all-to-all | bytes 786432 | tf_op jit(solution)/shard_map/all_to_all | solution.py:410
  76.1 0.0 copy-done.6
  76.1 0.0 copy-done.8
  76.1 6.1 %back_project.1 = f32[8,64,1024]{2,1,0:T(8,128)} custom-call(f32[16]{0:T(128)S(1)} %copy-done.6, s32[16]{0:T(128)S(1)} %bitcast.6, bf16[8,192,128]{2,1,0:T(8,128)(2,1)S(1)} %all_to_all.23.tiles), custom_call_target="tpu_custom_call" | custom-call | tf_op jit(solution)/shard_map/back_project/pallas_call | solution.py:351
  (2 shorter events, 0.1 us)
Async XLA Ops:
  0.0 1.6 %copy-start = (f32[8,64,1024]{2,1,0:T(8,128)S(1)}, f32[8,64,1024]{2,1,0:T(8,128)}, u32[]{:S(2)}) copy-start(f32[8,64,1024]{2,1,0:T(8,128)} %volume_in.1) | copy-start | bytes 6291460
  1.6 0.7 copy-start.5
  2.2 0.7 copy-start.7
  2.9 37.0 %copy-start.1 = (bf16[32,128,128]{2,1,0:T(8,128)(2,1)S(1)}, bf16[32,128,128]{2,1,0:T(8,128)(2,1)}, u32[]{:S(2)}) copy-start(bf16[32,128,128]{2,1,0:T(8,128)(2,1)} %measured.1) | copy-start | bytes 3145732
  2.9 37.0 %copy-start.2 = (f32[2,128,128]{2,1,0:T(8,128)S(1)}, f32[2,128,128]{2,1,0:T(8,128)}, u32[]{:S(2)}) copy-start(f32[2,128,128]{2,1,0:T(8,128)} %probe.1) | copy-start | bytes 393220
  2.9 37.0 %copy-start.3 = (bf16[256,256]{1,0:T(8,128)(2,1)S(1)}, bf16[256,256]{1,0:T(8,128)(2,1)}, u32[]{:S(2)}) copy-start(bf16[256,256]{1,0:T(8,128)(2,1)} %constant.31.clone.gather) | copy-start | bytes 393220
  2.9 37.0 %copy-start.4 = (bf16[256,256]{1,0:T(8,128)(2,1)S(1)}, bf16[256,256]{1,0:T(8,128)(2,1)}, u32[]{:S(2)}) copy-start(bf16[256,256]{1,0:T(8,128)(2,1)} %constant.30.clone.spread) | copy-start | bytes 393220
  2.9 37.0 %copy-start.9 = (s32[32,1]{0,1:T(1,128)S(1)}, s32[32,1]{0,1:T(1,128)}, u32[]{:S(2)}) copy-start(s32[32,1]{0,1:T(1,128)} %param.14) | copy-start | bytes 388
  2.9 37.0 %copy-start.10 = (s32[32]{0:T(128)S(1)}, s32[32]{0:T(128)}, u32[]{:S(2)}) copy-start(s32[32]{0:T(128)} %shifts_in.1) | copy-start | bytes 388
  38.2 1.7 %collective-permute-start = (s16[8,192,128]{2,1,0:T(8,128)(2,1)S(1)}, s16[8,192,128]{2,1,0:T(8,128)(2,1)S(1)}, u32[]{:S(2)}, u32[]{:S(2)}) collective-permute-start(s16[8,192,128]{2,1,0:T(8,128)(2,1)S(1)} %all_to_all.21.near_phases), channel_id=1, source_target_pairs={{0,8},{8,0},{16,24},{24,16},{32,40},{40,32},{48,56},{56,48},{64,72... | collective-permute-start | bytes 1179656 | tf_op jit(solution)/shard_map/ppermute | solution.py:389
  49.8 1.8 %collective-permute-start.1 = (bf16[8,192,128]{2,1,0:T(8,128)(2,1)S(1)}, bf16[8,192,128]{2,1,0:T(8,128)(2,1)S(1)}, u32[]{:S(2)}, u32[]{:S(2)}) collective-permute-start(bf16[8,192,128]{2,1,0:T(8,128)(2,1)S(1)} %get-tuple-element.8), channel_id=1, source_target_pairs={{0,8},{8,0},{16,24},{24,16},{32,40},{40,32},{48,56},{56,48},{64,72... | collective-permute-start | bytes 1179656 | tf_op jit(solution)/shard_map/ppermute | solution.py:389
  51.7 24.3 %copy-start.6 = (f32[16]{0:T(128)S(1)}, f32[16]{0:T(128)}, u32[]{:S(2)}) copy-start(f32[16]{0:T(128)} %shears_in.3) | copy-start | bytes 196
  51.8 24.3 %copy-start.8 = (s32[16,1]{0,1:T(1,128)S(1)}, s32[16,1]{0,1:T(1,128)}, u32[]{:S(2)}) copy-start(s32[16,1]{0,1:T(1,128)} %param.11) | copy-start | bytes 196

commit v4 on v3

--- a/solution.py
+++ b/solution.py
@@ -22,16 +22,16 @@
 WIDE = 9 * BLOCK
 FWD_FINE, FWD_COARSE = 4, 14
 BWD_FINE, BWD_COARSE = 16, 4
-OWN_ROWS, EDGE_ROWS = 32, 16
-PAIR_ROWS = OWN_ROWS + EDGE_ROWS
+OWN_ROWS, EDGE_ROWS = ANGLES * SLICES_DEV, ANGLES // 2 * SLICES_DEV
 PAIRS = SLICES_DEV // 2
-ROWS = PAIRS * PAIR_ROWS
+ROWS = OWN_ROWS + EDGE_ROWS
 GROUP = 16
 UNPACK_UNROLL = 2
 VMEM_LIMIT = 40 * 1024 * 1024
+ALL_VMEM = 60 * 1024 * 1024
 
 SIN_TERMS = (3.14159264, -5.16771008, 2.55007752, -0.598291286, 0.0776576603)
-COS_TERMS = (1.0, -4.93480214, 4.05870916, -1.335212, 0.234937314, -0.0243963244)
+COS_TERMS = (0.999999953, -4.93479283, 4.05841135, -1.33187657, 0.219689611)
 
 
 def iota(shape, dim):
@@ -69,7 +69,7 @@
     return pltpu.roll(value, value.shape[1] - steps, 1)
 
 
-def project_kernel(shears_in, shifts_in, volume_in, out, table, stack, volume, shears, shifts, sems):
+def project_kernel(shears_in, shifts_in, volume_in, out, table, stack, volume, gathered, shears, shifts, sems):
     copies = [
         pltpu.make_async_copy(shears_in, shears, sems.at[0]),
         pltpu.make_async_copy(shifts_in, shifts, sems.at[1]),
@@ -104,7 +104,6 @@
                 moved = rows if r == 0 else pltpu.roll(rows, r, 1)
                 stack[p, r * DEPTH : (r + 1) * DEPTH, half * WIDE : (half + 1) * WIDE] = moved.astype(jnp.bfloat16)
         both = jnp.dot(table[...], stack[p], preferred_element_type=jnp.float32)
-        edges = [[] for k in range(BLOCKS)]
         for half in range(2):
             sums = both[:, half * WIDE : (half + 1) * WIDE]
             total = pltpu.roll(sums[0:ANGLES], FIRST, 1)
@@ -117,19 +116,18 @@
             placed = []
             for k in range(BLOCKS):
                 here = jnp.where(shift == 0, block[k + 1], jnp.where(shift > 0, block[k], block[k + 2]))
-                placed.append(here.astype(jnp.int32))
-            nothing = jnp.zeros(shape, jnp.int32)
-            around = [nothing] + placed + [nothing]
+                placed.append(here)
+            around = [zero] + placed + [zero]
+            s = p * 2 + half
             for k in range(BLOCKS):
-                top = p * PAIR_ROWS + half * ANGLES
-                out[k, top : top + ANGLES] = placed[k].astype(jnp.int16)
+                gathered[k, pl.ds(s, ANGLES, stride=SLICES_DEV), :] = placed[k]
                 after, before = around[k + 2], around[k]
                 low = jnp.where(lane < HALO, after[:8], before[:8])
                 high = jnp.where(lane < HALO, after[8:], before[8:])
-                edges[k].append(jnp.where(outer, low, pltpu.roll(high, BLOCK // 2, 1)))
-        for k in range(BLOCKS):
-            top = p * PAIR_ROWS + OWN_ROWS
-            out[k, top : top + EDGE_ROWS] = jnp.concatenate(edges[k], axis=0).astype(jnp.int16)
+                edge = jnp.where(outer, low, pltpu.roll(high, BLOCK // 2, 1))
+                gathered[k, pl.ds(OWN_ROWS + s, ANGLES // 2, stride=SLICES_DEV), :] = edge
+    for k in range(BLOCKS):
+        out[k] = gathered[k].astype(jnp.int32).astype(jnp.int16)
 
 
 def project(shears, shifts, volume):
@@ -144,11 +142,12 @@
             pltpu.VMEM((FWD_COARSE * ANGLES, FWD_FINE * DEPTH), jnp.bfloat16),
             pltpu.VMEM((PAIRS, FWD_FINE * DEPTH, 2 * WIDE), jnp.bfloat16),
             pltpu.VMEM((SLICES_DEV, DEPTH, BLOCKS * BLOCK), jnp.float32),
+            pltpu.VMEM((BLOCKS, ROWS, BLOCK), jnp.float32),
             pltpu.SMEM((ANGLES,), jnp.float32),
             pltpu.SMEM((ANGLES,), jnp.int32),
             pltpu.SemaphoreType.DMA((2 + PAIRS,)),
         ],
-        compiler_params=pltpu.CompilerParams(vmem_limit_bytes=VMEM_LIMIT),
+        compiler_params=pltpu.CompilerParams(vmem_limit_bytes=ALL_VMEM),
     )(shears, shifts, volume)
 
 
@@ -168,17 +167,17 @@
 
     def unpack(chip, carried):
         for which, phases in ((core, near_phases), (1 - core, far_phases)):
-            start = pl.multiple_of((chip * 2 + which) * BLOCK, BLOCK)
-            for p in range(SLICES_DEV // 2):
-                base = pl.multiple_of(start + p * OWN_ROWS, OWN_ROWS)
-                rows = phases[chip, p * PAIR_ROWS : (p + 1) * PAIR_ROWS].astype(jnp.int32).astype(jnp.float32)
-                own[pl.ds(base, OWN_ROWS), :] = rows[:OWN_ROWS]
-                for half in range(2):
-                    packed = rows[OWN_ROWS + half * 8 : OWN_ROWS + half * 8 + 8]
-                    edge[pl.ds(base + half * 16, 8), :] = packed
-                    edge[pl.ds(base + half * 16 + 8, 8), :] = pltpu.roll(packed, BLOCK // 2, 1)
-            own_sum[pl.ds(start, BLOCK), :] = jnp.zeros((BLOCK, BLOCK), jnp.float32)
-            edge_sum[pl.ds(start, BLOCK), :] = jnp.zeros((BLOCK, BLOCK), jnp.float32)
+            base = pl.multiple_of((chip * 2 + which) * SLICES_DEV, SLICES_DEV)
+            rows = phases[chip].astype(jnp.int32).astype(jnp.float32)
+            zero = jnp.zeros((SLICES_DEV, BLOCK), jnp.float32)
+            for i in range(ANGLES):
+                here = pl.ds(base + i * SIDE, SLICES_DEV)
+                first = OWN_ROWS + i % (ANGLES // 2) * SLICES_DEV
+                packed = rows[first : first + SLICES_DEV]
+                own[here, :] = rows[i * SLICES_DEV : (i + 1) * SLICES_DEV]
+                edge[here, :] = packed if i < ANGLES // 2 else pltpu.roll(packed, BLOCK // 2, 1)
+                own_sum[here, :] = zero
+                edge_sum[here, :] = zero
         return carried
 
     lax.fori_loop(0, SLABS // 2, unpack, 0, unroll=UNPACK_UNROLL)
@@ -198,7 +197,7 @@
         rows, inside, amount, waves, fields = [], [], [], [], []
         for k in range(GROUP):
             shift = shifts[first + k]
-            rows.append(pl.ds(owners[first + k], SIDE, stride=ANGLES))
+            rows.append(pl.ds(pl.multiple_of(owners[first + k] * SIDE, SIDE), SIDE))
             bound = jnp.where(shift >= 0, shift, shift + BLOCK)
             inside.append((lane >= bound) == (shift >= 0))
             amount.append(bound)
@@ -247,17 +246,13 @@
 
     def pack(chip, carried):
         for which, out in ((core, near_out), (1 - core, far_out)):
-            start = pl.multiple_of((chip * 2 + which) * BLOCK, BLOCK)
-            for p in range(SLICES_DEV // 2):
-                base = pl.multiple_of(start + p * OWN_ROWS, OWN_ROWS)
-                top = p * PAIR_ROWS
-                out[chip, top : top + OWN_ROWS] = own_sum[pl.ds(base, OWN_ROWS), :].astype(jnp.bfloat16)
-                packed = []
-                for half in range(2):
-                    low = edge_sum[pl.ds(base + half * 16, 8), :]
-                    high = edge_sum[pl.ds(base + half * 16 + 8, 8), :]
-                    packed.append(jnp.where(outer, low, pltpu.roll(high, BLOCK // 2, 1)))
-                out[chip, top + OWN_ROWS : top + PAIR_ROWS] = jnp.concatenate(packed, axis=0).astype(jnp.bfloat16)
+            base = pl.multiple_of((chip * 2 + which) * SLICES_DEV, SLICES_DEV)
+            here = [pl.ds(base + i * SIDE, SLICES_DEV) for i in range(ANGLES)]
+            rows = [own_sum[here[i], :] for i in range(ANGLES)]
+            for i in range(ANGLES // 2):
+                high = pltpu.roll(edge_sum[here[i + ANGLES // 2], :], BLOCK // 2, 1)
+                rows.append(jnp.where(outer, edge_sum[here[i], :], high))
+            out[chip] = jnp.concatenate(rows, axis=0).astype(jnp.bfloat16)
         return carried
 
     lax.fori_loop(0, SLABS // 2, pack, 0, unroll=UNPACK_UNROLL)
@@ -283,7 +278,7 @@
     )(parity, owners, shifts, near_phases, far_phases, probe, measured, spread, gather)
 
 
-def back_kernel(shears_in, shifts_in, tiles, out_hbm, table, stack, out, shears, shifts, sems):
+def back_kernel(shears_in, shifts_in, tiles, out_hbm, table, stack, out, gathered, shears, shifts, sems):
     copies = [
         pltpu.make_async_copy(shears_in, shears, sems.at[0]),
         pltpu.make_async_copy(shifts_in, shifts, sems.at[1]),
@@ -304,14 +299,15 @@
     lane = iota(shape, 1)
     zero = jnp.zeros(shape, jnp.float32)
     sends = []
+    for k in range(TILES):
+        gathered[k] = tiles[k].astype(jnp.float32)
     for p in range(PAIRS):
-        top = p * PAIR_ROWS
         for half in range(2):
             own, margin = [], []
             for k in range(TILES):
-                first = top + half * ANGLES
-                own.append(tiles[k, first : first + ANGLES].astype(jnp.float32))
-                packed = tiles[k, top + OWN_ROWS : top + PAIR_ROWS].astype(jnp.float32)[half * 8 : half * 8 + 8]
+                s = p * 2 + half
+                own.append(gathered[k, pl.ds(s, ANGLES, stride=SLICES_DEV), :])
+                packed = gathered[k, pl.ds(OWN_ROWS + s, ANGLES // 2, stride=SLICES_DEV), :]
                 margin.append(jnp.concatenate([packed, pltpu.roll(packed, BLOCK // 2, 1)], axis=0))
             whole = []
             for k in range(TILES):
@@ -358,6 +354,7 @@
             pltpu.VMEM((BWD_COARSE * DEPTH, BWD_FINE * ANGLES), jnp.bfloat16),
             pltpu.VMEM((PAIRS, BWD_FINE * ANGLES, 2 * WIDE), jnp.bfloat16),
             pltpu.VMEM((SLICES_DEV, DEPTH, BLOCKS * BLOCK), jnp.float32),
+            pltpu.VMEM((TILES, ROWS, BLOCK), jnp.float32),
             pltpu.SMEM((ANGLES,), jnp.float32),
             pltpu.SMEM((ANGLES,), jnp.int32),
             pltpu.SemaphoreType.DMA((2 + PAIRS,)),

time: 82.7 us -> 77.8 us (0.941)
  local copies, waits for them, and re-layouts: 3.04 us -> 0.14 us
  Pallas kernels: 21 us -> 18.9 us
    pallas_call x1, Pallas kernels: 9.85 us -> 6.27 us  [frame_gradients(): pl.pallas_call(frames_kernel, name='frame_gradients', in_specs=[smem, hbm...]
    unnamed x22 -> x16, local copies, waits for them, and re-layouts: 2.94 us -> 0.04 us
    pallas_call x1, Pallas kernels: 5.04 us -> 6.4 us  [project(): pl.pallas_call(project_kernel, name='project', in_specs=[hbm, hbm, hbm],...]
where the time goes in v4:
time: 77.8 us; the launch traced here: 77.5 us
  blocking collectives  54.4 us (70%)
  Pallas kernels  18.9 us (24%)
  waiting for transfers between devices  3.31 us (4%)
    all_to_all x2, blocking collectives, between_chips(): lax.all_to_all(value, 'slab', 0, 0, tiled=True, axis_index_groups=groups)  23.9 us
    all_to_all x1, blocking collectives, body(): landed = lax.all_to_all(partials, 'tile', 0, 0, tiled=True)  17.9 us
    all_to_all x1, blocking collectives, body(): lax.all_to_all(copies_of(grad.astype(jnp.bfloat16), TILES), 'tile', 0, 0,...  12.6 us
    pallas_call x1, Pallas kernels, project(): pl.pallas_call(project_kernel, name='project', in_specs=[hbm, hbm, hbm],...  6.4 us
    pallas_call x1, Pallas kernels, frame_gradients(): pl.pallas_call(frames_kernel, name='frame_gradients', in_specs=[smem, hbm...  6.27 us
    pallas_call x1, Pallas kernels, back_project(): pl.pallas_call(back_kernel, name='back_project', in_specs=[hbm, hbm, pl.B...  6.18 us
    ppermute x2, waiting for transfers between devices, between_cores(): lax.ppermute(value, 'slab', [(i, i ^ 1) for i in range(lax.axis_size('sla...  3.31 us
  transfers between devices with their start and end apart: 2, of which 2 were waited for; matrix products, arithmetic and copies ran while one was open for 0% of the time, Pallas kernels for 0%

profile of v4, /device:TPU:0, one launch (start us, length us, event | category | flops | bytes accessed | tf_op | source)
XLA Modules:
  0.0 77.5 jit_solution(17311567318515070692)
XLA Ops:
  0.0 0.0 copy-start
  0.0 0.0 copy-start.1
  0.0 0.0 copy-start.2
  0.0 0.0 copy-start.3
  0.0 0.0 copy-start.6
  0.0 0.0 copy-start.7
  0.0 6.4 %project.1 = s16[8,192,128]{2,1,0:T(8,128)(2,1)} custom-call(f32[16]{0:T(128)} %shears_in.3, s32[16]{0:T(128)} %bitcast.5, f32[8,64,1024]{2,1,0:T(8,128)} %volume_in.1), custom_call_target="tpu_custom_call" | custom-call | tf_op jit(solution)/shard_map/project/pallas_call | solution.py:135
  6.4 17.9 %all_to_all.20 = s16[8,192,128]{2,1,0:T(8,128)(2,1)S(1)} all-to-all(s16[8,192,128]{2,1,0:T(8,128)(2,1)} %project.1), channel_id=1, replica_groups=mesh['slab'=16,'tile'=8] {'tile'}, dimensions={0} | all-to-all | bytes 786432 | tf_op jit(solution)/shard_map/all_to_all | solution.py:394
  24.3 0.1 convert_reduce_fusion
  24.5 0.1 broadcast_in_dim.6
  24.5 12.4 %all_to_all.21.near_phases = s16[8,192,128]{2,1,0:T(8,128)(2,1)S(1)} all-to-all(s16[8,192,128]{2,1,0:T(8,128)(2,1)S(1)} %broadcast_in_dim.6), channel_id=1, replica_groups={{0,16,32,48,64,80,96,112},{8,24,40,56,72,88,104,120},{1,17,33,49,65,81,..., dimensions={0} | all-to-all | bytes 786432 | tf_op jit(solution)/shard_map/all_to_all | solution.py:382
  36.9 0.0 collective-permute-start
  36.9 1.7 %collective-permute-done.far_phases = s16[8,192,128]{2,1,0:T(8,128)(2,1)S(1)} collective-permute-done((s16[8,192,128]{2,1,0:T(8,128)(2,1)S(1)}, s16[8,192,128]{2,1,0:T(8,128)(2,1)S(1)}, u32[]{:S(2)}, u32[]{:S(2)}) %collective-permute-start) | collective-permute-done | bytes 393248 | tf_op jit(solution)/shard_map/ppermute | solution.py:386
  38.6 0.0 copy-done
  38.6 0.0 copy-done.1
  38.6 0.0 copy-done.2
  38.6 0.0 copy-done.3
  38.6 0.0 copy-done.6
  38.6 0.0 copy-done.7
  38.7 6.3 %frame_gradients.1 = (bf16[8,192,128]{2,1,0:T(8,128)(2,1)S(1)}, bf16[8,192,128]{2,1,0:T(8,128)(2,1)S(1)}) custom-call(s32[1]{0:T(128)} %bitcast.1.parity, s32[32]{0:T(128)S(1)} %bitcast.7, s32[32]{0:T(128)S(1)} %copy-done.7, s16[8,192,128]{2,1,0:T(8,128)(2,1)S(1)} %all_to_all.21.near_phases, s16[8,192,128]{2,1,0:T(8,128)(2,1)S(1)} %collective-permute-done.far_phases, ...), custom_call_target="tpu_custom_call" | custom-call | tf_op jit(solution)/shard_map/frame_gradients/pallas_call | solution.py:267
  44.9 0.2 collective-permute-start.1
  45.1 1.6 %collective-permute-done.1 = bf16[8,192,128]{2,1,0:T(8,128)(2,1)S(1)} collective-permute-done((bf16[8,192,128]{2,1,0:T(8,128)(2,1)S(1)}, bf16[8,192,128]{2,1,0:T(8,128)(2,1)S(1)}, u32[]{:S(2)}, u32[]{:S(2)}) %collective-permute-start.1) | collective-permute-done | bytes 393248 | tf_op jit(solution)/shard_map/ppermute | solution.py:386
  46.7 0.1 add_convert_fusion
  46.8 0.0 copy-start.4
  46.9 0.0 copy-start.5
  46.9 11.5 %all_to_all.22 = bf16[8,192,128]{2,1,0:T(8,128)(2,1)S(1)} all-to-all(bf16[8,192,128]{2,1,0:T(8,128)(2,1)S(1)} %add_convert_fusion), channel_id=1, replica_groups={{0,16,32,48,64,80,96,112},{8,24,40,56,72,88,104,120},{1,17,33,49,65,81,..., dimensions={0} | all-to-all | bytes 786432 | tf_op jit(solution)/shard_map/all_to_all | solution.py:382
  58.4 0.1 convert_element_type.26
  58.5 0.1 broadcast_in_dim.7
  58.5 12.6 %all_to_all.23.tiles = bf16[8,192,128]{2,1,0:T(8,128)(2,1)S(1)} all-to-all(bf16[8,192,128]{2,1,0:T(8,128)(2,1)S(1)} %broadcast_in_dim.7), channel_id=1, replica_groups=mesh['slab'=16,'tile'=8] {'tile'}, dimensions={0} | all-to-all | bytes 786432 | tf_op jit(solution)/shard_map/all_to_all | solution.py:407
  71.2 0.0 copy-done.4
  71.2 0.0 copy-done.5
  71.2 6.2 %back_project.1 = f32[8,64,1024]{2,1,0:T(8,128)} custom-call(f32[16]{0:T(128)S(1)} %copy-done.4, s32[16]{0:T(128)S(1)} %bitcast.6, bf16[8,192,128]{2,1,0:T(8,128)(2,1)S(1)} %all_to_all.23.tiles), custom_call_target="tpu_custom_call" | custom-call | tf_op jit(solution)/shard_map/back_project/pallas_call | solution.py:347
  (2 shorter events, 0.1 us)
Async XLA Ops:
  0.0 38.6 %copy-start = (bf16[32,128,128]{2,1,0:T(8,128)(2,1)S(1)}, bf16[32,128,128]{2,1,0:T(8,128)(2,1)}, u32[]{:S(2)}) copy-start(bf16[32,128,128]{2,1,0:T(8,128)(2,1)} %measured.1) | copy-start | bytes 3145732
  0.0 38.6 %copy-start.1 = (f32[2,128,128]{2,1,0:T(8,128)S(1)}, f32[2,128,128]{2,1,0:T(8,128)}, u32[]{:S(2)}) copy-start(f32[2,128,128]{2,1,0:T(8,128)} %probe.1) | copy-start | bytes 393220
  0.0 38.6 %copy-start.2 = (bf16[256,256]{1,0:T(8,128)(2,1)S(1)}, bf16[256,256]{1,0:T(8,128)(2,1)}, u32[]{:S(2)}) copy-start(bf16[256,256]{1,0:T(8,128)(2,1)} %constant.31.clone.gather) | copy-start | bytes 393220
  0.0 38.6 %copy-start.3 = (bf16[256,256]{1,0:T(8,128)(2,1)S(1)}, bf16[256,256]{1,0:T(8,128)(2,1)}, u32[]{:S(2)}) copy-start(bf16[256,256]{1,0:T(8,128)(2,1)} %constant.30.clone.spread) | copy-start | bytes 393220
  0.0 38.6 %copy-start.6 = (s32[32,1]{0,1:T(1,128)S(1)}, s32[32,1]{0,1:T(1,128)}, u32[]{:S(2)}) copy-start(s32[32,1]{0,1:T(1,128)} %param.14) | copy-start | bytes 388
  0.0 38.6 %copy-start.7 = (s32[32]{0:T(128)S(1)}, s32[32]{0:T(128)}, u32[]{:S(2)}) copy-start(s32[32]{0:T(128)} %shifts_in.1) | copy-start | bytes 388
  36.9 1.7 %collective-permute-start = (s16[8,192,128]{2,1,0:T(8,128)(2,1)S(1)}, s16[8,192,128]{2,1,0:T(8,128)(2,1)S(1)}, u32[]{:S(2)}, u32[]{:S(2)}) collective-permute-start(s16[8,192,128]{2,1,0:T(8,128)(2,1)S(1)} %all_to_all.21.near_phases), channel_id=1, source_target_pairs={{0,8},{8,0},{16,24},{24,16},{32,40},{40,32},{48,56},{56,48},{64,72... | collective-permute-start | bytes 1179656 | tf_op jit(solution)/shard_map/ppermute | solution.py:386
  44.9 1.8 %collective-permute-start.1 = (bf16[8,192,128]{2,1,0:T(8,128)(2,1)S(1)}, bf16[8,192,128]{2,1,0:T(8,128)(2,1)S(1)}, u32[]{:S(2)}, u32[]{:S(2)}) collective-permute-start(bf16[8,192,128]{2,1,0:T(8,128)(2,1)S(1)} %get-tuple-element.8), channel_id=1, source_target_pairs={{0,8},{8,0},{16,24},{24,16},{32,40},{40,32},{48,56},{56,48},{64,72... | collective-permute-start | bytes 1179656 | tf_op jit(solution)/shard_map/ppermute | solution.py:386
  46.8 24.3 %copy-start.4 = (f32[16]{0:T(128)S(1)}, f32[16]{0:T(128)}, u32[]{:S(2)}) copy-start(f32[16]{0:T(128)} %shears_in.3) | copy-start | bytes 196
  46.9 24.3 %copy-start.5 = (s32[16,1]{0,1:T(1,128)S(1)}, s32[16,1]{0,1:T(1,128)}, u32[]{:S(2)}) copy-start(s32[16,1]{0,1:T(1,128)} %param.11) | copy-start | bytes 196

commit v5 on v4

--- a/solution.py
+++ b/solution.py
@@ -21,11 +21,11 @@
 FIRST = 38
 WIDE = 9 * BLOCK
 FWD_FINE, FWD_COARSE = 4, 14
-BWD_FINE, BWD_COARSE = 16, 4
+BWD_FINE, BWD_COARSE = 14, 4
 OWN_ROWS, EDGE_ROWS = ANGLES * SLICES_DEV, ANGLES // 2 * SLICES_DEV
 PAIRS = SLICES_DEV // 2
 ROWS = OWN_ROWS + EDGE_ROWS
-GROUP = 16
+GROUP = 32
 UNPACK_UNROLL = 2
 VMEM_LIMIT = 40 * 1024 * 1024
 ALL_VMEM = 60 * 1024 * 1024
@@ -92,6 +92,7 @@
     shape = (ANGLES, BLOCK)
     shift = pick_rows([shifts[i] for i in range(ANGLES)], shape, 0, ANGLES)
     lane = iota((8, BLOCK), 1)
+    full_lane = iota(shape, 1)
     outer = (lane < HALO) | (lane >= BLOCK - HALO)
     zero = jnp.zeros(shape, jnp.float32)
     for p in range(PAIRS):
@@ -99,20 +100,29 @@
         for half in range(2):
             rows = jnp.concatenate(
                 [volume[p * 2 + half], jnp.zeros((DEPTH, WIDE - BLOCKS * BLOCK), jnp.float32)], axis=1
-            )
+            ).astype(jnp.bfloat16)
             for r in range(FWD_FINE):
-                moved = rows if r == 0 else pltpu.roll(rows, r, 1)
-                stack[p, r * DEPTH : (r + 1) * DEPTH, half * WIDE : (half + 1) * WIDE] = moved.astype(jnp.bfloat16)
-        both = jnp.dot(table[...], stack[p], preferred_element_type=jnp.float32)
+                moved = rows if r == 0 else jnp.concatenate([rows[:, WIDE - r :], rows[:, : WIDE - r]], axis=1)
+                stack[p, r * DEPTH : (r + 1) * DEPTH, half * WIDE : (half + 1) * WIDE] = moved
+        fixed = []
+        for n in range(WIDE // BLOCK):
+            sums = jnp.dot(table[...], stack[p, :, n * 2 * BLOCK : (n + 1) * 2 * BLOCK], preferred_element_type=jnp.float32)
+            for b in range(2):
+                rolled = [
+                    pltpu.roll(sums[j * ANGLES : (j + 1) * ANGLES, b * BLOCK : (b + 1) * BLOCK], FIRST + FWD_FINE * j, 1)
+                    for j in range(FWD_COARSE)
+                ]
+                if (2 * n + b) % (BLOCKS + 1) == 0:
+                    before = [zero] * FWD_COARSE
+                total = jnp.where(full_lane >= FIRST, rolled[0], before[0])
+                for j in range(1, FWD_COARSE):
+                    total = total + jnp.where(full_lane >= FIRST + FWD_FINE * j, rolled[j], before[j])
+                before = rolled
+                turns = total * (1.0 / (2.0 * math.pi))
+                turns = turns - jnp.floor(turns + 0.5)
+                fixed.append(jnp.minimum(jnp.floor(turns * 65536.0 + 0.5), 32767.0))
         for half in range(2):
-            sums = both[:, half * WIDE : (half + 1) * WIDE]
-            total = pltpu.roll(sums[0:ANGLES], FIRST, 1)
-            for j in range(1, FWD_COARSE):
-                total = total + pltpu.roll(sums[j * ANGLES : (j + 1) * ANGLES], FIRST + FWD_FINE * j, 1)
-            turns = total * (1.0 / (2.0 * math.pi))
-            turns = turns - jnp.floor(turns + 0.5)
-            fixed = jnp.minimum(jnp.floor(turns * 65536.0 + 0.5), 32767.0)
-            block = [zero] + [fixed[:, k * BLOCK : (k + 1) * BLOCK] for k in range(BLOCKS + 1)] + [zero]
+            block = [zero] + fixed[half * (BLOCKS + 1) : (half + 1) * (BLOCKS + 1)] + [zero]
             placed = []
             for k in range(BLOCKS):
                 here = jnp.where(shift == 0, block[k + 1], jnp.where(shift > 0, block[k], block[k + 2]))
@@ -324,10 +334,10 @@
                     for k in range(BLOCKS + 1)
                 ],
                 axis=1,
-            )
+            ).astype(jnp.bfloat16)
             for r in range(BWD_FINE):
-                moved = left(placed, FIRST + r)
-                stack[p, r * ANGLES : (r + 1) * ANGLES, half * WIDE : (half + 1) * WIDE] = moved.astype(jnp.bfloat16)
+                moved = jnp.concatenate([placed[:, FIRST + r :], placed[:, : FIRST + r]], axis=1)
+                stack[p, r * ANGLES : (r + 1) * ANGLES, half * WIDE : (half + 1) * WIDE] = moved
         both = jnp.dot(table[...], stack[p], preferred_element_type=jnp.float32)
         for half in range(2):
             sums = both[:, half * WIDE : (half + 1) * WIDE]

time: 77.8 us -> 76.7 us (0.986)
  Pallas kernels: 18.9 us -> 17.7 us
where the time goes in v5:
time: 76.7 us; the launch traced here: 76.4 us
  blocking collectives  54.4 us (71%)
  Pallas kernels  17.7 us (23%)
  waiting for transfers between devices  3.31 us (4%)
    all_to_all x2, blocking collectives, between_chips(): lax.all_to_all(value, 'slab', 0, 0, tiled=True, axis_index_groups=groups)  23.9 us
    all_to_all x1, blocking collectives, body(): landed = lax.all_to_all(partials, 'tile', 0, 0, tiled=True)  17.9 us
    all_to_all x1, blocking collectives, body(): lax.all_to_all(copies_of(grad.astype(jnp.bfloat16), TILES), 'tile', 0, 0,...  12.6 us
    pallas_call x1, Pallas kernels, frame_gradients(): pl.pallas_call(frames_kernel, name='frame_gradients', in_specs=[smem, hbm...  6.04 us
    pallas_call x1, Pallas kernels, back_project(): pl.pallas_call(back_kernel, name='back_project', in_specs=[hbm, hbm, pl.B...  5.84 us
    pallas_call x1, Pallas kernels, project(): pl.pallas_call(project_kernel, name='project', in_specs=[hbm, hbm, hbm],...  5.83 us
    ppermute x2, waiting for transfers between devices, between_cores(): lax.ppermute(value, 'slab', [(i, i ^ 1) for i in range(lax.axis_size('sla...  3.31 us
  transfers between devices with their start and end apart: 2, of which 2 were waited for; matrix products, arithmetic and copies ran while one was open for 0% of the time, Pallas kernels for 0%

profile of v5, /device:TPU:0, one launch (start us, length us, event | category | flops | bytes accessed | tf_op | source)
XLA Modules:
  0.0 76.4 jit_solution(14713138741729891052)
XLA Ops:
  0.0 0.0 copy-start
  0.0 0.0 copy-start.1
  0.0 0.0 copy-start.2
  0.0 0.0 copy-start.3
  0.0 0.0 copy-start.6
  0.0 0.0 copy-start.7
  0.0 5.8 %project.1 = s16[8,192,128]{2,1,0:T(8,128)(2,1)} custom-call(f32[16]{0:T(128)} %shears_in.3, s32[16]{0:T(128)} %bitcast.5, f32[8,64,1024]{2,1,0:T(8,128)} %volume_in.1), custom_call_target="tpu_custom_call" | custom-call | tf_op jit(solution)/shard_map/project/pallas_call | solution.py:145
  5.9 17.9 %all_to_all.20 = s16[8,192,128]{2,1,0:T(8,128)(2,1)S(1)} all-to-all(s16[8,192,128]{2,1,0:T(8,128)(2,1)} %project.1), channel_id=1, replica_groups=mesh['slab'=16,'tile'=8] {'tile'}, dimensions={0} | all-to-all | bytes 786432 | tf_op jit(solution)/shard_map/all_to_all | solution.py:404
  23.8 0.1 convert_reduce_fusion
  23.9 0.1 broadcast_in_dim.6
  24.0 12.4 %all_to_all.21.near_phases = s16[8,192,128]{2,1,0:T(8,128)(2,1)S(1)} all-to-all(s16[8,192,128]{2,1,0:T(8,128)(2,1)S(1)} %broadcast_in_dim.6), channel_id=1, replica_groups={{0,16,32,48,64,80,96,112},{8,24,40,56,72,88,104,120},{1,17,33,49,65,81,..., dimensions={0} | all-to-all | bytes 786432 | tf_op jit(solution)/shard_map/all_to_all | solution.py:392
  36.3 0.0 collective-permute-start
  36.3 1.7 %collective-permute-done.far_phases = s16[8,192,128]{2,1,0:T(8,128)(2,1)S(1)} collective-permute-done((s16[8,192,128]{2,1,0:T(8,128)(2,1)S(1)}, s16[8,192,128]{2,1,0:T(8,128)(2,1)S(1)}, u32[]{:S(2)}, u32[]{:S(2)}) %collective-permute-start) | collective-permute-done | bytes 393248 | tf_op jit(solution)/shard_map/ppermute | solution.py:396
  38.0 0.0 copy-done
  38.0 0.0 copy-done.1
  38.0 0.0 copy-done.2
  38.0 0.0 copy-done.3
  38.1 0.0 copy-done.6
  38.1 0.0 copy-done.7
  38.1 6.0 %frame_gradients.1 = (bf16[8,192,128]{2,1,0:T(8,128)(2,1)S(1)}, bf16[8,192,128]{2,1,0:T(8,128)(2,1)S(1)}) custom-call(s32[1]{0:T(128)} %bitcast.1.parity, s32[32]{0:T(128)S(1)} %bitcast.7, s32[32]{0:T(128)S(1)} %copy-done.7, s16[8,192,128]{2,1,0:T(8,128)(2,1)S(1)} %all_to_all.21.near_phases, s16[8,192,128]{2,1,0:T(8,128)(2,1)S(1)} %collective-permute-done.far_phases, ...), custom_call_target="tpu_custom_call" | custom-call | tf_op jit(solution)/shard_map/frame_gradients/pallas_call | solution.py:277
  44.1 0.2 collective-permute-start.1
  44.3 1.6 %collective-permute-done.1 = bf16[8,192,128]{2,1,0:T(8,128)(2,1)S(1)} collective-permute-done((bf16[8,192,128]{2,1,0:T(8,128)(2,1)S(1)}, bf16[8,192,128]{2,1,0:T(8,128)(2,1)S(1)}, u32[]{:S(2)}, u32[]{:S(2)}) %collective-permute-start.1) | collective-permute-done | bytes 393248 | tf_op jit(solution)/shard_map/ppermute | solution.py:396
  45.9 0.1 add_convert_fusion
  46.0 0.0 copy-start.4
  46.1 0.0 copy-start.5
  46.1 11.5 %all_to_all.22 = bf16[8,192,128]{2,1,0:T(8,128)(2,1)S(1)} all-to-all(bf16[8,192,128]{2,1,0:T(8,128)(2,1)S(1)} %add_convert_fusion), channel_id=1, replica_groups={{0,16,32,48,64,80,96,112},{8,24,40,56,72,88,104,120},{1,17,33,49,65,81,..., dimensions={0} | all-to-all | bytes 786432 | tf_op jit(solution)/shard_map/all_to_all | solution.py:392
  57.6 0.1 convert_element_type.26
  57.7 0.1 broadcast_in_dim.7
  57.8 12.6 %all_to_all.23.tiles = bf16[8,192,128]{2,1,0:T(8,128)(2,1)S(1)} all-to-all(bf16[8,192,128]{2,1,0:T(8,128)(2,1)S(1)} %broadcast_in_dim.7), channel_id=1, replica_groups=mesh['slab'=16,'tile'=8] {'tile'}, dimensions={0} | all-to-all | bytes 786432 | tf_op jit(solution)/shard_map/all_to_all | solution.py:417
  70.4 0.0 copy-done.4
  70.4 0.0 copy-done.5
  70.4 5.8 %back_project.1 = f32[8,64,1024]{2,1,0:T(8,128)} custom-call(f32[16]{0:T(128)S(1)} %copy-done.4, s32[16]{0:T(128)S(1)} %bitcast.6, bf16[8,192,128]{2,1,0:T(8,128)(2,1)S(1)} %all_to_all.23.tiles), custom_call_target="tpu_custom_call" | custom-call | tf_op jit(solution)/shard_map/back_project/pallas_call | solution.py:357
  (2 shorter events, 0.1 us)
Async XLA Ops:
  0.0 38.0 %copy-start = (bf16[32,128,128]{2,1,0:T(8,128)(2,1)S(1)}, bf16[32,128,128]{2,1,0:T(8,128)(2,1)}, u32[]{:S(2)}) copy-start(bf16[32,128,128]{2,1,0:T(8,128)(2,1)} %measured.1) | copy-start | bytes 3145732
  0.0 38.0 %copy-start.1 = (f32[2,128,128]{2,1,0:T(8,128)S(1)}, f32[2,128,128]{2,1,0:T(8,128)}, u32[]{:S(2)}) copy-start(f32[2,128,128]{2,1,0:T(8,128)} %probe.1) | copy-start | bytes 393220
  0.0 38.0 %copy-start.2 = (bf16[256,256]{1,0:T(8,128)(2,1)S(1)}, bf16[256,256]{1,0:T(8,128)(2,1)}, u32[]{:S(2)}) copy-start(bf16[256,256]{1,0:T(8,128)(2,1)} %constant.31.clone.gather) | copy-start | bytes 393220
  0.0 38.0 %copy-start.3 = (bf16[256,256]{1,0:T(8,128)(2,1)S(1)}, bf16[256,256]{1,0:T(8,128)(2,1)}, u32[]{:S(2)}) copy-start(bf16[256,256]{1,0:T(8,128)(2,1)} %constant.30.clone.spread) | copy-start | bytes 393220
  0.0 38.1 %copy-start.6 = (s32[32,1]{0,1:T(1,128)S(1)}, s32[32,1]{0,1:T(1,128)}, u32[]{:S(2)}) copy-start(s32[32,1]{0,1:T(1,128)} %param.14) | copy-start | bytes 388
  0.0 38.1 %copy-start.7 = (s32[32]{0:T(128)S(1)}, s32[32]{0:T(128)}, u32[]{:S(2)}) copy-start(s32[32]{0:T(128)} %shifts_in.1) | copy-start | bytes 388
  36.3 1.7 %collective-permute-start = (s16[8,192,128]{2,1,0:T(8,128)(2,1)S(1)}, s16[8,192,128]{2,1,0:T(8,128)(2,1)S(1)}, u32[]{:S(2)}, u32[]{:S(2)}) collective-permute-start(s16[8,192,128]{2,1,0:T(8,128)(2,1)S(1)} %all_to_all.21.near_phases), channel_id=1, source_target_pairs={{0,8},{8,0},{16,24},{24,16},{32,40},{40,32},{48,56},{56,48},{64,72... | collective-permute-start | bytes 1179656 | tf_op jit(solution)/shard_map/ppermute | solution.py:396
  44.1 1.8 %collective-permute-start.1 = (bf16[8,192,128]{2,1,0:T(8,128)(2,1)S(1)}, bf16[8,192,128]{2,1,0:T(8,128)(2,1)S(1)}, u32[]{:S(2)}, u32[]{:S(2)}) collective-permute-start(bf16[8,192,128]{2,1,0:T(8,128)(2,1)S(1)} %get-tuple-element.8), channel_id=1, source_target_pairs={{0,8},{8,0},{16,24},{24,16},{32,40},{40,32},{48,56},{56,48},{64,72... | collective-permute-start | bytes 1179656 | tf_op jit(solution)/shard_map/ppermute | solution.py:396
  46.0 24.3 %copy-start.4 = (f32[16]{0:T(128)S(1)}, f32[16]{0:T(128)}, u32[]{:S(2)}) copy-start(f32[16]{0:T(128)} %shears_in.3) | copy-start | bytes 196
  46.1 24.3 %copy-start.5 = (s32[16,1]{0,1:T(1,128)S(1)}, s32[16,1]{0,1:T(1,128)}, u32[]{:S(2)}) copy-start(s32[16,1]{0,1:T(1,128)} %param.11) | copy-start | bytes 196

commit v6 on v5

--- a/solution.py
+++ b/solution.py
@@ -26,6 +26,7 @@
 PAIRS = SLICES_DEV // 2
 ROWS = OWN_ROWS + EDGE_ROWS
 GROUP = 32
+MERGED = 4
 UNPACK_UNROLL = 2
 VMEM_LIMIT = 40 * 1024 * 1024
 ALL_VMEM = 60 * 1024 * 1024
@@ -95,7 +96,7 @@
     full_lane = iota(shape, 1)
     outer = (lane < HALO) | (lane >= BLOCK - HALO)
     zero = jnp.zeros(shape, jnp.float32)
-    for p in range(PAIRS):
+    def build(p):
         copies[2 + p].wait()
         for half in range(2):
             rows = jnp.concatenate(
@@ -104,6 +105,8 @@
             for r in range(FWD_FINE):
                 moved = rows if r == 0 else jnp.concatenate([rows[:, WIDE - r :], rows[:, : WIDE - r]], axis=1)
                 stack[p, r * DEPTH : (r + 1) * DEPTH, half * WIDE : (half + 1) * WIDE] = moved
+
+    def finish(p):
         fixed = []
         for n in range(WIDE // BLOCK):
             sums = jnp.dot(table[...], stack[p, :, n * 2 * BLOCK : (n + 1) * 2 * BLOCK], preferred_element_type=jnp.float32)
@@ -136,6 +139,12 @@
                 high = jnp.where(lane < HALO, after[8:], before[8:])
                 edge = jnp.where(outer, low, pltpu.roll(high, BLOCK // 2, 1))
                 gathered[k, pl.ds(OWN_ROWS + s, ANGLES // 2, stride=SLICES_DEV), :] = edge
+
+    build(0)
+    for p in range(PAIRS):
+        if p + 1 < PAIRS:
+            build(p + 1)
+        finish(p)
     for k in range(BLOCKS):
         out[k] = gathered[k].astype(jnp.int32).astype(jnp.int16)
 
@@ -178,7 +187,7 @@
     def unpack(chip, carried):
         for which, phases in ((core, near_phases), (1 - core, far_phases)):
             base = pl.multiple_of((chip * 2 + which) * SLICES_DEV, SLICES_DEV)
-            rows = phases[chip].astype(jnp.int32).astype(jnp.float32)
+            rows = phases[chip].astype(jnp.int32).astype(jnp.float32) * (1.0 / 65536.0)
             zero = jnp.zeros((SLICES_DEV, BLOCK), jnp.float32)
             for i in range(ANGLES):
                 here = pl.ds(base + i * SIDE, SLICES_DEV)
@@ -201,6 +210,14 @@
         top = jnp.concatenate([value[:SIDE, :SIDE], value[SIDE:, :SIDE]], axis=1)
         bottom = jnp.concatenate([value[:SIDE, SIDE:], value[SIDE:, SIDE:]], axis=1)
         return jnp.concatenate([top, bottom], axis=0)
+
+    def across(values, matrix, per_pair):
+        results = []
+        for first in range(0, len(values), MERGED * per_pair):
+            rows = jnp.concatenate(values[first : first + MERGED * per_pair], axis=0)
+            product = jnp.dot(rows, matrix[...], preferred_element_type=jnp.float32)
+            results += [product[g * 2 * SIDE : (g + 1) * 2 * SIDE] for g in range(MERGED)]
+        return results
 
     def group(step, carried):
         first = step * GROUP
@@ -213,20 +230,15 @@
             amount.append(bound)
         for k in range(GROUP):
             chosen = jnp.where(inside[k], tiled(own[rows[k], :]), tiled(edge[rows[k], :])).reshape(SIDE, BLOCK)
-            turns = pltpu.roll(chosen, lax.rem(BLOCK - amount[k], BLOCK), 1) * (1.0 / 65536.0)
+            turns = pltpu.roll(chosen, lax.rem(BLOCK - amount[k], BLOCK), 1)
             object_im, object_re = sine_and_cosine(turns)
             wave_re = probe[0] * object_re - probe[1] * object_im
             wave_im = probe[0] * object_im + probe[1] * object_re
             waves.append((wave_re, wave_im))
             fields.append(jnp.concatenate([wave_re.astype(jnp.bfloat16), wave_im.astype(jnp.bfloat16)], axis=1))
         pairs = range(GROUP // 2)
-        half = [
-            jnp.dot(
-                jnp.concatenate(fields[2 * g : 2 * g + 2], axis=0), spread[...], preferred_element_type=jnp.float32
-            ).astype(jnp.bfloat16)
-            for g in pairs
-        ]
-        far = [jnp.dot(gather[...], turned(half[g]), preferred_element_type=jnp.float32) for g in pairs]
+        half = across(fields, spread, 2)
+        far = [jnp.dot(gather[...], turned(half[g].astype(jnp.bfloat16)), preferred_element_type=jnp.float32) for g in pairs]
         resid = []
         for g in pairs:
             far_re, far_im = far[g][:SIDE], far[g][SIDE:]
@@ -238,9 +250,9 @@
                 jnp.concatenate([(far_re * factor).astype(jnp.bfloat16), (far_im * factor).astype(jnp.bfloat16)], axis=0)
             )
         back = [
-            jnp.dot(spread[...], resid[g], preferred_element_type=jnp.float32).astype(jnp.bfloat16) for g in pairs
+            jnp.dot(spread[...], resid[g], preferred_element_type=jnp.float32) for g in pairs
         ]
-        near = [jnp.dot(turned(back[g]), gather[...], preferred_element_type=jnp.float32) for g in pairs]
+        near = across([turned(back[g].astype(jnp.bfloat16)) for g in pairs], gather, 1)
         grads = []
         for k in range(GROUP):
             part = near[k // 2][(k % 2) * SIDE : (k % 2 + 1) * SIDE]
@@ -311,7 +323,7 @@
     sends = []
     for k in range(TILES):
         gathered[k] = tiles[k].astype(jnp.float32)
-    for p in range(PAIRS):
+    def build(p):
         for half in range(2):
             own, margin = [], []
             for k in range(TILES):
@@ -338,6 +350,8 @@
             for r in range(BWD_FINE):
                 moved = jnp.concatenate([placed[:, FIRST + r :], placed[:, : FIRST + r]], axis=1)
                 stack[p, r * ANGLES : (r + 1) * ANGLES, half * WIDE : (half + 1) * WIDE] = moved
+
+    def finish(p):
         both = jnp.dot(table[...], stack[p], preferred_element_type=jnp.float32)
         for half in range(2):
             sums = both[:, half * WIDE : (half + 1) * WIDE]
@@ -348,6 +362,11 @@
         part = pl.ds(p * 2, 2)
         sends.append(pltpu.make_async_copy(out.at[part], out_hbm.at[part], sems.at[2 + p]))
         sends[-1].start()
+
+    for p in range(PAIRS):
+        build(p)
+    for p in range(PAIRS):
+        finish(p)
     for send in sends:
         send.wait()
 

time: 76.7 us -> 75.6 us (0.986)
  Pallas kernels: 17.7 us -> 16.6 us
where the time goes in v6:
time: 75.6 us; the launch traced here: 75.3 us
  blocking collectives  54.4 us (72%)
  Pallas kernels  16.6 us (22%)
  waiting for transfers between devices  3.31 us (4%)
    all_to_all x2, blocking collectives, between_chips(): lax.all_to_all(value, 'slab', 0, 0, tiled=True, axis_index_groups=groups)  23.9 us
    all_to_all x1, blocking collectives, body(): landed = lax.all_to_all(partials, 'tile', 0, 0, tiled=True)  17.9 us
    all_to_all x1, blocking collectives, body(): lax.all_to_all(copies_of(grad.astype(jnp.bfloat16), TILES), 'tile', 0, 0,...  12.6 us
    pallas_call x1, Pallas kernels, frame_gradients(): pl.pallas_call(frames_kernel, name='frame_gradients', in_specs=[smem, hbm...  5.77 us
    pallas_call x1, Pallas kernels, project(): pl.pallas_call(project_kernel, name='project', in_specs=[hbm, hbm, hbm],...  5.51 us
    pallas_call x1, Pallas kernels, back_project(): pl.pallas_call(back_kernel, name='back_project', in_specs=[hbm, hbm, pl.B...  5.32 us
    ppermute x2, waiting for transfers between devices, between_cores(): lax.ppermute(value, 'slab', [(i, i ^ 1) for i in range(lax.axis_size('sla...  3.31 us
  transfers between devices with their start and end apart: 2, of which 2 were waited for; matrix products, arithmetic and copies ran while one was open for 0% of the time, Pallas kernels for 0%

profile of v6, /device:TPU:0, one launch (start us, length us, event | category | flops | bytes accessed | tf_op | source)
XLA Modules:
  0.0 75.3 jit_solution(13054598150724082732)
XLA Ops:
  0.0 0.0 copy-start
  0.0 0.0 copy-start.1
  0.0 0.0 copy-start.2
  0.0 0.0 copy-start.3
  0.0 0.0 copy-start.6
  0.0 0.0 copy-start.7
  0.0 5.5 %project.1 = s16[8,192,128]{2,1,0:T(8,128)(2,1)} custom-call(f32[16]{0:T(128)} %shears_in.3, s32[16]{0:T(128)} %bitcast.5, f32[8,64,1024]{2,1,0:T(8,128)} %volume_in.1), custom_call_target="tpu_custom_call" | custom-call | tf_op jit(solution)/shard_map/project/pallas_call | solution.py:154
  5.5 17.9 %all_to_all.20 = s16[8,192,128]{2,1,0:T(8,128)(2,1)S(1)} all-to-all(s16[8,192,128]{2,1,0:T(8,128)(2,1)} %project.1), channel_id=1, replica_groups=mesh['slab'=16,'tile'=8] {'tile'}, dimensions={0} | all-to-all | bytes 786432 | tf_op jit(solution)/shard_map/all_to_all | solution.py:423
  23.4 0.1 convert_reduce_fusion
  23.6 0.1 broadcast_in_dim.6
  23.6 12.4 %all_to_all.21.near_phases = s16[8,192,128]{2,1,0:T(8,128)(2,1)S(1)} all-to-all(s16[8,192,128]{2,1,0:T(8,128)(2,1)S(1)} %broadcast_in_dim.6), channel_id=1, replica_groups={{0,16,32,48,64,80,96,112},{8,24,40,56,72,88,104,120},{1,17,33,49,65,81,..., dimensions={0} | all-to-all | bytes 786432 | tf_op jit(solution)/shard_map/all_to_all | solution.py:411
  36.0 0.0 collective-permute-start
  36.0 1.7 %collective-permute-done.far_phases = s16[8,192,128]{2,1,0:T(8,128)(2,1)S(1)} collective-permute-done((s16[8,192,128]{2,1,0:T(8,128)(2,1)S(1)}, s16[8,192,128]{2,1,0:T(8,128)(2,1)S(1)}, u32[]{:S(2)}, u32[]{:S(2)}) %collective-permute-start) | collective-permute-done | bytes 393248 | tf_op jit(solution)/shard_map/ppermute | solution.py:415
  37.7 0.0 copy-done
  37.7 0.0 copy-done.1
  37.7 0.0 copy-done.2
  37.7 0.0 copy-done.3
  37.7 0.0 copy-done.6
  37.8 0.0 copy-done.7
  37.8 5.8 %frame_gradients.1 = (bf16[8,192,128]{2,1,0:T(8,128)(2,1)S(1)}, bf16[8,192,128]{2,1,0:T(8,128)(2,1)S(1)}) custom-call(s32[1]{0:T(128)} %bitcast.1.parity, s32[32]{0:T(128)S(1)} %bitcast.7, s32[32]{0:T(128)S(1)} %copy-done.7, s16[8,192,128]{2,1,0:T(8,128)(2,1)S(1)} %all_to_all.21.near_phases, s16[8,192,128]{2,1,0:T(8,128)(2,1)S(1)} %collective-permute-done.far_phases, ...), custom_call_target="tpu_custom_call" | custom-call | tf_op jit(solution)/shard_map/frame_gradients/pallas_call | solution.py:289
  43.5 0.2 collective-permute-start.1
  43.8 1.6 %collective-permute-done.1 = bf16[8,192,128]{2,1,0:T(8,128)(2,1)S(1)} collective-permute-done((bf16[8,192,128]{2,1,0:T(8,128)(2,1)S(1)}, bf16[8,192,128]{2,1,0:T(8,128)(2,1)S(1)}, u32[]{:S(2)}, u32[]{:S(2)}) %collective-permute-start.1) | collective-permute-done | bytes 393248 | tf_op jit(solution)/shard_map/ppermute | solution.py:415
  45.3 0.1 add_convert_fusion
  45.5 0.0 copy-start.4
  45.5 0.0 copy-start.5
  45.5 11.5 %all_to_all.22 = bf16[8,192,128]{2,1,0:T(8,128)(2,1)S(1)} all-to-all(bf16[8,192,128]{2,1,0:T(8,128)(2,1)S(1)} %add_convert_fusion), channel_id=1, replica_groups={{0,16,32,48,64,80,96,112},{8,24,40,56,72,88,104,120},{1,17,33,49,65,81,..., dimensions={0} | all-to-all | bytes 786432 | tf_op jit(solution)/shard_map/all_to_all | solution.py:411
  57.0 0.1 convert_element_type.26
  57.1 0.1 broadcast_in_dim.7
  57.2 12.6 %all_to_all.23.tiles = bf16[8,192,128]{2,1,0:T(8,128)(2,1)S(1)} all-to-all(bf16[8,192,128]{2,1,0:T(8,128)(2,1)S(1)} %broadcast_in_dim.7), channel_id=1, replica_groups=mesh['slab'=16,'tile'=8] {'tile'}, dimensions={0} | all-to-all | bytes 786432 | tf_op jit(solution)/shard_map/all_to_all | solution.py:436
  69.8 0.0 copy-done.4
  69.8 0.0 copy-done.5
  69.8 5.3 %back_project.1 = f32[8,64,1024]{2,1,0:T(8,128)} custom-call(f32[16]{0:T(128)S(1)} %copy-done.4, s32[16]{0:T(128)S(1)} %bitcast.6, bf16[8,192,128]{2,1,0:T(8,128)(2,1)S(1)} %all_to_all.23.tiles), custom_call_target="tpu_custom_call" | custom-call | tf_op jit(solution)/shard_map/back_project/pallas_call | solution.py:376
  (2 shorter events, 0.1 us)
Async XLA Ops:
  0.0 37.7 %copy-start = (bf16[32,128,128]{2,1,0:T(8,128)(2,1)S(1)}, bf16[32,128,128]{2,1,0:T(8,128)(2,1)}, u32[]{:S(2)}) copy-start(bf16[32,128,128]{2,1,0:T(8,128)(2,1)} %measured.1) | copy-start | bytes 3145732
  0.0 37.7 %copy-start.1 = (f32[2,128,128]{2,1,0:T(8,128)S(1)}, f32[2,128,128]{2,1,0:T(8,128)}, u32[]{:S(2)}) copy-start(f32[2,128,128]{2,1,0:T(8,128)} %probe.1) | copy-start | bytes 393220
  0.0 37.7 %copy-start.2 = (bf16[256,256]{1,0:T(8,128)(2,1)S(1)}, bf16[256,256]{1,0:T(8,128)(2,1)}, u32[]{:S(2)}) copy-start(bf16[256,256]{1,0:T(8,128)(2,1)} %constant.31.clone.gather) | copy-start | bytes 393220
  0.0 37.7 %copy-start.3 = (bf16[256,256]{1,0:T(8,128)(2,1)S(1)}, bf16[256,256]{1,0:T(8,128)(2,1)}, u32[]{:S(2)}) copy-start(bf16[256,256]{1,0:T(8,128)(2,1)} %constant.30.clone.spread) | copy-start | bytes 393220
  0.0 37.7 %copy-start.6 = (s32[32,1]{0,1:T(1,128)S(1)}, s32[32,1]{0,1:T(1,128)}, u32[]{:S(2)}) copy-start(s32[32,1]{0,1:T(1,128)} %param.14) | copy-start | bytes 388
  0.0 37.7 %copy-start.7 = (s32[32]{0:T(128)S(1)}, s32[32]{0:T(128)}, u32[]{:S(2)}) copy-start(s32[32]{0:T(128)} %shifts_in.1) | copy-start | bytes 388
  36.0 1.7 %collective-permute-start = (s16[8,192,128]{2,1,0:T(8,128)(2,1)S(1)}, s16[8,192,128]{2,1,0:T(8,128)(2,1)S(1)}, u32[]{:S(2)}, u32[]{:S(2)}) collective-permute-start(s16[8,192,128]{2,1,0:T(8,128)(2,1)S(1)} %all_to_all.21.near_phases), channel_id=1, source_target_pairs={{0,8},{8,0},{16,24},{24,16},{32,40},{40,32},{48,56},{56,48},{64,72... | collective-permute-start | bytes 1179656 | tf_op jit(solution)/shard_map/ppermute | solution.py:415
  43.5 1.8 %collective-permute-start.1 = (bf16[8,192,128]{2,1,0:T(8,128)(2,1)S(1)}, bf16[8,192,128]{2,1,0:T(8,128)(2,1)S(1)}, u32[]{:S(2)}, u32[]{:S(2)}) collective-permute-start(bf16[8,192,128]{2,1,0:T(8,128)(2,1)S(1)} %get-tuple-element.8), channel_id=1, source_target_pairs={{0,8},{8,0},{16,24},{24,16},{32,40},{40,32},{48,56},{56,48},{64,72... | collective-permute-start | bytes 1179656 | tf_op jit(solution)/shard_map/ppermute | solution.py:415
  45.5 24.3 %copy-start.4 = (f32[16]{0:T(128)S(1)}, f32[16]{0:T(128)}, u32[]{:S(2)}) copy-start(f32[16]{0:T(128)} %shears_in.3) | copy-start | bytes 196
  45.5 24.3 %copy-start.5 = (s32[16,1]{0,1:T(1,128)S(1)}, s32[16,1]{0,1:T(1,128)}, u32[]{:S(2)}) copy-start(s32[16,1]{0,1:T(1,128)} %param.11) | copy-start | bytes 196

commit v7 on v6

--- a/solution.py
+++ b/solution.py
@@ -245,7 +245,7 @@
             amplitude = jnp.concatenate(
                 [measured[first + 2 * g].astype(jnp.float32), measured[first + 2 * g + 1].astype(jnp.float32)], axis=1
             )
-            factor = 1.0 - amplitude * lax.rsqrt(far_re * far_re + far_im * far_im + 0.25)
+            factor = amplitude * lax.rsqrt(far_re * far_re + far_im * far_im + 0.25)
             resid.append(
                 jnp.concatenate([(far_re * factor).astype(jnp.bfloat16), (far_im * factor).astype(jnp.bfloat16)], axis=0)
             )
@@ -257,7 +257,7 @@
         for k in range(GROUP):
             part = near[k // 2][(k % 2) * SIDE : (k % 2 + 1) * SIDE]
             wave_re, wave_im = waves[k]
-            grads.append(pltpu.roll(part[:, SIDE:] * wave_re - part[:, :SIDE] * wave_im, amount[k], 1))
+            grads.append(pltpu.roll(part[:, :SIDE] * wave_im - part[:, SIDE:] * wave_re, amount[k], 1))
         for k in range(GROUP):
             grad = tiled(grads[k])
             own_sum[rows[k], :] = own_sum[rows[k], :] + jnp.where(inside[k], grad, 0.0).reshape(SIDE, BLOCK)

time: 75.6 us -> 75.5 us (level)
  no operation moved by 1% of the time
where the time goes in v7:
time: 75.5 us; the launch traced here: 75.2 us
  blocking collectives  54.4 us (72%)
  Pallas kernels  16.5 us (22%)
  waiting for transfers between devices  3.31 us (4%)
    all_to_all x2, blocking collectives, between_chips(): lax.all_to_all(value, 'slab', 0, 0, tiled=True, axis_index_groups=groups)  23.9 us
    all_to_all x1, blocking collectives, body(): landed = lax.all_to_all(partials, 'tile', 0, 0, tiled=True)  17.9 us
    all_to_all x1, blocking collectives, body(): lax.all_to_all(copies_of(grad.astype(jnp.bfloat16), TILES), 'tile', 0, 0,...  12.6 us
    pallas_call x1, Pallas kernels, frame_gradients(): pl.pallas_call(frames_kernel, name='frame_gradients', in_specs=[smem, hbm...  5.67 us
    pallas_call x1, Pallas kernels, project(): pl.pallas_call(project_kernel, name='project', in_specs=[hbm, hbm, hbm],...  5.51 us
    pallas_call x1, Pallas kernels, back_project(): pl.pallas_call(back_kernel, name='back_project', in_specs=[hbm, hbm, pl.B...  5.33 us
    ppermute x2, waiting for transfers between devices, between_cores(): lax.ppermute(value, 'slab', [(i, i ^ 1) for i in range(lax.axis_size('sla...  3.31 us
  transfers between devices with their start and end apart: 2, of which 2 were waited for; matrix products, arithmetic and copies ran while one was open for 0% of the time, Pallas kernels for 0%

profile of v7, /device:TPU:0, one launch (start us, length us, event | category | flops | bytes accessed | tf_op | source)
XLA Modules:
  0.0 75.2 jit_solution(9515526014750616660)
XLA Ops:
  0.0 0.0 copy-start
  0.0 0.0 copy-start.1
  0.0 0.0 copy-start.2
  0.0 0.0 copy-start.3
  0.0 0.0 copy-start.6
  0.0 0.0 copy-start.7
  0.0 5.5 %project.1 = s16[8,192,128]{2,1,0:T(8,128)(2,1)} custom-call(f32[16]{0:T(128)} %shears_in.3, s32[16]{0:T(128)} %bitcast.5, f32[8,64,1024]{2,1,0:T(8,128)} %volume_in.1), custom_call_target="tpu_custom_call" | custom-call | tf_op jit(solution)/shard_map/project/pallas_call | solution.py:154
  5.5 17.9 %all_to_all.20 = s16[8,192,128]{2,1,0:T(8,128)(2,1)S(1)} all-to-all(s16[8,192,128]{2,1,0:T(8,128)(2,1)} %project.1), channel_id=1, replica_groups=mesh['slab'=16,'tile'=8] {'tile'}, dimensions={0} | all-to-all | bytes 786432 | tf_op jit(solution)/shard_map/all_to_all | solution.py:423
  23.4 0.1 convert_reduce_fusion
  23.6 0.1 broadcast_in_dim.6
  23.6 12.4 %all_to_all.21.near_phases = s16[8,192,128]{2,1,0:T(8,128)(2,1)S(1)} all-to-all(s16[8,192,128]{2,1,0:T(8,128)(2,1)S(1)} %broadcast_in_dim.6), channel_id=1, replica_groups={{0,16,32,48,64,80,96,112},{8,24,40,56,72,88,104,120},{1,17,33,49,65,81,..., dimensions={0} | all-to-all | bytes 786432 | tf_op jit(solution)/shard_map/all_to_all | solution.py:411
  36.0 0.0 collective-permute-start
  36.0 1.7 %collective-permute-done.far_phases = s16[8,192,128]{2,1,0:T(8,128)(2,1)S(1)} collective-permute-done((s16[8,192,128]{2,1,0:T(8,128)(2,1)S(1)}, s16[8,192,128]{2,1,0:T(8,128)(2,1)S(1)}, u32[]{:S(2)}, u32[]{:S(2)}) %collective-permute-start) | collective-permute-done | bytes 393248 | tf_op jit(solution)/shard_map/ppermute | solution.py:415
  37.7 0.0 copy-done
  37.7 0.0 copy-done.1
  37.7 0.0 copy-done.2
  37.7 0.0 copy-done.3
  37.7 0.0 copy-done.6
  37.8 0.0 copy-done.7
  37.8 5.7 %frame_gradients.1 = (bf16[8,192,128]{2,1,0:T(8,128)(2,1)S(1)}, bf16[8,192,128]{2,1,0:T(8,128)(2,1)S(1)}) custom-call(s32[1]{0:T(128)} %bitcast.1.parity, s32[32]{0:T(128)S(1)} %bitcast.7, s32[32]{0:T(128)S(1)} %copy-done.7, s16[8,192,128]{2,1,0:T(8,128)(2,1)S(1)} %all_to_all.21.near_phases, s16[8,192,128]{2,1,0:T(8,128)(2,1)S(1)} %collective-permute-done.far_phases, ...), custom_call_target="tpu_custom_call" | custom-call | tf_op jit(solution)/shard_map/frame_gradients/pallas_call | solution.py:289
  43.4 0.2 collective-permute-start.1
  43.7 1.6 %collective-permute-done.1 = bf16[8,192,128]{2,1,0:T(8,128)(2,1)S(1)} collective-permute-done((bf16[8,192,128]{2,1,0:T(8,128)(2,1)S(1)}, bf16[8,192,128]{2,1,0:T(8,128)(2,1)S(1)}, u32[]{:S(2)}, u32[]{:S(2)}) %collective-permute-start.1) | collective-permute-done | bytes 393248 | tf_op jit(solution)/shard_map/ppermute | solution.py:415
  45.2 0.1 add_convert_fusion
  45.4 0.0 copy-start.4
  45.4 0.0 copy-start.5
  45.4 11.5 %all_to_all.22 = bf16[8,192,128]{2,1,0:T(8,128)(2,1)S(1)} all-to-all(bf16[8,192,128]{2,1,0:T(8,128)(2,1)S(1)} %add_convert_fusion), channel_id=1, replica_groups={{0,16,32,48,64,80,96,112},{8,24,40,56,72,88,104,120},{1,17,33,49,65,81,..., dimensions={0} | all-to-all | bytes 786432 | tf_op jit(solution)/shard_map/all_to_all | solution.py:411
  56.9 0.1 convert_element_type.26
  57.0 0.1 broadcast_in_dim.7
  57.1 12.6 %all_to_all.23.tiles = bf16[8,192,128]{2,1,0:T(8,128)(2,1)S(1)} all-to-all(bf16[8,192,128]{2,1,0:T(8,128)(2,1)S(1)} %broadcast_in_dim.7), channel_id=1, replica_groups=mesh['slab'=16,'tile'=8] {'tile'}, dimensions={0} | all-to-all | bytes 786432 | tf_op jit(solution)/shard_map/all_to_all | solution.py:436
  69.7 0.0 copy-done.4
  69.7 0.0 copy-done.5
  69.7 5.3 %back_project.1 = f32[8,64,1024]{2,1,0:T(8,128)} custom-call(f32[16]{0:T(128)S(1)} %copy-done.4, s32[16]{0:T(128)S(1)} %bitcast.6, bf16[8,192,128]{2,1,0:T(8,128)(2,1)S(1)} %all_to_all.23.tiles), custom_call_target="tpu_custom_call" | custom-call | tf_op jit(solution)/shard_map/back_project/pallas_call | solution.py:376
  (2 shorter events, 0.1 us)
Async XLA Ops:
  0.0 37.7 %copy-start = (bf16[32,128,128]{2,1,0:T(8,128)(2,1)S(1)}, bf16[32,128,128]{2,1,0:T(8,128)(2,1)}, u32[]{:S(2)}) copy-start(bf16[32,128,128]{2,1,0:T(8,128)(2,1)} %measured.1) | copy-start | bytes 3145732
  0.0 37.7 %copy-start.1 = (f32[2,128,128]{2,1,0:T(8,128)S(1)}, f32[2,128,128]{2,1,0:T(8,128)}, u32[]{:S(2)}) copy-start(f32[2,128,128]{2,1,0:T(8,128)} %probe.1) | copy-start | bytes 393220
  0.0 37.7 %copy-start.2 = (bf16[256,256]{1,0:T(8,128)(2,1)S(1)}, bf16[256,256]{1,0:T(8,128)(2,1)}, u32[]{:S(2)}) copy-start(bf16[256,256]{1,0:T(8,128)(2,1)} %constant.31.clone.gather) | copy-start | bytes 393220
  0.0 37.7 %copy-start.3 = (bf16[256,256]{1,0:T(8,128)(2,1)S(1)}, bf16[256,256]{1,0:T(8,128)(2,1)}, u32[]{:S(2)}) copy-start(bf16[256,256]{1,0:T(8,128)(2,1)} %constant.30.clone.spread) | copy-start | bytes 393220
  0.0 37.7 %copy-start.6 = (s32[32,1]{0,1:T(1,128)S(1)}, s32[32,1]{0,1:T(1,128)}, u32[]{:S(2)}) copy-start(s32[32,1]{0,1:T(1,128)} %param.14) | copy-start | bytes 388
  0.0 37.7 %copy-start.7 = (s32[32]{0:T(128)S(1)}, s32[32]{0:T(128)}, u32[]{:S(2)}) copy-start(s32[32]{0:T(128)} %shifts_in.1) | copy-start | bytes 388
  36.0 1.7 %collective-permute-start = (s16[8,192,128]{2,1,0:T(8,128)(2,1)S(1)}, s16[8,192,128]{2,1,0:T(8,128)(2,1)S(1)}, u32[]{:S(2)}, u32[]{:S(2)}) collective-permute-start(s16[8,192,128]{2,1,0:T(8,128)(2,1)S(1)} %all_to_all.21.near_phases), channel_id=1, source_target_pairs={{0,8},{8,0},{16,24},{24,16},{32,40},{40,32},{48,56},{56,48},{64,72... | collective-permute-start | bytes 1179656 | tf_op jit(solution)/shard_map/ppermute | solution.py:415
  43.4 1.8 %collective-permute-start.1 = (bf16[8,192,128]{2,1,0:T(8,128)(2,1)S(1)}, bf16[8,192,128]{2,1,0:T(8,128)(2,1)S(1)}, u32[]{:S(2)}, u32[]{:S(2)}) collective-permute-start(bf16[8,192,128]{2,1,0:T(8,128)(2,1)S(1)} %get-tuple-element.8), channel_id=1, source_target_pairs={{0,8},{8,0},{16,24},{24,16},{32,40},{40,32},{48,56},{56,48},{64,72... | collective-permute-start | bytes 1179656 | tf_op jit(solution)/shard_map/ppermute | solution.py:415
  45.4 24.3 %copy-start.4 = (f32[16]{0:T(128)S(1)}, f32[16]{0:T(128)}, u32[]{:S(2)}) copy-start(f32[16]{0:T(128)} %shears_in.3) | copy-start | bytes 196
  45.4 24.3 %copy-start.5 = (s32[16,1]{0,1:T(1,128)S(1)}, s32[16,1]{0,1:T(1,128)}, u32[]{:S(2)}) copy-start(s32[16,1]{0,1:T(1,128)} %param.11) | copy-start | bytes 196

commit v8 on v6

--- a/solution.py
+++ b/solution.py
@@ -245,7 +245,8 @@
             amplitude = jnp.concatenate(
                 [measured[first + 2 * g].astype(jnp.float32), measured[first + 2 * g + 1].astype(jnp.float32)], axis=1
             )
-            factor = 1.0 - amplitude * lax.rsqrt(far_re * far_re + far_im * far_im + 0.25)
+            ratio = amplitude * lax.rsqrt(far_re * far_re + far_im * far_im + 0.25)
+            factor = 0.5 * jnp.mean(ratio, axis=(0, 1), keepdims=True) - ratio
             resid.append(
                 jnp.concatenate([(far_re * factor).astype(jnp.bfloat16), (far_im * factor).astype(jnp.bfloat16)], axis=0)
             )

time: 75.6 us -> 76 us (level)
  no operation moved by 1% of the time
where the time goes in v8:
time: 76 us; the launch traced here: 75.7 us
  blocking collectives  54.4 us (72%)
  Pallas kernels  17 us (22%)
  waiting for transfers between devices  3.31 us (4%)
    all_to_all x2, blocking collectives, between_chips(): lax.all_to_all(value, 'slab', 0, 0, tiled=True, axis_index_groups=groups)  23.9 us
    all_to_all x1, blocking collectives, body(): landed = lax.all_to_all(partials, 'tile', 0, 0, tiled=True)  17.9 us
    all_to_all x1, blocking collectives, body(): lax.all_to_all(copies_of(grad.astype(jnp.bfloat16), TILES), 'tile', 0, 0,...  12.6 us
    pallas_call x1, Pallas kernels, frame_gradients(): pl.pallas_call(frames_kernel, name='frame_gradients', in_specs=[smem, hbm...  6.16 us
    pallas_call x1, Pallas kernels, project(): pl.pallas_call(project_kernel, name='project', in_specs=[hbm, hbm, hbm],...  5.51 us
    pallas_call x1, Pallas kernels, back_project(): pl.pallas_call(back_kernel, name='back_project', in_specs=[hbm, hbm, pl.B...  5.33 us
    ppermute x2, waiting for transfers between devices, between_cores(): lax.ppermute(value, 'slab', [(i, i ^ 1) for i in range(lax.axis_size('sla...  3.31 us
  transfers between devices with their start and end apart: 2, of which 2 were waited for; matrix products, arithmetic and copies ran while one was open for 0% of the time, Pallas kernels for 0%

profile of v8, /device:TPU:0, one launch (start us, length us, event | category | flops | bytes accessed | tf_op | source)
XLA Modules:
  0.0 75.7 jit_solution(8221175163218950596)
XLA Ops:
  0.0 0.0 copy-start
  0.0 0.0 copy-start.1
  0.0 0.0 copy-start.2
  0.0 0.0 copy-start.3
  0.0 0.0 copy-start.6
  0.0 0.0 copy-start.7
  0.0 5.5 %project.1 = s16[8,192,128]{2,1,0:T(8,128)(2,1)} custom-call(f32[16]{0:T(128)} %shears_in.3, s32[16]{0:T(128)} %bitcast.5, f32[8,64,1024]{2,1,0:T(8,128)} %volume_in.1), custom_call_target="tpu_custom_call" | custom-call | tf_op jit(solution)/shard_map/project/pallas_call | solution.py:154
  5.5 17.9 %all_to_all.20 = s16[8,192,128]{2,1,0:T(8,128)(2,1)S(1)} all-to-all(s16[8,192,128]{2,1,0:T(8,128)(2,1)} %project.1), channel_id=1, replica_groups=mesh['slab'=16,'tile'=8] {'tile'}, dimensions={0} | all-to-all | bytes 786432 | tf_op jit(solution)/shard_map/all_to_all | solution.py:424
  23.4 0.1 convert_reduce_fusion
  23.6 0.1 broadcast_in_dim.6
  23.6 12.4 %all_to_all.21.near_phases = s16[8,192,128]{2,1,0:T(8,128)(2,1)S(1)} all-to-all(s16[8,192,128]{2,1,0:T(8,128)(2,1)S(1)} %broadcast_in_dim.6), channel_id=1, replica_groups={{0,16,32,48,64,80,96,112},{8,24,40,56,72,88,104,120},{1,17,33,49,65,81,..., dimensions={0} | all-to-all | bytes 786432 | tf_op jit(solution)/shard_map/all_to_all | solution.py:412
  36.0 0.0 collective-permute-start
  36.0 1.7 %collective-permute-done.far_phases = s16[8,192,128]{2,1,0:T(8,128)(2,1)S(1)} collective-permute-done((s16[8,192,128]{2,1,0:T(8,128)(2,1)S(1)}, s16[8,192,128]{2,1,0:T(8,128)(2,1)S(1)}, u32[]{:S(2)}, u32[]{:S(2)}) %collective-permute-start) | collective-permute-done | bytes 393248 | tf_op jit(solution)/shard_map/ppermute | solution.py:416
  37.7 0.0 copy-done
  37.7 0.0 copy-done.1
  37.7 0.0 copy-done.2
  37.7 0.0 copy-done.3
  37.7 0.0 copy-done.6
  37.8 0.0 copy-done.7
  37.8 6.2 %frame_gradients.1 = (bf16[8,192,128]{2,1,0:T(8,128)(2,1)S(1)}, bf16[8,192,128]{2,1,0:T(8,128)(2,1)S(1)}) custom-call(s32[1]{0:T(128)} %bitcast.1.parity, s32[32]{0:T(128)S(1)} %bitcast.7, s32[32]{0:T(128)S(1)} %copy-done.7, s16[8,192,128]{2,1,0:T(8,128)(2,1)S(1)} %all_to_all.21.near_phases, s16[8,192,128]{2,1,0:T(8,128)(2,1)S(1)} %collective-permute-done.far_phases, ...), custom_call_target="tpu_custom_call" | custom-call | tf_op jit(solution)/shard_map/frame_gradients/pallas_call | solution.py:290
  43.9 0.2 collective-permute-start.1
  44.1 1.6 %collective-permute-done.1 = bf16[8,192,128]{2,1,0:T(8,128)(2,1)S(1)} collective-permute-done((bf16[8,192,128]{2,1,0:T(8,128)(2,1)S(1)}, bf16[8,192,128]{2,1,0:T(8,128)(2,1)S(1)}, u32[]{:S(2)}, u32[]{:S(2)}) %collective-permute-start.1) | collective-permute-done | bytes 393248 | tf_op jit(solution)/shard_map/ppermute | solution.py:416
  45.7 0.1 add_convert_fusion
  45.8 0.0 copy-start.4
  45.9 0.0 copy-start.5
  45.9 11.5 %all_to_all.22 = bf16[8,192,128]{2,1,0:T(8,128)(2,1)S(1)} all-to-all(bf16[8,192,128]{2,1,0:T(8,128)(2,1)S(1)} %add_convert_fusion), channel_id=1, replica_groups={{0,16,32,48,64,80,96,112},{8,24,40,56,72,88,104,120},{1,17,33,49,65,81,..., dimensions={0} | all-to-all | bytes 786432 | tf_op jit(solution)/shard_map/all_to_all | solution.py:412
  57.4 0.1 convert_element_type.26
  57.5 0.1 broadcast_in_dim.7
  57.5 12.6 %all_to_all.23.tiles = bf16[8,192,128]{2,1,0:T(8,128)(2,1)S(1)} all-to-all(bf16[8,192,128]{2,1,0:T(8,128)(2,1)S(1)} %broadcast_in_dim.7), channel_id=1, replica_groups=mesh['slab'=16,'tile'=8] {'tile'}, dimensions={0} | all-to-all | bytes 786432 | tf_op jit(solution)/shard_map/all_to_all | solution.py:437
  70.2 0.0 copy-done.4
  70.2 0.0 copy-done.5
  70.2 5.3 %back_project.1 = f32[8,64,1024]{2,1,0:T(8,128)} custom-call(f32[16]{0:T(128)S(1)} %copy-done.4, s32[16]{0:T(128)S(1)} %bitcast.6, bf16[8,192,128]{2,1,0:T(8,128)(2,1)S(1)} %all_to_all.23.tiles), custom_call_target="tpu_custom_call" | custom-call | tf_op jit(solution)/shard_map/back_project/pallas_call | solution.py:377
  (2 shorter events, 0.1 us)
Async XLA Ops:
  0.0 37.7 %copy-start = (bf16[32,128,128]{2,1,0:T(8,128)(2,1)S(1)}, bf16[32,128,128]{2,1,0:T(8,128)(2,1)}, u32[]{:S(2)}) copy-start(bf16[32,128,128]{2,1,0:T(8,128)(2,1)} %measured.1) | copy-start | bytes 3145732
  0.0 37.7 %copy-start.1 = (f32[2,128,128]{2,1,0:T(8,128)S(1)}, f32[2,128,128]{2,1,0:T(8,128)}, u32[]{:S(2)}) copy-start(f32[2,128,128]{2,1,0:T(8,128)} %probe.1) | copy-start | bytes 393220
  0.0 37.7 %copy-start.2 = (bf16[256,256]{1,0:T(8,128)(2,1)S(1)}, bf16[256,256]{1,0:T(8,128)(2,1)}, u32[]{:S(2)}) copy-start(bf16[256,256]{1,0:T(8,128)(2,1)} %constant.31.clone.gather) | copy-start | bytes 393220
  0.0 37.7 %copy-start.3 = (bf16[256,256]{1,0:T(8,128)(2,1)S(1)}, bf16[256,256]{1,0:T(8,128)(2,1)}, u32[]{:S(2)}) copy-start(bf16[256,256]{1,0:T(8,128)(2,1)} %constant.30.clone.spread) | copy-start | bytes 393220
  0.0 37.7 %copy-start.6 = (s32[32,1]{0,1:T(1,128)S(1)}, s32[32,1]{0,1:T(1,128)}, u32[]{:S(2)}) copy-start(s32[32,1]{0,1:T(1,128)} %param.14) | copy-start | bytes 388
  0.0 37.7 %copy-start.7 = (s32[32]{0:T(128)S(1)}, s32[32]{0:T(128)}, u32[]{:S(2)}) copy-start(s32[32]{0:T(128)} %shifts_in.1) | copy-start | bytes 388
  36.0 1.7 %collective-permute-start = (s16[8,192,128]{2,1,0:T(8,128)(2,1)S(1)}, s16[8,192,128]{2,1,0:T(8,128)(2,1)S(1)}, u32[]{:S(2)}, u32[]{:S(2)}) collective-permute-start(s16[8,192,128]{2,1,0:T(8,128)(2,1)S(1)} %all_to_all.21.near_phases), channel_id=1, source_target_pairs={{0,8},{8,0},{16,24},{24,16},{32,40},{40,32},{48,56},{56,48},{64,72... | collective-permute-start | bytes 1179656 | tf_op jit(solution)/shard_map/ppermute | solution.py:416
  43.9 1.8 %collective-permute-start.1 = (bf16[8,192,128]{2,1,0:T(8,128)(2,1)S(1)}, bf16[8,192,128]{2,1,0:T(8,128)(2,1)S(1)}, u32[]{:S(2)}, u32[]{:S(2)}) collective-permute-start(bf16[8,192,128]{2,1,0:T(8,128)(2,1)S(1)} %get-tuple-element.8), channel_id=1, source_target_pairs={{0,8},{8,0},{16,24},{24,16},{32,40},{40,32},{48,56},{56,48},{64,72... | collective-permute-start | bytes 1179656 | tf_op jit(solution)/shard_map/ppermute | solution.py:416
  45.8 24.3 %copy-start.4 = (f32[16]{0:T(128)S(1)}, f32[16]{0:T(128)}, u32[]{:S(2)}) copy-start(f32[16]{0:T(128)} %shears_in.3) | copy-start | bytes 196
  45.9 24.3 %copy-start.5 = (s32[16,1]{0,1:T(1,128)S(1)}, s32[16,1]{0,1:T(1,128)}, u32[]{:S(2)}) copy-start(s32[16,1]{0,1:T(1,128)} %param.11) | copy-start | bytes 196

commit v9 on v8

--- a/solution.py
+++ b/solution.py
@@ -203,6 +203,13 @@
     for copy in copies:
         copy.wait()
 
+    power = probe[0] * probe[0] + probe[1] * probe[1]
+    sample = measured[0, 0:16].astype(jnp.float32)
+    for k in range(4, FRAMES, 4):
+        sample = sample + measured[k, k * 4 % SIDE : k * 4 % SIDE + 16].astype(jnp.float32)
+    share = lax.rsqrt(jnp.mean(power, axis=(0, 1), keepdims=True) + 0.25)
+    share = share * jnp.mean(sample, axis=(0, 1), keepdims=True) * (0.75 / (FRAMES // 4))
+
     def tiled(value):
         return value.reshape(SIDE // 8, 8, BLOCK)
 
@@ -246,7 +253,7 @@
                 [measured[first + 2 * g].astype(jnp.float32), measured[first + 2 * g + 1].astype(jnp.float32)], axis=1
             )
             ratio = amplitude * lax.rsqrt(far_re * far_re + far_im * far_im + 0.25)
-            factor = 0.5 * jnp.mean(ratio, axis=(0, 1), keepdims=True) - ratio
+            factor = share - ratio
             resid.append(
                 jnp.concatenate([(far_re * factor).astype(jnp.bfloat16), (far_im * factor).astype(jnp.bfloat16)], axis=0)
             )

time: 76 us -> 75.6 us (level)
  no operation moved by 1% of the time
where the time goes in v9:
time: 75.6 us; the launch traced here: 75.3 us
  blocking collectives  54.4 us (72%)
  Pallas kernels  16.6 us (22%)
  waiting for transfers between devices  3.31 us (4%)
    all_to_all x2, blocking collectives, between_chips(): lax.all_to_all(value, 'slab', 0, 0, tiled=True, axis_index_groups=groups)  23.9 us
    all_to_all x1, blocking collectives, body(): landed = lax.all_to_all(partials, 'tile', 0, 0, tiled=True)  17.9 us
    all_to_all x1, blocking collectives, body(): lax.all_to_all(copies_of(grad.astype(jnp.bfloat16), TILES), 'tile', 0, 0,...  12.6 us
    pallas_call x1, Pallas kernels, frame_gradients(): pl.pallas_call(frames_kernel, name='frame_gradients', in_specs=[smem, hbm...  5.76 us
    pallas_call x1, Pallas kernels, project(): pl.pallas_call(project_kernel, name='project', in_specs=[hbm, hbm, hbm],...  5.51 us
    pallas_call x1, Pallas kernels, back_project(): pl.pallas_call(back_kernel, name='back_project', in_specs=[hbm, hbm, pl.B...  5.32 us
    ppermute x2, waiting for transfers between devices, between_cores(): lax.ppermute(value, 'slab', [(i, i ^ 1) for i in range(lax.axis_size('sla...  3.31 us
  transfers between devices with their start and end apart: 2, of which 2 were waited for; matrix products, arithmetic and copies ran while one was open for 0% of the time, Pallas kernels for 0%

profile of v9, /device:TPU:0, one launch (start us, length us, event | category | flops | bytes accessed | tf_op | source)
XLA Modules:
  0.0 75.3 jit_solution(10052281571984059000)
XLA Ops:
  0.0 0.0 copy-start
  0.0 0.0 copy-start.1
  0.0 0.0 copy-start.2
  0.0 0.0 copy-start.3
  0.0 0.0 copy-start.6
  0.0 0.0 copy-start.7
  0.0 5.5 %project.1 = s16[8,192,128]{2,1,0:T(8,128)(2,1)} custom-call(f32[16]{0:T(128)} %shears_in.3, s32[16]{0:T(128)} %bitcast.5, f32[8,64,1024]{2,1,0:T(8,128)} %volume_in.1), custom_call_target="tpu_custom_call" | custom-call | tf_op jit(solution)/shard_map/project/pallas_call | solution.py:154
  5.5 17.9 %all_to_all.20 = s16[8,192,128]{2,1,0:T(8,128)(2,1)S(1)} all-to-all(s16[8,192,128]{2,1,0:T(8,128)(2,1)} %project.1), channel_id=1, replica_groups=mesh['slab'=16,'tile'=8] {'tile'}, dimensions={0} | all-to-all | bytes 786432 | tf_op jit(solution)/shard_map/all_to_all | solution.py:431
  23.4 0.1 convert_reduce_fusion
  23.6 0.1 broadcast_in_dim.6
  23.6 12.4 %all_to_all.21.near_phases = s16[8,192,128]{2,1,0:T(8,128)(2,1)S(1)} all-to-all(s16[8,192,128]{2,1,0:T(8,128)(2,1)S(1)} %broadcast_in_dim.6), channel_id=1, replica_groups={{0,16,32,48,64,80,96,112},{8,24,40,56,72,88,104,120},{1,17,33,49,65,81,..., dimensions={0} | all-to-all | bytes 786432 | tf_op jit(solution)/shard_map/all_to_all | solution.py:419
  36.0 0.0 collective-permute-start
  36.0 1.7 %collective-permute-done.far_phases = s16[8,192,128]{2,1,0:T(8,128)(2,1)S(1)} collective-permute-done((s16[8,192,128]{2,1,0:T(8,128)(2,1)S(1)}, s16[8,192,128]{2,1,0:T(8,128)(2,1)S(1)}, u32[]{:S(2)}, u32[]{:S(2)}) %collective-permute-start) | collective-permute-done | bytes 393248 | tf_op jit(solution)/shard_map/ppermute | solution.py:423
  37.7 0.0 copy-done
  37.7 0.0 copy-done.1
  37.7 0.0 copy-done.2
  37.7 0.0 copy-done.3
  37.7 0.0 copy-done.6
  37.8 0.0 copy-done.7
  37.8 5.8 %frame_gradients.1 = (bf16[8,192,128]{2,1,0:T(8,128)(2,1)S(1)}, bf16[8,192,128]{2,1,0:T(8,128)(2,1)S(1)}) custom-call(s32[1]{0:T(128)} %bitcast.1.parity, s32[32]{0:T(128)S(1)} %bitcast.7, s32[32]{0:T(128)S(1)} %copy-done.7, s16[8,192,128]{2,1,0:T(8,128)(2,1)S(1)} %all_to_all.21.near_phases, s16[8,192,128]{2,1,0:T(8,128)(2,1)S(1)} %collective-permute-done.far_phases, ...), custom_call_target="tpu_custom_call" | custom-call | tf_op jit(solution)/shard_map/frame_gradients/pallas_call | solution.py:297
  43.5 0.2 collective-permute-start.1
  43.7 1.6 %collective-permute-done.1 = bf16[8,192,128]{2,1,0:T(8,128)(2,1)S(1)} collective-permute-done((bf16[8,192,128]{2,1,0:T(8,128)(2,1)S(1)}, bf16[8,192,128]{2,1,0:T(8,128)(2,1)S(1)}, u32[]{:S(2)}, u32[]{:S(2)}) %collective-permute-start.1) | collective-permute-done | bytes 393248 | tf_op jit(solution)/shard_map/ppermute | solution.py:423
  45.3 0.1 add_convert_fusion
  45.4 0.0 copy-start.4
  45.5 0.0 copy-start.5
  45.5 11.5 %all_to_all.22 = bf16[8,192,128]{2,1,0:T(8,128)(2,1)S(1)} all-to-all(bf16[8,192,128]{2,1,0:T(8,128)(2,1)S(1)} %add_convert_fusion), channel_id=1, replica_groups={{0,16,32,48,64,80,96,112},{8,24,40,56,72,88,104,120},{1,17,33,49,65,81,..., dimensions={0} | all-to-all | bytes 786432 | tf_op jit(solution)/shard_map/all_to_all | solution.py:419
  57.0 0.1 convert_element_type.26
  57.1 0.1 broadcast_in_dim.7
  57.2 12.6 %all_to_all.23.tiles = bf16[8,192,128]{2,1,0:T(8,128)(2,1)S(1)} all-to-all(bf16[8,192,128]{2,1,0:T(8,128)(2,1)S(1)} %broadcast_in_dim.7), channel_id=1, replica_groups=mesh['slab'=16,'tile'=8] {'tile'}, dimensions={0} | all-to-all | bytes 786432 | tf_op jit(solution)/shard_map/all_to_all | solution.py:444
  69.8 0.0 copy-done.4
  69.8 0.0 copy-done.5
  69.8 5.3 %back_project.1 = f32[8,64,1024]{2,1,0:T(8,128)} custom-call(f32[16]{0:T(128)S(1)} %copy-done.4, s32[16]{0:T(128)S(1)} %bitcast.6, bf16[8,192,128]{2,1,0:T(8,128)(2,1)S(1)} %all_to_all.23.tiles), custom_call_target="tpu_custom_call" | custom-call | tf_op jit(solution)/shard_map/back_project/pallas_call | solution.py:384
  (2 shorter events, 0.1 us)
Async XLA Ops:
  0.0 37.7 %copy-start = (bf16[32,128,128]{2,1,0:T(8,128)(2,1)S(1)}, bf16[32,128,128]{2,1,0:T(8,128)(2,1)}, u32[]{:S(2)}) copy-start(bf16[32,128,128]{2,1,0:T(8,128)(2,1)} %measured.1) | copy-start | bytes 3145732
  0.0 37.7 %copy-start.1 = (f32[2,128,128]{2,1,0:T(8,128)S(1)}, f32[2,128,128]{2,1,0:T(8,128)}, u32[]{:S(2)}) copy-start(f32[2,128,128]{2,1,0:T(8,128)} %probe.1) | copy-start | bytes 393220
  0.0 37.7 %copy-start.2 = (bf16[256,256]{1,0:T(8,128)(2,1)S(1)}, bf16[256,256]{1,0:T(8,128)(2,1)}, u32[]{:S(2)}) copy-start(bf16[256,256]{1,0:T(8,128)(2,1)} %constant.31.clone.gather) | copy-start | bytes 393220
  0.0 37.7 %copy-start.3 = (bf16[256,256]{1,0:T(8,128)(2,1)S(1)}, bf16[256,256]{1,0:T(8,128)(2,1)}, u32[]{:S(2)}) copy-start(bf16[256,256]{1,0:T(8,128)(2,1)} %constant.30.clone.spread) | copy-start | bytes 393220
  0.0 37.7 %copy-start.6 = (s32[32,1]{0,1:T(1,128)S(1)}, s32[32,1]{0,1:T(1,128)}, u32[]{:S(2)}) copy-start(s32[32,1]{0,1:T(1,128)} %param.14) | copy-start | bytes 388
  0.0 37.7 %copy-start.7 = (s32[32]{0:T(128)S(1)}, s32[32]{0:T(128)}, u32[]{:S(2)}) copy-start(s32[32]{0:T(128)} %shifts_in.1) | copy-start | bytes 388
  36.0 1.7 %collective-permute-start = (s16[8,192,128]{2,1,0:T(8,128)(2,1)S(1)}, s16[8,192,128]{2,1,0:T(8,128)(2,1)S(1)}, u32[]{:S(2)}, u32[]{:S(2)}) collective-permute-start(s16[8,192,128]{2,1,0:T(8,128)(2,1)S(1)} %all_to_all.21.near_phases), channel_id=1, source_target_pairs={{0,8},{8,0},{16,24},{24,16},{32,40},{40,32},{48,56},{56,48},{64,72... | collective-permute-start | bytes 1179656 | tf_op jit(solution)/shard_map/ppermute | solution.py:423
  43.5 1.8 %collective-permute-start.1 = (bf16[8,192,128]{2,1,0:T(8,128)(2,1)S(1)}, bf16[8,192,128]{2,1,0:T(8,128)(2,1)S(1)}, u32[]{:S(2)}, u32[]{:S(2)}) collective-permute-start(bf16[8,192,128]{2,1,0:T(8,128)(2,1)S(1)} %get-tuple-element.8), channel_id=1, source_target_pairs={{0,8},{8,0},{16,24},{24,16},{32,40},{40,32},{48,56},{56,48},{64,72... | collective-permute-start | bytes 1179656 | tf_op jit(solution)/shard_map/ppermute | solution.py:423
  45.4 24.3 %copy-start.4 = (f32[16]{0:T(128)S(1)}, f32[16]{0:T(128)}, u32[]{:S(2)}) copy-start(f32[16]{0:T(128)} %shears_in.3) | copy-start | bytes 196
  45.5 24.3 %copy-start.5 = (s32[16,1]{0,1:T(1,128)S(1)}, s32[16,1]{0,1:T(1,128)}, u32[]{:S(2)}) copy-start(s32[16,1]{0,1:T(1,128)} %param.11) | copy-start | bytes 196

commit v10 on v9

--- a/solution.py
+++ b/solution.py
@@ -146,7 +146,7 @@
             build(p + 1)
         finish(p)
     for k in range(BLOCKS):
-        out[k] = gathered[k].astype(jnp.int32).astype(jnp.int16)
+        out[k] = gathered[k, :ROWS].astype(jnp.int32).astype(jnp.int16)
 
 
 def project(shears, shifts, volume):
@@ -161,7 +161,7 @@
             pltpu.VMEM((FWD_COARSE * ANGLES, FWD_FINE * DEPTH), jnp.bfloat16),
             pltpu.VMEM((PAIRS, FWD_FINE * DEPTH, 2 * WIDE), jnp.bfloat16),
             pltpu.VMEM((SLICES_DEV, DEPTH, BLOCKS * BLOCK), jnp.float32),
-            pltpu.VMEM((BLOCKS, ROWS, BLOCK), jnp.float32),
+            pltpu.VMEM((BLOCKS, ROWS + SLICES_DEV, BLOCK), jnp.float32),
             pltpu.SMEM((ANGLES,), jnp.float32),
             pltpu.SMEM((ANGLES,), jnp.int32),
             pltpu.SemaphoreType.DMA((2 + PAIRS,)),
@@ -330,7 +330,7 @@
     zero = jnp.zeros(shape, jnp.float32)
     sends = []
     for k in range(TILES):
-        gathered[k] = tiles[k].astype(jnp.float32)
+        gathered[k, :ROWS] = tiles[k].astype(jnp.float32)
     def build(p):
         for half in range(2):
             own, margin = [], []
@@ -391,7 +391,7 @@
             pltpu.VMEM((BWD_COARSE * DEPTH, BWD_FINE * ANGLES), jnp.bfloat16),
             pltpu.VMEM((PAIRS, BWD_FINE * ANGLES, 2 * WIDE), jnp.bfloat16),
             pltpu.VMEM((SLICES_DEV, DEPTH, BLOCKS * BLOCK), jnp.float32),
-            pltpu.VMEM((TILES, ROWS, BLOCK), jnp.float32),
+            pltpu.VMEM((TILES, ROWS + SLICES_DEV, BLOCK), jnp.float32),
             pltpu.SMEM((ANGLES,), jnp.float32),
             pltpu.SMEM((ANGLES,), jnp.int32),
             pltpu.SemaphoreType.DMA((2 + PAIRS,)),

time: 75.6 us -> 75.6 us (level)
  no operation moved by 1% of the time
where the time goes in v10:
time: 75.6 us; the launch traced here: 75.3 us
  blocking collectives  54.4 us (72%)
  Pallas kernels  16.6 us (22%)
  waiting for transfers between devices  3.31 us (4%)
    all_to_all x2, blocking collectives, between_chips(): lax.all_to_all(value, 'slab', 0, 0, tiled=True, axis_index_groups=groups)  23.9 us
    all_to_all x1, blocking collectives, body(): landed = lax.all_to_all(partials, 'tile', 0, 0, tiled=True)  17.9 us
    all_to_all x1, blocking collectives, body(): lax.all_to_all(copies_of(grad.astype(jnp.bfloat16), TILES), 'tile', 0, 0,...  12.6 us
    pallas_call x1, Pallas kernels, frame_gradients(): pl.pallas_call(frames_kernel, name='frame_gradients', in_specs=[smem, hbm...  5.76 us
    pallas_call x1, Pallas kernels, project(): pl.pallas_call(project_kernel, name='project', in_specs=[hbm, hbm, hbm],...  5.52 us
    pallas_call x1, Pallas kernels, back_project(): pl.pallas_call(back_kernel, name='back_project', in_specs=[hbm, hbm, pl.B...  5.32 us
    ppermute x2, waiting for transfers between devices, between_cores(): lax.ppermute(value, 'slab', [(i, i ^ 1) for i in range(lax.axis_size('sla...  3.31 us
  transfers between devices with their start and end apart: 2, of which 2 were waited for; matrix products, arithmetic and copies ran while one was open for 0% of the time, Pallas kernels for 0%

profile of v10, /device:TPU:0, one launch (start us, length us, event | category | flops | bytes accessed | tf_op | source)
XLA Modules:
  0.0 75.3 jit_solution(9853666039189380094)
XLA Ops:
  0.0 0.0 copy-start
  0.0 0.0 copy-start.1
  0.0 0.0 copy-start.2
  0.0 0.0 copy-start.3
  0.0 0.0 copy-start.6
  0.0 0.0 copy-start.7
  0.0 5.5 %project.1 = s16[8,192,128]{2,1,0:T(8,128)(2,1)} custom-call(f32[16]{0:T(128)} %shears_in.3, s32[16]{0:T(128)} %bitcast.5, f32[8,64,1024]{2,1,0:T(8,128)} %volume_in.1), custom_call_target="tpu_custom_call" | custom-call | tf_op jit(solution)/shard_map/project/pallas_call | solution.py:154
  5.5 17.9 %all_to_all.20 = s16[8,192,128]{2,1,0:T(8,128)(2,1)S(1)} all-to-all(s16[8,192,128]{2,1,0:T(8,128)(2,1)} %project.1), channel_id=1, replica_groups=mesh['slab'=16,'tile'=8] {'tile'}, dimensions={0} | all-to-all | bytes 786432 | tf_op jit(solution)/shard_map/all_to_all | solution.py:431
  23.4 0.1 convert_reduce_fusion
  23.6 0.1 broadcast_in_dim.6
  23.6 12.4 %all_to_all.21.near_phases = s16[8,192,128]{2,1,0:T(8,128)(2,1)S(1)} all-to-all(s16[8,192,128]{2,1,0:T(8,128)(2,1)S(1)} %broadcast_in_dim.6), channel_id=1, replica_groups={{0,16,32,48,64,80,96,112},{8,24,40,56,72,88,104,120},{1,17,33,49,65,81,..., dimensions={0} | all-to-all | bytes 786432 | tf_op jit(solution)/shard_map/all_to_all | solution.py:419
  36.0 0.0 collective-permute-start
  36.0 1.7 %collective-permute-done.far_phases = s16[8,192,128]{2,1,0:T(8,128)(2,1)S(1)} collective-permute-done((s16[8,192,128]{2,1,0:T(8,128)(2,1)S(1)}, s16[8,192,128]{2,1,0:T(8,128)(2,1)S(1)}, u32[]{:S(2)}, u32[]{:S(2)}) %collective-permute-start) | collective-permute-done | bytes 393248 | tf_op jit(solution)/shard_map/ppermute | solution.py:423
  37.7 0.0 copy-done
  37.7 0.0 copy-done.1
  37.7 0.0 copy-done.2
  37.7 0.0 copy-done.3
  37.7 0.0 copy-done.6
  37.8 0.0 copy-done.7
  37.8 5.8 %frame_gradients.1 = (bf16[8,192,128]{2,1,0:T(8,128)(2,1)S(1)}, bf16[8,192,128]{2,1,0:T(8,128)(2,1)S(1)}) custom-call(s32[1]{0:T(128)} %bitcast.1.parity, s32[32]{0:T(128)S(1)} %bitcast.7, s32[32]{0:T(128)S(1)} %copy-done.7, s16[8,192,128]{2,1,0:T(8,128)(2,1)S(1)} %all_to_all.21.near_phases, s16[8,192,128]{2,1,0:T(8,128)(2,1)S(1)} %collective-permute-done.far_phases, ...), custom_call_target="tpu_custom_call" | custom-call | tf_op jit(solution)/shard_map/frame_gradients/pallas_call | solution.py:297
  43.5 0.2 collective-permute-start.1
  43.7 1.6 %collective-permute-done.1 = bf16[8,192,128]{2,1,0:T(8,128)(2,1)S(1)} collective-permute-done((bf16[8,192,128]{2,1,0:T(8,128)(2,1)S(1)}, bf16[8,192,128]{2,1,0:T(8,128)(2,1)S(1)}, u32[]{:S(2)}, u32[]{:S(2)}) %collective-permute-start.1) | collective-permute-done | bytes 393248 | tf_op jit(solution)/shard_map/ppermute | solution.py:423
  45.3 0.1 add_convert_fusion
  45.5 0.0 copy-start.4
  45.5 0.0 copy-start.5
  45.5 11.5 %all_to_all.22 = bf16[8,192,128]{2,1,0:T(8,128)(2,1)S(1)} all-to-all(bf16[8,192,128]{2,1,0:T(8,128)(2,1)S(1)} %add_convert_fusion), channel_id=1, replica_groups={{0,16,32,48,64,80,96,112},{8,24,40,56,72,88,104,120},{1,17,33,49,65,81,..., dimensions={0} | all-to-all | bytes 786432 | tf_op jit(solution)/shard_map/all_to_all | solution.py:419
  57.0 0.1 convert_element_type.26
  57.1 0.1 broadcast_in_dim.7
  57.2 12.6 %all_to_all.23.tiles = bf16[8,192,128]{2,1,0:T(8,128)(2,1)S(1)} all-to-all(bf16[8,192,128]{2,1,0:T(8,128)(2,1)S(1)} %broadcast_in_dim.7), channel_id=1, replica_groups=mesh['slab'=16,'tile'=8] {'tile'}, dimensions={0} | all-to-all | bytes 786432 | tf_op jit(solution)/shard_map/all_to_all | solution.py:444
  69.8 0.0 copy-done.4
  69.8 0.0 copy-done.5
  69.8 5.3 %back_project.1 = f32[8,64,1024]{2,1,0:T(8,128)} custom-call(f32[16]{0:T(128)S(1)} %copy-done.4, s32[16]{0:T(128)S(1)} %bitcast.6, bf16[8,192,128]{2,1,0:T(8,128)(2,1)S(1)} %all_to_all.23.tiles), custom_call_target="tpu_custom_call" | custom-call | tf_op jit(solution)/shard_map/back_project/pallas_call | solution.py:384
  (2 shorter events, 0.1 us)
Async XLA Ops:
  0.0 37.7 %copy-start = (bf16[32,128,128]{2,1,0:T(8,128)(2,1)S(1)}, bf16[32,128,128]{2,1,0:T(8,128)(2,1)}, u32[]{:S(2)}) copy-start(bf16[32,128,128]{2,1,0:T(8,128)(2,1)} %measured.1) | copy-start | bytes 3145732
  0.0 37.7 %copy-start.1 = (f32[2,128,128]{2,1,0:T(8,128)S(1)}, f32[2,128,128]{2,1,0:T(8,128)}, u32[]{:S(2)}) copy-start(f32[2,128,128]{2,1,0:T(8,128)} %probe.1) | copy-start | bytes 393220
  0.0 37.7 %copy-start.2 = (bf16[256,256]{1,0:T(8,128)(2,1)S(1)}, bf16[256,256]{1,0:T(8,128)(2,1)}, u32[]{:S(2)}) copy-start(bf16[256,256]{1,0:T(8,128)(2,1)} %constant.31.clone.gather) | copy-start | bytes 393220
  0.0 37.7 %copy-start.3 = (bf16[256,256]{1,0:T(8,128)(2,1)S(1)}, bf16[256,256]{1,0:T(8,128)(2,1)}, u32[]{:S(2)}) copy-start(bf16[256,256]{1,0:T(8,128)(2,1)} %constant.30.clone.spread) | copy-start | bytes 393220
  0.0 37.7 %copy-start.6 = (s32[32,1]{0,1:T(1,128)S(1)}, s32[32,1]{0,1:T(1,128)}, u32[]{:S(2)}) copy-start(s32[32,1]{0,1:T(1,128)} %param.14) | copy-start | bytes 388
  0.0 37.7 %copy-start.7 = (s32[32]{0:T(128)S(1)}, s32[32]{0:T(128)}, u32[]{:S(2)}) copy-start(s32[32]{0:T(128)} %shifts_in.1) | copy-start | bytes 388
  36.0 1.7 %collective-permute-start = (s16[8,192,128]{2,1,0:T(8,128)(2,1)S(1)}, s16[8,192,128]{2,1,0:T(8,128)(2,1)S(1)}, u32[]{:S(2)}, u32[]{:S(2)}) collective-permute-start(s16[8,192,128]{2,1,0:T(8,128)(2,1)S(1)} %all_to_all.21.near_phases), channel_id=1, source_target_pairs={{0,8},{8,0},{16,24},{24,16},{32,40},{40,32},{48,56},{56,48},{64,72... | collective-permute-start | bytes 1179656 | tf_op jit(solution)/shard_map/ppermute | solution.py:423
  43.5 1.8 %collective-permute-start.1 = (bf16[8,192,128]{2,1,0:T(8,128)(2,1)S(1)}, bf16[8,192,128]{2,1,0:T(8,128)(2,1)S(1)}, u32[]{:S(2)}, u32[]{:S(2)}) collective-permute-start(bf16[8,192,128]{2,1,0:T(8,128)(2,1)S(1)} %get-tuple-element.8), channel_id=1, source_target_pairs={{0,8},{8,0},{16,24},{24,16},{32,40},{40,32},{48,56},{56,48},{64,72... | collective-permute-start | bytes 1179656 | tf_op jit(solution)/shard_map/ppermute | solution.py:423
  45.5 24.3 %copy-start.4 = (f32[16]{0:T(128)S(1)}, f32[16]{0:T(128)}, u32[]{:S(2)}) copy-start(f32[16]{0:T(128)} %shears_in.3) | copy-start | bytes 196
  45.5 24.3 %copy-start.5 = (s32[16,1]{0,1:T(1,128)S(1)}, s32[16,1]{0,1:T(1,128)}, u32[]{:S(2)}) copy-start(s32[16,1]{0,1:T(1,128)} %param.11) | copy-start | bytes 196

commit v11 on v10

--- a/solution.py
+++ b/solution.py
@@ -328,24 +328,25 @@
     shift = pick_rows([shifts[i] for i in range(ANGLES)], shape, 0, ANGLES)
     lane = iota(shape, 1)
     zero = jnp.zeros(shape, jnp.float32)
+    outer = (lane < HALO) | (lane >= BLOCK - HALO)
+    from_left = iota((ANGLES // 2, BLOCK), 1) % (BLOCK // 2) < HALO
+    empty = jnp.zeros((ANGLES // 2, BLOCK), jnp.float32)
     sends = []
     for k in range(TILES):
         gathered[k, :ROWS] = tiles[k].astype(jnp.float32)
     def build(p):
         for half in range(2):
-            own, margin = [], []
+            own, margin = [], [empty]
             for k in range(TILES):
                 s = p * 2 + half
                 own.append(gathered[k, pl.ds(s, ANGLES, stride=SLICES_DEV), :])
-                packed = gathered[k, pl.ds(OWN_ROWS + s, ANGLES // 2, stride=SLICES_DEV), :]
-                margin.append(jnp.concatenate([packed, pltpu.roll(packed, BLOCK // 2, 1)], axis=0))
+                margin.append(gathered[k, pl.ds(OWN_ROWS + s, ANGLES // 2, stride=SLICES_DEV), :])
+            margin.append(empty)
             whole = []
             for k in range(TILES):
-                total = own[k]
-                if k > 0:
-                    total = total + jnp.where(lane < HALO, margin[k - 1], 0.0)
-                if k < TILES - 1:
-                    total = total + jnp.where(lane >= BLOCK - HALO, margin[k + 1], 0.0)
+                packed = jnp.where(from_left, margin[k], margin[k + 2])
+                added = jnp.concatenate([packed, pltpu.roll(packed, BLOCK // 2, 1)], axis=0)
+                total = own[k] + jnp.where(outer, added, 0.0)
                 whole.append(total.astype(jnp.bfloat16).astype(jnp.float32))
             whole = [zero] + whole + [zero, zero]
             placed = jnp.concatenate(

time: 75.6 us -> 75.6 us (level)
  no operation moved by 1% of the time
where the time goes in v11:
time: 75.6 us; the launch traced here: 75.3 us
  blocking collectives  54.4 us (72%)
  Pallas kernels  16.6 us (22%)
  waiting for transfers between devices  3.31 us (4%)
    all_to_all x2, blocking collectives, between_chips(): lax.all_to_all(value, 'slab', 0, 0, tiled=True, axis_index_groups=groups)  23.9 us
    all_to_all x1, blocking collectives, body(): landed = lax.all_to_all(partials, 'tile', 0, 0, tiled=True)  17.9 us
    all_to_all x1, blocking collectives, body(): lax.all_to_all(copies_of(grad.astype(jnp.bfloat16), TILES), 'tile', 0, 0,...  12.6 us
    pallas_call x1, Pallas kernels, frame_gradients(): pl.pallas_call(frames_kernel, name='frame_gradients', in_specs=[smem, hbm...  5.76 us
    pallas_call x1, Pallas kernels, project(): pl.pallas_call(project_kernel, name='project', in_specs=[hbm, hbm, hbm],...  5.52 us
    pallas_call x1, Pallas kernels, back_project(): pl.pallas_call(back_kernel, name='back_project', in_specs=[hbm, hbm, pl.B...  5.31 us
    ppermute x2, waiting for transfers between devices, between_cores(): lax.ppermute(value, 'slab', [(i, i ^ 1) for i in range(lax.axis_size('sla...  3.31 us
  transfers between devices with their start and end apart: 2, of which 2 were waited for; matrix products, arithmetic and copies ran while one was open for 0% of the time, Pallas kernels for 0%

profile of v11, /device:TPU:0, one launch (start us, length us, event | category | flops | bytes accessed | tf_op | source)
XLA Modules:
  0.0 75.3 jit_solution(18415167222789000845)
XLA Ops:
  0.0 0.0 copy-start
  0.0 0.0 copy-start.1
  0.0 0.0 copy-start.2
  0.0 0.0 copy-start.3
  0.0 0.0 copy-start.6
  0.0 0.0 copy-start.7
  0.0 5.5 %project.1 = s16[8,192,128]{2,1,0:T(8,128)(2,1)} custom-call(f32[16]{0:T(128)} %shears_in.3, s32[16]{0:T(128)} %bitcast.5, f32[8,64,1024]{2,1,0:T(8,128)} %volume_in.1), custom_call_target="tpu_custom_call" | custom-call | tf_op jit(solution)/shard_map/project/pallas_call | solution.py:154
  5.5 17.9 %all_to_all.20 = s16[8,192,128]{2,1,0:T(8,128)(2,1)S(1)} all-to-all(s16[8,192,128]{2,1,0:T(8,128)(2,1)} %project.1), channel_id=1, replica_groups=mesh['slab'=16,'tile'=8] {'tile'}, dimensions={0} | all-to-all | bytes 786432 | tf_op jit(solution)/shard_map/all_to_all | solution.py:432
  23.4 0.1 convert_reduce_fusion
  23.6 0.1 broadcast_in_dim.6
  23.6 12.4 %all_to_all.21.near_phases = s16[8,192,128]{2,1,0:T(8,128)(2,1)S(1)} all-to-all(s16[8,192,128]{2,1,0:T(8,128)(2,1)S(1)} %broadcast_in_dim.6), channel_id=1, replica_groups={{0,16,32,48,64,80,96,112},{8,24,40,56,72,88,104,120},{1,17,33,49,65,81,..., dimensions={0} | all-to-all | bytes 786432 | tf_op jit(solution)/shard_map/all_to_all | solution.py:420
  36.0 0.0 collective-permute-start
  36.0 1.7 %collective-permute-done.far_phases = s16[8,192,128]{2,1,0:T(8,128)(2,1)S(1)} collective-permute-done((s16[8,192,128]{2,1,0:T(8,128)(2,1)S(1)}, s16[8,192,128]{2,1,0:T(8,128)(2,1)S(1)}, u32[]{:S(2)}, u32[]{:S(2)}) %collective-permute-start) | collective-permute-done | bytes 393248 | tf_op jit(solution)/shard_map/ppermute | solution.py:424
  37.7 0.0 copy-done
  37.7 0.0 copy-done.1
  37.7 0.0 copy-done.2
  37.7 0.0 copy-done.3
  37.7 0.0 copy-done.6
  37.8 0.0 copy-done.7
  37.8 5.8 %frame_gradients.1 = (bf16[8,192,128]{2,1,0:T(8,128)(2,1)S(1)}, bf16[8,192,128]{2,1,0:T(8,128)(2,1)S(1)}) custom-call(s32[1]{0:T(128)} %bitcast.1.parity, s32[32]{0:T(128)S(1)} %bitcast.7, s32[32]{0:T(128)S(1)} %copy-done.7, s16[8,192,128]{2,1,0:T(8,128)(2,1)S(1)} %all_to_all.21.near_phases, s16[8,192,128]{2,1,0:T(8,128)(2,1)S(1)} %collective-permute-done.far_phases, ...), custom_call_target="tpu_custom_call" | custom-call | tf_op jit(solution)/shard_map/frame_gradients/pallas_call | solution.py:297
  43.5 0.2 collective-permute-start.1
  43.8 1.6 %collective-permute-done.1 = bf16[8,192,128]{2,1,0:T(8,128)(2,1)S(1)} collective-permute-done((bf16[8,192,128]{2,1,0:T(8,128)(2,1)S(1)}, bf16[8,192,128]{2,1,0:T(8,128)(2,1)S(1)}, u32[]{:S(2)}, u32[]{:S(2)}) %collective-permute-start.1) | collective-permute-done | bytes 393248 | tf_op jit(solution)/shard_map/ppermute | solution.py:424
  45.3 0.1 add_convert_fusion
  45.5 0.0 copy-start.4
  45.5 0.0 copy-start.5
  45.5 11.5 %all_to_all.22 = bf16[8,192,128]{2,1,0:T(8,128)(2,1)S(1)} all-to-all(bf16[8,192,128]{2,1,0:T(8,128)(2,1)S(1)} %add_convert_fusion), channel_id=1, replica_groups={{0,16,32,48,64,80,96,112},{8,24,40,56,72,88,104,120},{1,17,33,49,65,81,..., dimensions={0} | all-to-all | bytes 786432 | tf_op jit(solution)/shard_map/all_to_all | solution.py:420
  57.0 0.1 convert_element_type.26
  57.1 0.1 broadcast_in_dim.7
  57.2 12.6 %all_to_all.23.tiles = bf16[8,192,128]{2,1,0:T(8,128)(2,1)S(1)} all-to-all(bf16[8,192,128]{2,1,0:T(8,128)(2,1)S(1)} %broadcast_in_dim.7), channel_id=1, replica_groups=mesh['slab'=16,'tile'=8] {'tile'}, dimensions={0} | all-to-all | bytes 786432 | tf_op jit(solution)/shard_map/all_to_all | solution.py:445
  69.8 0.0 copy-done.4
  69.8 0.0 copy-done.5
  69.8 5.3 %back_project.1 = f32[8,64,1024]{2,1,0:T(8,128)} custom-call(f32[16]{0:T(128)S(1)} %copy-done.4, s32[16]{0:T(128)S(1)} %bitcast.6, bf16[8,192,128]{2,1,0:T(8,128)(2,1)S(1)} %all_to_all.23.tiles), custom_call_target="tpu_custom_call" | custom-call | tf_op jit(solution)/shard_map/back_project/pallas_call | solution.py:385
  (2 shorter events, 0.1 us)
Async XLA Ops:
  0.0 37.7 %copy-start = (bf16[32,128,128]{2,1,0:T(8,128)(2,1)S(1)}, bf16[32,128,128]{2,1,0:T(8,128)(2,1)}, u32[]{:S(2)}) copy-start(bf16[32,128,128]{2,1,0:T(8,128)(2,1)} %measured.1) | copy-start | bytes 3145732
  0.0 37.7 %copy-start.1 = (f32[2,128,128]{2,1,0:T(8,128)S(1)}, f32[2,128,128]{2,1,0:T(8,128)}, u32[]{:S(2)}) copy-start(f32[2,128,128]{2,1,0:T(8,128)} %probe.1) | copy-start | bytes 393220
  0.0 37.7 %copy-start.2 = (bf16[256,256]{1,0:T(8,128)(2,1)S(1)}, bf16[256,256]{1,0:T(8,128)(2,1)}, u32[]{:S(2)}) copy-start(bf16[256,256]{1,0:T(8,128)(2,1)} %constant.31.clone.gather) | copy-start | bytes 393220
  0.0 37.7 %copy-start.3 = (bf16[256,256]{1,0:T(8,128)(2,1)S(1)}, bf16[256,256]{1,0:T(8,128)(2,1)}, u32[]{:S(2)}) copy-start(bf16[256,256]{1,0:T(8,128)(2,1)} %constant.30.clone.spread) | copy-start | bytes 393220
  0.0 37.7 %copy-start.6 = (s32[32,1]{0,1:T(1,128)S(1)}, s32[32,1]{0,1:T(1,128)}, u32[]{:S(2)}) copy-start(s32[32,1]{0,1:T(1,128)} %param.14) | copy-start | bytes 388
  0.0 37.7 %copy-start.7 = (s32[32]{0:T(128)S(1)}, s32[32]{0:T(128)}, u32[]{:S(2)}) copy-start(s32[32]{0:T(128)} %shifts_in.1) | copy-start | bytes 388
  36.0 1.7 %collective-permute-start = (s16[8,192,128]{2,1,0:T(8,128)(2,1)S(1)}, s16[8,192,128]{2,1,0:T(8,128)(2,1)S(1)}, u32[]{:S(2)}, u32[]{:S(2)}) collective-permute-start(s16[8,192,128]{2,1,0:T(8,128)(2,1)S(1)} %all_to_all.21.near_phases), channel_id=1, source_target_pairs={{0,8},{8,0},{16,24},{24,16},{32,40},{40,32},{48,56},{56,48},{64,72... | collective-permute-start | bytes 1179656 | tf_op jit(solution)/shard_map/ppermute | solution.py:424
  43.5 1.8 %collective-permute-start.1 = (bf16[8,192,128]{2,1,0:T(8,128)(2,1)S(1)}, bf16[8,192,128]{2,1,0:T(8,128)(2,1)S(1)}, u32[]{:S(2)}, u32[]{:S(2)}) collective-permute-start(bf16[8,192,128]{2,1,0:T(8,128)(2,1)S(1)} %get-tuple-element.8), channel_id=1, source_target_pairs={{0,8},{8,0},{16,24},{24,16},{32,40},{40,32},{48,56},{56,48},{64,72... | collective-permute-start | bytes 1179656 | tf_op jit(solution)/shard_map/ppermute | solution.py:424
  45.5 24.3 %copy-start.4 = (f32[16]{0:T(128)S(1)}, f32[16]{0:T(128)}, u32[]{:S(2)}) copy-start(f32[16]{0:T(128)} %shears_in.3) | copy-start | bytes 196
  45.5 24.3 %copy-start.5 = (s32[16,1]{0,1:T(1,128)S(1)}, s32[16,1]{0,1:T(1,128)}, u32[]{:S(2)}) copy-start(s32[16,1]{0,1:T(1,128)} %param.11) | copy-start | bytes 196

commit v12 on v10

--- a/solution.py
+++ b/solution.py
@@ -26,7 +26,7 @@
 PAIRS = SLICES_DEV // 2
 ROWS = OWN_ROWS + EDGE_ROWS
 GROUP = 32
-MERGED = 4
+MERGED = 8
 UNPACK_UNROLL = 2
 VMEM_LIMIT = 40 * 1024 * 1024
 ALL_VMEM = 60 * 1024 * 1024
@@ -130,14 +130,12 @@
             for k in range(BLOCKS):
                 here = jnp.where(shift == 0, block[k + 1], jnp.where(shift > 0, block[k], block[k + 2]))
                 placed.append(here)
-            around = [zero] + placed + [zero]
+            packed = [jnp.where(outer, here[:8], pltpu.roll(here[8:], BLOCK // 2, 1)) for here in placed]
+            packed = [zero[:8]] + packed + [zero[:8]]
             s = p * 2 + half
             for k in range(BLOCKS):
                 gathered[k, pl.ds(s, ANGLES, stride=SLICES_DEV), :] = placed[k]
-                after, before = around[k + 2], around[k]
-                low = jnp.where(lane < HALO, after[:8], before[:8])
-                high = jnp.where(lane < HALO, after[8:], before[8:])
-                edge = jnp.where(outer, low, pltpu.roll(high, BLOCK // 2, 1))
+                edge = jnp.where(lane % (BLOCK // 2) < HALO, packed[k + 2], packed[k])
                 gathered[k, pl.ds(OWN_ROWS + s, ANGLES // 2, stride=SLICES_DEV), :] = edge
 
     build(0)

time: 75.6 us -> 75.6 us (level)
  no operation moved by 1% of the time
where the time goes in v12:
time: 75.6 us; the launch traced here: 75.3 us
  blocking collectives  54.4 us (72%)
  Pallas kernels  16.6 us (22%)
  waiting for transfers between devices  3.31 us (4%)
    all_to_all x2, blocking collectives, between_chips(): lax.all_to_all(value, 'slab', 0, 0, tiled=True, axis_index_groups=groups)  23.9 us
    all_to_all x1, blocking collectives, body(): landed = lax.all_to_all(partials, 'tile', 0, 0, tiled=True)  17.9 us
    all_to_all x1, blocking collectives, body(): lax.all_to_all(copies_of(grad.astype(jnp.bfloat16), TILES), 'tile', 0, 0,...  12.6 us
    pallas_call x1, Pallas kernels, frame_gradients(): pl.pallas_call(frames_kernel, name='frame_gradients', in_specs=[smem, hbm...  5.79 us
    pallas_call x1, Pallas kernels, project(): pl.pallas_call(project_kernel, name='project', in_specs=[hbm, hbm, hbm],...  5.51 us
    pallas_call x1, Pallas kernels, back_project(): pl.pallas_call(back_kernel, name='back_project', in_specs=[hbm, hbm, pl.B...  5.33 us
    ppermute x2, waiting for transfers between devices, between_cores(): lax.ppermute(value, 'slab', [(i, i ^ 1) for i in range(lax.axis_size('sla...  3.31 us
  transfers between devices with their start and end apart: 2, of which 2 were waited for; matrix products, arithmetic and copies ran while one was open for 0% of the time, Pallas kernels for 0%

profile of v12, /device:TPU:0, one launch (start us, length us, event | category | flops | bytes accessed | tf_op | source)
XLA Modules:
  0.0 75.3 jit_solution(16849178545910442601)
XLA Ops:
  0.0 0.0 copy-start
  0.0 0.0 copy-start.1
  0.0 0.0 copy-start.2
  0.0 0.0 copy-start.3
  0.0 0.0 copy-start.6
  0.0 0.0 copy-start.7
  0.0 5.5 %project.1 = s16[8,192,128]{2,1,0:T(8,128)(2,1)} custom-call(f32[16]{0:T(128)} %shears_in.3, s32[16]{0:T(128)} %bitcast.5, f32[8,64,1024]{2,1,0:T(8,128)} %volume_in.1), custom_call_target="tpu_custom_call" | custom-call | tf_op jit(solution)/shard_map/project/pallas_call | solution.py:152
  5.5 17.9 %all_to_all.20 = s16[8,192,128]{2,1,0:T(8,128)(2,1)S(1)} all-to-all(s16[8,192,128]{2,1,0:T(8,128)(2,1)} %project.1), channel_id=1, replica_groups=mesh['slab'=16,'tile'=8] {'tile'}, dimensions={0} | all-to-all | bytes 786432 | tf_op jit(solution)/shard_map/all_to_all | solution.py:429
  23.4 0.1 convert_reduce_fusion
  23.6 0.1 broadcast_in_dim.6
  23.6 12.4 %all_to_all.21.near_phases = s16[8,192,128]{2,1,0:T(8,128)(2,1)S(1)} all-to-all(s16[8,192,128]{2,1,0:T(8,128)(2,1)S(1)} %broadcast_in_dim.6), channel_id=1, replica_groups={{0,16,32,48,64,80,96,112},{8,24,40,56,72,88,104,120},{1,17,33,49,65,81,..., dimensions={0} | all-to-all | bytes 786432 | tf_op jit(solution)/shard_map/all_to_all | solution.py:417
  36.0 0.0 collective-permute-start
  36.0 1.7 %collective-permute-done.far_phases = s16[8,192,128]{2,1,0:T(8,128)(2,1)S(1)} collective-permute-done((s16[8,192,128]{2,1,0:T(8,128)(2,1)S(1)}, s16[8,192,128]{2,1,0:T(8,128)(2,1)S(1)}, u32[]{:S(2)}, u32[]{:S(2)}) %collective-permute-start) | collective-permute-done | bytes 393248 | tf_op jit(solution)/shard_map/ppermute | solution.py:421
  37.7 0.0 copy-done
  37.7 0.0 copy-done.1
  37.7 0.0 copy-done.2
  37.7 0.0 copy-done.3
  37.7 0.0 copy-done.6
  37.7 0.0 copy-done.7
  37.8 5.8 %frame_gradients.1 = (bf16[8,192,128]{2,1,0:T(8,128)(2,1)S(1)}, bf16[8,192,128]{2,1,0:T(8,128)(2,1)S(1)}) custom-call(s32[1]{0:T(128)} %bitcast.1.parity, s32[32]{0:T(128)S(1)} %bitcast.7, s32[32]{0:T(128)S(1)} %copy-done.7, s16[8,192,128]{2,1,0:T(8,128)(2,1)S(1)} %all_to_all.21.near_phases, s16[8,192,128]{2,1,0:T(8,128)(2,1)S(1)} %collective-permute-done.far_phases, ...), custom_call_target="tpu_custom_call" | custom-call | tf_op jit(solution)/shard_map/frame_gradients/pallas_call | solution.py:295
  43.6 0.2 collective-permute-start.1
  43.8 1.6 %collective-permute-done.1 = bf16[8,192,128]{2,1,0:T(8,128)(2,1)S(1)} collective-permute-done((bf16[8,192,128]{2,1,0:T(8,128)(2,1)S(1)}, bf16[8,192,128]{2,1,0:T(8,128)(2,1)S(1)}, u32[]{:S(2)}, u32[]{:S(2)}) %collective-permute-start.1) | collective-permute-done | bytes 393248 | tf_op jit(solution)/shard_map/ppermute | solution.py:421
  45.4 0.1 add_convert_fusion
  45.5 0.0 copy-start.4
  45.5 0.0 copy-start.5
  45.5 11.5 %all_to_all.22 = bf16[8,192,128]{2,1,0:T(8,128)(2,1)S(1)} all-to-all(bf16[8,192,128]{2,1,0:T(8,128)(2,1)S(1)} %add_convert_fusion), channel_id=1, replica_groups={{0,16,32,48,64,80,96,112},{8,24,40,56,72,88,104,120},{1,17,33,49,65,81,..., dimensions={0} | all-to-all | bytes 786432 | tf_op jit(solution)/shard_map/all_to_all | solution.py:417
  57.0 0.1 convert_element_type.26
  57.1 0.1 broadcast_in_dim.7
  57.2 12.6 %all_to_all.23.tiles = bf16[8,192,128]{2,1,0:T(8,128)(2,1)S(1)} all-to-all(bf16[8,192,128]{2,1,0:T(8,128)(2,1)S(1)} %broadcast_in_dim.7), channel_id=1, replica_groups=mesh['slab'=16,'tile'=8] {'tile'}, dimensions={0} | all-to-all | bytes 786432 | tf_op jit(solution)/shard_map/all_to_all | solution.py:442
  69.8 0.0 copy-done.4
  69.8 0.0 copy-done.5
  69.8 5.3 %back_project.1 = f32[8,64,1024]{2,1,0:T(8,128)} custom-call(f32[16]{0:T(128)S(1)} %copy-done.4, s32[16]{0:T(128)S(1)} %bitcast.6, bf16[8,192,128]{2,1,0:T(8,128)(2,1)S(1)} %all_to_all.23.tiles), custom_call_target="tpu_custom_call" | custom-call | tf_op jit(solution)/shard_map/back_project/pallas_call | solution.py:382
  (2 shorter events, 0.1 us)
Async XLA Ops:
  0.0 37.7 %copy-start = (bf16[32,128,128]{2,1,0:T(8,128)(2,1)S(1)}, bf16[32,128,128]{2,1,0:T(8,128)(2,1)}, u32[]{:S(2)}) copy-start(bf16[32,128,128]{2,1,0:T(8,128)(2,1)} %measured.1) | copy-start | bytes 3145732
  0.0 37.7 %copy-start.1 = (f32[2,128,128]{2,1,0:T(8,128)S(1)}, f32[2,128,128]{2,1,0:T(8,128)}, u32[]{:S(2)}) copy-start(f32[2,128,128]{2,1,0:T(8,128)} %probe.1) | copy-start | bytes 393220
  0.0 37.7 %copy-start.2 = (bf16[256,256]{1,0:T(8,128)(2,1)S(1)}, bf16[256,256]{1,0:T(8,128)(2,1)}, u32[]{:S(2)}) copy-start(bf16[256,256]{1,0:T(8,128)(2,1)} %constant.31.clone.gather) | copy-start | bytes 393220
  0.0 37.7 %copy-start.3 = (bf16[256,256]{1,0:T(8,128)(2,1)S(1)}, bf16[256,256]{1,0:T(8,128)(2,1)}, u32[]{:S(2)}) copy-start(bf16[256,256]{1,0:T(8,128)(2,1)} %constant.30.clone.spread) | copy-start | bytes 393220
  0.0 37.7 %copy-start.6 = (s32[32,1]{0,1:T(1,128)S(1)}, s32[32,1]{0,1:T(1,128)}, u32[]{:S(2)}) copy-start(s32[32,1]{0,1:T(1,128)} %param.14) | copy-start | bytes 388
  0.0 37.7 %copy-start.7 = (s32[32]{0:T(128)S(1)}, s32[32]{0:T(128)}, u32[]{:S(2)}) copy-start(s32[32]{0:T(128)} %shifts_in.1) | copy-start | bytes 388
  36.0 1.7 %collective-permute-start = (s16[8,192,128]{2,1,0:T(8,128)(2,1)S(1)}, s16[8,192,128]{2,1,0:T(8,128)(2,1)S(1)}, u32[]{:S(2)}, u32[]{:S(2)}) collective-permute-start(s16[8,192,128]{2,1,0:T(8,128)(2,1)S(1)} %all_to_all.21.near_phases), channel_id=1, source_target_pairs={{0,8},{8,0},{16,24},{24,16},{32,40},{40,32},{48,56},{56,48},{64,72... | collective-permute-start | bytes 1179656 | tf_op jit(solution)/shard_map/ppermute | solution.py:421
  43.6 1.8 %collective-permute-start.1 = (bf16[8,192,128]{2,1,0:T(8,128)(2,1)S(1)}, bf16[8,192,128]{2,1,0:T(8,128)(2,1)S(1)}, u32[]{:S(2)}, u32[]{:S(2)}) collective-permute-start(bf16[8,192,128]{2,1,0:T(8,128)(2,1)S(1)} %get-tuple-element.8), channel_id=1, source_target_pairs={{0,8},{8,0},{16,24},{24,16},{32,40},{40,32},{48,56},{56,48},{64,72... | collective-permute-start | bytes 1179656 | tf_op jit(solution)/shard_map/ppermute | solution.py:421
  45.5 24.3 %copy-start.4 = (f32[16]{0:T(128)S(1)}, f32[16]{0:T(128)}, u32[]{:S(2)}) copy-start(f32[16]{0:T(128)} %shears_in.3) | copy-start | bytes 196
  45.5 24.3 %copy-start.5 = (s32[16,1]{0,1:T(1,128)S(1)}, s32[16,1]{0,1:T(1,128)}, u32[]{:S(2)}) copy-start(s32[16,1]{0,1:T(1,128)} %param.11) | copy-start | bytes 196
